TPU v7x, 32 devices: a whole 2x2x4 slice. The times are simulated.
32 devices in a mesh: row: 4 (over y, core), col: 8 (over z, x).
Axes of the slice: x: 2, y: 2, z: 4, core: 2. Of those that a mesh axis runs over, the one named last changes fastest.
Arguments:
- source_desc: bfloat16 [8192, 64], P('row', 'col'), may hold values from -9 to 9
- target_desc: bfloat16 [16384, 64], P('col'), may hold values from -9 to 9
- source_mass: bfloat16 [8192], P('row'), may hold values from 0.099609375 to 10
- target_mass: bfloat16 [16384], P('col'), may hold values from 0.099609375 to 10
Outputs:
- cross_source: float32 [8192], P('row')
- cross_target: float32 [16384], P('col')
- self_source: float32 [8192], P('row')
- self_target: float32 [16384], P('col')
All inputs are finite; a program needn't handle non-finite values.
Results may differ from a plain program's by a relative error of at most 0.0003.
Values may be sent and summed in bfloat16 or wider, within the bound.
No kernel may reach another device: no remote copies, remote signals or barrier semaphores. Data moves between devices by JAX's collectives and lax.ppermute only.
A program may use at most 64 MiB of HBM per device.

v0:
```python
import math

import jax
import jax.numpy as jnp
from jax import lax
from jax.sharding import PartitionSpec as P

ITERS = 2


EPSILON = 0.25
REACH = 1.0
DAMPING = 1.0 / (1.0 + EPSILON / REACH)


def merged(value, axis, join):
    pieces = jax.tree.map(lambda part: lax.all_gather(part, axis), value)
    head = jax.tree.map(lambda part: part[0], pieces)
    tail = jax.tree.map(lambda part: part[1:], pieces)
    total, _ = lax.scan(lambda total, section: (join(total, section), None), head, tail)
    return total


def half_norms(points):
    wide = points.astype(jnp.float32)
    return 0.5 * jnp.sum(wide * wide, axis=1)


def tile_stats(
    left_desc, right_desc, left_norm, right_norm, left_weight, right_weight, want_rows, want_cols
):
    count = left_desc.shape[0]
    block = math.gcd(512, count)
    blocks = count // block
    width = left_desc.shape[1]
    right_count = right_desc.shape[0]
    inputs = (
        left_desc.reshape(blocks, block, width),
        left_norm.reshape(blocks, block),
        left_weight.reshape(blocks, block),
    )

    def advance(carry, pieces):
        piece_desc, piece_norm, piece_weight = pieces
        product = lax.dot_general(
            piece_desc, right_desc, (((1,), (1,)), ((), ())), preferred_element_type=jnp.float32
        )
        scaled = (piece_norm[:, None] + right_norm[None, :] - product) / EPSILON
        emitted = ()
        if want_rows:
            row_score = right_weight[None, :] - scaled
            row_top = jnp.max(row_score, axis=1)
            row_total = jnp.sum(jnp.exp(row_score - row_top[:, None]), axis=1)
            emitted = (row_top, row_total)
        if want_cols:
            col_top, col_total = carry
            col_score = piece_weight[:, None] - scaled
            fresh_top = jnp.maximum(col_top, jnp.max(col_score, axis=0))
            col_total = col_total * jnp.exp(col_top - fresh_top) + jnp.sum(
                jnp.exp(col_score - fresh_top[None, :]), axis=0
            )
            carry = (fresh_top, col_total)
        return (carry, emitted)

    if want_cols:
        start = (
            jnp.full((right_count,), -jnp.inf, jnp.float32),
            jnp.zeros((right_count,), jnp.float32),
        )
    else:
        start = ()
    carry, emitted = lax.scan(advance, start, inputs)
    rows_out = (emitted[0].reshape(count), emitted[1].reshape(count)) if want_rows else None
    cols_out = carry if want_cols else None
    return (rows_out, cols_out)


def merge_pairs(first, second):
    joined = jnp.maximum(first[0], second[0])
    total = first[1] * jnp.exp(first[0] - joined) + second[1] * jnp.exp(second[0] - joined)
    return (joined, total)


def reduce_col(maxima, totals):
    merged_top, merged_total = merged((maxima, totals), "col", merge_pairs)
    return merged_top + jnp.log(merged_total)


def reduce_row(maxima, totals):
    merged_top, merged_total = merged((maxima, totals), "row", merge_pairs)
    return merged_top + jnp.log(merged_total)


def body(source_desc, target_desc, source_mass, target_mass):
    row_devices = lax.axis_size("row")
    col_devices = lax.axis_size("col")
    row_index = lax.axis_index("row")
    col_index = lax.axis_index("col")
    tile_count = source_mass.shape[0]
    source_part = tile_count // col_devices
    target_part = target_desc.shape[0] // row_devices
    mass_piece = lax.dynamic_slice_in_dim(source_mass, col_index * source_part, source_part, 0)
    source_rows = lax.all_gather(source_desc, "col", axis=1, tiled=True)
    desc_piece = lax.dynamic_slice_in_dim(source_rows, col_index * source_part, source_part, 0)
    source_cols, source_col_mass = (
        lax.all_gather(desc_piece, "row", axis=0, tiled=True),
        lax.all_gather(mass_piece, "row", axis=0, tiled=True),
    )
    target_piece = lax.dynamic_slice_in_dim(target_desc, row_index * target_part, target_part, 0)
    target_mass_piece = lax.dynamic_slice_in_dim(
        target_mass, row_index * target_part, target_part, 0
    )
    target_rows, target_row_mass = (
        lax.all_gather(target_piece, "col", axis=0, tiled=True),
        lax.all_gather(target_mass_piece, "col", axis=0, tiled=True),
    )
    source_log = jnp.log(source_mass.astype(jnp.float32))
    source_col_log = jnp.log(source_col_mass.astype(jnp.float32))
    target_log = jnp.log(target_mass.astype(jnp.float32))
    target_row_log = jnp.log(target_row_mass.astype(jnp.float32))
    source_row_norm = half_norms(source_rows)
    source_col_norm = half_norms(source_cols)
    target_col_norm = half_norms(target_desc)
    target_row_norm = half_norms(target_rows)
    cross_source = jnp.zeros((tile_count,), jnp.float32)
    cross_target = jnp.zeros((target_desc.shape[0],), jnp.float32)
    self_source = jnp.zeros((tile_count,), jnp.float32)
    self_target = jnp.zeros((target_desc.shape[0],), jnp.float32)
    source_view = jnp.zeros((source_cols.shape[0],), jnp.float32)
    target_view = jnp.zeros((target_rows.shape[0],), jnp.float32)
    for iteration in range(ITERS):
        mirror_work = iteration + 1 < ITERS
        cross_rows, cross_cols = tile_stats(
            source_rows,
            target_desc,
            source_row_norm,
            target_col_norm,
            source_log + cross_source / EPSILON,
            target_log + cross_target / EPSILON,
            True,
            True,
        )
        source_self_rows, source_self_cols = tile_stats(
            source_rows,
            source_cols,
            source_row_norm,
            source_col_norm,
            source_log + self_source / EPSILON,
            source_col_log + source_view / EPSILON,
            True,
            mirror_work,
        )
        target_self_rows, target_self_cols = tile_stats(
            target_rows,
            target_desc,
            target_row_norm,
            target_col_norm,
            target_row_log + target_view / EPSILON,
            target_log + self_target / EPSILON,
            mirror_work,
            True,
        )
        col_maxima = [cross_rows[0], source_self_rows[0]]
        col_totals = [cross_rows[1], source_self_rows[1]]
        row_maxima = [cross_cols[0], target_self_cols[0]]
        row_totals = [cross_cols[1], target_self_cols[1]]
        if mirror_work:
            col_maxima.append(target_self_rows[0])
            col_totals.append(target_self_rows[1])
            row_maxima.append(source_self_cols[0])
            row_totals.append(source_self_cols[1])
        col_logs = reduce_col(jnp.concatenate(col_maxima), jnp.concatenate(col_totals))
        row_logs = reduce_row(jnp.concatenate(row_maxima), jnp.concatenate(row_totals))
        target_count = target_desc.shape[0]
        cross_source = 0.5 * cross_source + 0.5 * DAMPING * (-EPSILON * col_logs[:tile_count])
        self_source = 0.5 * self_source + 0.5 * DAMPING * (
            -EPSILON * col_logs[tile_count : 2 * tile_count]
        )
        cross_target = 0.5 * cross_target + 0.5 * DAMPING * (-EPSILON * row_logs[:target_count])
        self_target = 0.5 * self_target + 0.5 * DAMPING * (
            -EPSILON * row_logs[target_count : 2 * target_count]
        )
        if mirror_work:
            target_view = 0.5 * target_view + 0.5 * DAMPING * (
                -EPSILON * col_logs[2 * tile_count :]
            )
            source_view = 0.5 * source_view + 0.5 * DAMPING * (
                -EPSILON * row_logs[2 * target_count :]
            )
    return (cross_source, cross_target, self_source, self_target)


def solution(mesh):
    return jax.shard_map(
        body,
        mesh=mesh,
        in_specs=(P("row", "col"), P("col", None), P("row"), P("col")),
        out_specs=(P("row"), P("col"), P("row"), P("col")),
        check_vma=False,
    )
```

profile of v0, /device:TPU:0, one launch (start us, length us, event | category | flops | bytes accessed | tf_op | source)
XLA Modules:
  0.0 418.5 jit_solution(15101972781240597285)
XLA Ops:
  0.6 32.8 %all_gather.63 = bf16[2048,64]{0,1:T(8,128)(2,1)S(1)} all-gather(bf16[2048,8]{0,1:T(8,128)(2,1)} %param.24), channel_id=1, replica_groups=mesh['row'=4,'col'=8] {'col'}, dimensions={1}, use_global_device_ids=true | all-gather | bytes 294912 | tf_op jit(solution)/shard_map/all_gather | solution.py:103
  33.4 5.4 %all_gather.64 = bf16[1024,64]{0,1:T(8,128)(2,1)S(1)} all-gather(bf16[256,64]{0,1:T(8,128)(2,1)S(1)} %constant_dynamic-slice_fusion.20), channel_id=1, replica_groups=mesh['row'=4,'col'=8] {'row'}, dimensions={0}, use_global_device_ids=true | all-gather | bytes 163840 | tf_op jit(solution)/shard_map/all_gather | solution.py:106
  39.8 5.1 %all-gather.8 = bf16[4,1,256]{2,1,0:T(2,128)(2,1)S(1)} all-gather(bf16[1,1,256]{2,1,0:T(2,128)(2,1)S(1)} %reshape.164), channel_id=1, replica_groups=mesh['row'=4,'col'=8] {'row'}, dimensions={0}, use_global_device_ids=true | all-gather | bytes 2560 | tf_op jit(solution)/shard_map/all_gather | solution.py:107
  46.0 7.3 %while.147 = (s32[]{:T(128)}, f32[1024]{0:T(1024)S(1)}, f32[1024]{0:T(1024)S(1)}, f32[4,512]{1,0:T(4,128)S(1)}, f32[4,512]{1,0:T(4,128)S(1)}, /*index=5*/f32[4,5...) while((s32[]{:T(128)}, f32[1024]{0:T(1024)S(1)}, ...), condition=%wide.region_14.15_spmd.clone, body=%wide.region_9.14_spmd.clone.sunk | while | flops 73928704 | bytes 4681880 | solution.py:72
  53.4 31.5 %all_gather.67 = bf16[4096,64]{0,1:T(8,128)(2,1)S(1)} all-gather(bf16[512,64]{0,1:T(8,128)(2,1)S(1)} %constant_dynamic-slice_fusion.19), channel_id=1, replica_groups=mesh['row'=4,'col'=8] {'col'}, dimensions={0}, use_global_device_ids=true | all-gather | bytes 589824 | tf_op jit(solution)/shard_map/all_gather | solution.py:114
  85.7 26.1 %all-gather.9 = bf16[8,1,512]{2,1,0:T(2,128)(2,1)S(1)} all-gather(bf16[1,1,512]{2,1,0:T(2,128)(2,1)S(1)} %reshape.166), channel_id=1, replica_groups=mesh['row'=4,'col'=8] {'col'}, dimensions={0}, use_global_device_ids=true | all-gather | bytes 9216 | tf_op jit(solution)/shard_map/all_gather | solution.py:115
  112.0 53.9 %while.148 = (s32[]{:T(128)}, f32[2048]{0:T(1024)S(1)}, f32[2048]{0:T(1024)S(1)}, f32[8,512]{1,0:T(8,128)S(1)}, f32[8,512]{1,0:T(8,128)S(1)}, /*index=5*/f32[8,5...) while((s32[]{:T(128)}, f32[2048]{0:T(1024)S(1)}, ...), condition=%wide.region_21.22_spmd.clone, body=%wide.region_16.21_spmd.clone.sunk | while | flops 147858432 | bytes 8941720 | solution.py:72
  115.2 3.4 exponential_reduce_fusion.19
  121.9 3.4 exponential_reduce_fusion.19
  128.6 3.4 exponential_reduce_fusion.19
  135.4 3.4 exponential_reduce_fusion.19
  142.1 3.4 exponential_reduce_fusion.19
  148.9 3.4 exponential_reduce_fusion.19
  155.6 3.4 exponential_reduce_fusion.19
  162.3 3.4 exponential_reduce_fusion.19
  165.9 26.8 %while.146 = (s32[]{:T(128)}, f32[2048]{0:T(1024)S(1)}, f32[2048]{0:T(1024)S(1)}, f32[4,512]{1,0:T(4,128)S(1)}, f32[4,512]{1,0:T(4,128)S(1)}, /*index=5*/f32[4,5...) while((s32[]{:T(128)}, f32[2048]{0:T(1024)S(1)}, ...), condition=%wide.region_7.8_spmd.clone, body=%wide.region_2.7_spmd.clone.sunk | while | flops 147858432 | bytes 8941720 | solution.py:72
  169.1 3.4 exponential_reduce_fusion.17
  175.8 3.4 exponential_reduce_fusion.17
  182.6 3.4 exponential_reduce_fusion.17
  189.3 3.4 exponential_reduce_fusion.17
  192.8 31.0 %all-gather.1 = f32[65536]{0:T(1024)S(1)} all-gather(f32[8192]{0:T(1024)S(1)} %pad_maximum_fusion.1), channel_id=3, replica_groups=mesh['row'=4,'col'=8] {'col'}, dimensions={0}, use_global_device_ids=true | all-gather | bytes 294912 | tf_op jit(solution)/shard_map/all_gather | solution.py:17
  223.9 30.7 %all-gather = f32[65536]{0:T(1024)S(1)} all-gather(f32[8192]{0:T(1024)S(1)} %pad_maximum_fusion), channel_id=2, replica_groups=mesh['row'=4,'col'=8] {'col'}, dimensions={0}, use_global_device_ids=true | all-gather | bytes 294912 | tf_op jit(solution)/shard_map/all_gather | solution.py:17
  255.8 45.7 %while.150 = (s32[]{:T(128)}, f32[2048]{0:T(1024)S(1)}, f32[2048]{0:T(1024)S(1)}, f32[8,512]{1,0:T(8,128)S(1)}, f32[8,512]{1,0:T(8,128)S(1)}, /*index=5*/f32[204...) while((s32[]{:T(128)}, f32[2048]{0:T(1024)S(1)}, ...), condition=%wide.region_41.42_spmd.clone, body=%wide.region_38.41_spmd.clone.sunk | while | flops 141568000 | bytes 8908920 | solution.py:72
  301.5 5.3 %all-gather.3 = f32[20480]{0:T(1024)S(1)} all-gather(f32[5120]{0:T(1024)S(1)} %pad_maximum_fusion.3), channel_id=5, replica_groups=mesh['row'=4,'col'=8] {'row'}, dimensions={0}, use_global_device_ids=true | all-gather | bytes 102400 | tf_op jit(solution)/shard_map/all_gather | solution.py:17
  306.8 5.5 %all-gather.2 = f32[20480]{0:T(1024)S(1)} all-gather(f32[5120]{0:T(1024)S(1)} %pad_maximum_fusion.2), channel_id=4, replica_groups=mesh['row'=4,'col'=8] {'row'}, dimensions={0}, use_global_device_ids=true | all-gather | bytes 102400 | tf_op jit(solution)/shard_map/all_gather | solution.py:17
  312.7 26.8 %while.149 = (s32[]{:T(128)}, f32[2048]{0:T(1024)S(1)}, f32[2048]{0:T(1024)S(1)}, f32[4,512]{1,0:T(4,128)S(1)}, f32[4,512]{1,0:T(4,128)S(1)}, /*index=5*/f32[4,5...) while((s32[]{:T(128)}, f32[2048]{0:T(1024)S(1)}, ...), condition=%wide.region_31.32_spmd.clone, body=%wide.region_26.31_spmd.clone.sunk | while | flops 147858432 | bytes 8941720 | solution.py:72
  315.9 3.4 exponential_reduce_fusion.20
  339.5 5.2 %all-gather.7 = f32[16384]{0:T(1024)S(1)} all-gather(f32[4096]{0:T(1024)S(1)} %pad_maximum_fusion.7), channel_id=9, replica_groups=mesh['row'=4,'col'=8] {'row'}, dimensions={0}, use_global_device_ids=true | all-gather | bytes 81920 | tf_op jit(solution)/shard_map/all_gather | solution.py:17
  344.8 5.2 %all-gather.6 = f32[16384]{0:T(1024)S(1)} all-gather(f32[4096]{0:T(1024)S(1)} %pad_maximum_fusion.6), channel_id=8, replica_groups=mesh['row'=4,'col'=8] {'row'}, dimensions={0}, use_global_device_ids=true | all-gather | bytes 81920 | tf_op jit(solution)/shard_map/all_gather | solution.py:17
  351.0 5.0 %while.143 = (s32[]{:T(128)}, f32[4,512]{1,0:T(4,128)S(1)}, f32[4,512]{1,0:T(4,128)S(1)}, f32[1024]{0:T(1024)S(1)}, f32[4,512]{1,0:T(4,128)S(1)}, /*index=5*/f32...) while((s32[]{:T(128)}, f32[4,512]{1,0:T(4,128)S(1)}, ...), condition=%wide.region_35.36_spmd, body=%wide.region_32.35_spmd.sunk | while | flops 70777856 | bytes 4616309 | solution.py:72
  356.1 30.5 %all-gather.5 = f32[32768]{0:T(1024)S(1)} all-gather(f32[4096]{0:T(1024)S(1)} %pad_maximum_fusion.5), channel_id=7, replica_groups=mesh['row'=4,'col'=8] {'col'}, dimensions={0}, use_global_device_ids=true | all-gather | bytes 147456 | tf_op jit(solution)/shard_map/all_gather | solution.py:17
  386.7 30.5 %all-gather.4 = f32[32768]{0:T(1024)S(1)} all-gather(f32[4096]{0:T(1024)S(1)} %pad_maximum_fusion.4), channel_id=6, replica_groups=mesh['row'=4,'col'=8] {'col'}, dimensions={0}, use_global_device_ids=true | all-gather | bytes 147456 | tf_op jit(solution)/shard_map/all_gather | solution.py:17
  (363 shorter events, 128.4 us)
Async XLA Ops:
  46.0 7.4 %copy-start = (bf16[2048,64]{0,1:T(8,128)(2,1)S(1)}, bf16[2048,64]{0,1:T(8,128)(2,1)}, u32[]{:S(2)}) copy-start(bf16[2048,64]{0,1:T(8,128)(2,1)} %param.25) | copy-start | bytes 786436
  46.0 39.6 %copy-start.1 = (bf16[2048]{0:T(1024)(128)(2,1)S(1)}, bf16[2048]{0:T(1024)(128)(2,1)}, u32[]{:S(2)}) copy-start(bf16[2048]{0:T(1024)(128)(2,1)} %param.27) | copy-start | bytes 12292
  255.7 45.7 %copy-start.2 = (bf16[2048]{0:T(1024)(128)(2,1)S(1)}, bf16[2048]{0:T(1024)(128)(2,1)}, u32[]{:S(2)}) copy-start(bf16[2048]{0:T(1024)(128)(2,1)} %param.26) | copy-start | bytes 12292
where the time goes:
time: 419 us; the launch traced here: 418 us
  blocking collectives  245 us (58%)
  other arithmetic  85.4 us (20%)
  matrix products  78.8 us (19%)
  local copies, waits for them, and re-layouts  6.13 us (1%)
    all_gather x8, blocking collectives, merged(): pieces = jax.tree.map(lambda part: lax.all_gather(part, axis), value)  144 us
    dot_general x32, matrix products, advance(): lax.dot_general(piece_desc, right_desc, (((1,), (1,)), ((), ())), preferr...  78.8 us
    reduce_sum x24, other arithmetic, advance(): row_total = jnp.sum(jnp.exp(row_score - row_top[:, None]), axis=1)  59.7 us
    all_gather x1, blocking collectives, body(): source_rows = lax.all_gather(source_desc, 'col', axis=1, tiled=True)  32.8 us
    all_gather x1, blocking collectives, body(): lax.all_gather(target_piece, 'col', axis=0, tiled=True)  31.5 us
    all_gather x1, blocking collectives, body(): lax.all_gather(target_mass_piece, 'col', axis=0, tiled=True)  26.1 us
    reduce_sum x8, other arithmetic, advance(): jnp.sum(jnp.exp(col_score - fresh_top[None, :]), axis=0)  22.2 us

commit v1 on v0

v1 whole, which is shorter than its diff:
```python
import functools
import math

import jax, jax.numpy as jnp
from jax import lax
from jax.experimental import pallas as pl
from jax.experimental.pallas import tpu as pltpu
from jax.sharding import PartitionSpec as P

EPSILON = 0.25
REACH = 1.0
DAMPING = 1.0 / (1.0 + EPSILON / REACH)

LOG2E = math.log2(math.e)
STRIP = 256

def split3(x):
    hi = x.astype(jnp.bfloat16)
    rest = x - hi.astype(jnp.float32)
    mid = rest.astype(jnp.bfloat16)
    lo = (rest - mid.astype(jnp.float32)).astype(jnp.bfloat16)
    return hi, mid, lo

def fill_lanes(rhs, desc_ref, weight):
    wide = desc_ref[...].astype(jnp.float32)
    ch = wide.shape[0]
    bias = weight - 2.0 * jnp.sum(wide * wide, axis=0, keepdims=True)
    hi, mid, lo = split3(bias)
    n = wide.shape[1]
    rhs[0:ch, :] = (4.0 * wide).astype(jnp.bfloat16)
    rhs[ch:3 * ch, :] = jnp.full((2 * ch, n), -2.0, jnp.bfloat16)
    row = lax.broadcasted_iota(jnp.int32, (ch, n), 0)
    hi, mid, lo = (p.astype(jnp.float32) for p in (hi, mid, lo))
    extra = jnp.where(row == 0, hi, jnp.where(row == 1, mid, jnp.where(row == 2, lo, 0.0)))
    rhs[3 * ch:4 * ch, :] = extra.astype(jnp.bfloat16)

def row_operand(points):
    wide = points.astype(jnp.float32)
    square = wide * wide
    high = square.astype(jnp.bfloat16)
    low = (square - high.astype(jnp.float32)).astype(jnp.bfloat16)
    col = lax.broadcasted_iota(jnp.int32, points.shape, 1)
    ones = jnp.where(col < 3, 1.0, 0.0).astype(jnp.bfloat16)
    return jnp.concatenate([points, high, low, ones], axis=1)

def to_rows(vector):
    pieces = [jnp.broadcast_to(vector[:, k:k + 128], (128, 128)).T for k in range(0, vector.shape[1], 128)]
    return jnp.concatenate(pieces, axis=0)

def to_lanes(block):
    return jnp.concatenate([block[k:k + 128, :].T[0:1, :] for k in range(0, block.shape[0], 128)], axis=1)

def rows_sum_lanes(block):
    return jnp.concatenate([jnp.sum(block[k:k + 128, :].T, axis=0, keepdims=True) for k in range(0, block.shape[0], 128)], axis=1)

def fold_rows(x, op):
    parts = [x[k:k + 8, :] for k in range(0, x.shape[0], 8)]
    while len(parts) > 1:
        parts = [op(parts[i], parts[i + 1]) if i + 1 < len(parts) else parts[i] for i in range(0, len(parts), 2)]
    return parts[0]

def fold_lanes(x, op):
    parts = [x[:, k:k + 128] for k in range(0, x.shape[1], 128)]
    return functools.reduce(op, parts)

def cross_kernel(t_ref, w_ref, s_ref, z_ref, row_ref, col_ref, rhs, fbuf, ctop, csum):
    i = pl.program_id(0)
    n = s_ref.shape[1]
    bt = t_ref.shape[0]

    @pl.when(i == 0)
    def _():
        fill_lanes(rhs, s_ref, z_ref[...])
        ctop[...] = jnp.full(ctop.shape, -jnp.inf, jnp.float32)
        csum[...] = jnp.zeros(csum.shape, jnp.float32)

    lhs = row_operand(t_ref[...])
    wrow = to_rows(w_ref[...])
    wide = jnp.concatenate([wrow, wrow], axis=1)
    rmax = None
    for k in range(0, n, STRIP):
        g = jnp.dot(lhs, rhs[:, k:k + STRIP], preferred_element_type=jnp.float32)
        f = (g + wide) * LOG2E
        fbuf[:, k:k + STRIP] = f
        m = fold_lanes(f, jnp.maximum)
        rmax = m if rmax is None else jnp.maximum(rmax, m)
        top = jnp.max(fold_rows(f, jnp.maximum), axis=0, keepdims=True)
        old = ctop[:, k:k + STRIP]
        new = jnp.maximum(old, top)
        csum[:, k:k + STRIP] = csum[:, k:k + STRIP] * jnp.exp2(old - new)
        ctop[:, k:k + STRIP] = new
    r1 = jnp.max(rmax, axis=1, keepdims=True)
    r = jnp.broadcast_to(r1, (bt, 128))
    racc = jnp.zeros((bt, 128), jnp.float32)
    for k in range(0, n, STRIP):
        for h in range(k, k + STRIP, 128):
            f = fbuf[:, h:h + 128]
            racc = racc + jnp.exp2(f - r)
            e2 = jnp.exp2(f - ctop[0:1, h:h + 128])
            csum[:, h:h + 128] = csum[:, h:h + 128] + fold_rows(e2, jnp.add)
    total = jnp.sum(racc, axis=1, keepdims=True)
    row_ref[...] = to_lanes(jnp.broadcast_to(r1 + jnp.log2(total), (bt, 128)))

    @pl.when(i == pl.num_programs(0) - 1)
    def _():
        col_ref[...] = ctop[0:1, :] + jnp.log2(jnp.sum(csum[...], axis=0, keepdims=True))

def cross_tile(t, w, s, z, block=256):
    nt, ch = t.shape
    n = s.shape[1]
    bt = min(block, nt)
    whole = lambda shape: pl.BlockSpec(shape, lambda i: (0,) * len(shape))
    return pl.pallas_call(
        cross_kernel,
        grid=(nt // bt,),
        in_specs=[pl.BlockSpec((bt, ch), lambda i: (i, 0)), pl.BlockSpec((1, bt), lambda i: (0, i)), whole((ch, n)), whole((1, n))],
        out_specs=[pl.BlockSpec((1, bt), lambda i: (0, i)), whole((1, n))],
        out_shape=[jax.ShapeDtypeStruct((1, nt), jnp.float32), jax.ShapeDtypeStruct((1, n), jnp.float32)],
        scratch_shapes=[pltpu.VMEM((4 * ch, n), jnp.bfloat16), pltpu.VMEM((bt, n), jnp.float32), pltpu.VMEM((8, n), jnp.float32), pltpu.VMEM((8, n), jnp.float32)],
        cost_estimate=pl.CostEstimate(flops=2 * nt * n * 4 * ch, bytes_accessed=4 * (nt + n) * ch, transcendentals=2 * nt * n),
        name="cross_tile",
    )(t, w, s, z)

def self_kernel(u_ref, s_ref, z_ref, e_ref, row_ref, rhs):
    i = pl.program_id(0)
    n = s_ref.shape[1]
    bt = u_ref.shape[0]

    @pl.when(i == 0)
    def _():
        fill_lanes(rhs, s_ref, z_ref[...])

    lhs = row_operand(u_ref[...])
    racc = jnp.zeros((bt, 128), jnp.float32)
    for k in range(0, n, STRIP):
        g = jnp.dot(lhs, rhs[:, k:k + STRIP], preferred_element_type=jnp.float32)
        e = jnp.exp(g)
        racc = racc + fold_lanes(e, jnp.add)
        e_ref[:, k:k + STRIP] = e.astype(jnp.bfloat16)
    row_ref[...] = rows_sum_lanes(racc)

def self_tile(u, s, z, block=256):
    nu, ch = u.shape
    n = s.shape[1]
    bt = min(block, nu)
    whole = lambda shape: pl.BlockSpec(shape, lambda i: (0,) * len(shape))
    return pl.pallas_call(
        self_kernel,
        grid=(nu // bt,),
        in_specs=[pl.BlockSpec((bt, ch), lambda i: (i, 0)), whole((ch, n)), whole((1, n))],
        out_specs=[pl.BlockSpec((bt, n), lambda i: (i, 0)), pl.BlockSpec((1, bt), lambda i: (0, i))],
        out_shape=[jax.ShapeDtypeStruct((nu, n), jnp.bfloat16), jax.ShapeDtypeStruct((1, nu), jnp.float32)],
        scratch_shapes=[pltpu.VMEM((4 * ch, n), jnp.bfloat16)],
        cost_estimate=pl.CostEstimate(flops=2 * nu * n * 4 * ch, bytes_accessed=2 * nu * n, transcendentals=nu * n),
        name="self_tile",
    )(u, s, z)

def weigh_kernel(e_ref, w_ref, out_ref, acc):
    i = pl.program_id(0)
    hi, mid, lo = (p.astype(jnp.float32) for p in split3(w_ref[...]))
    row = lax.broadcasted_iota(jnp.int32, (16, hi.shape[1]), 0)
    lhs = jnp.where(row == 0, hi, jnp.where(row == 1, mid, jnp.where(row == 2, lo, 0.0))).astype(jnp.bfloat16)
    part = jnp.dot(lhs, e_ref[...], preferred_element_type=jnp.float32)

    @pl.when(i == 0)
    def _():
        acc[...] = jnp.zeros(acc.shape, jnp.float32)
    acc[...] += part

    @pl.when(i == pl.num_programs(0) - 1)
    def _():
        out_ref[...] = jnp.sum(acc[...], axis=0, keepdims=True)

def weigh_tile(e, w, block=512):
    nu, n = e.shape
    bt = min(block, nu)
    return pl.pallas_call(
        weigh_kernel,
        grid=(nu // bt,),
        in_specs=[pl.BlockSpec((bt, n), lambda i: (i, 0)), pl.BlockSpec((1, bt), lambda i: (0, i))],
        out_specs=pl.BlockSpec((1, n), lambda i: (0, 0)),
        out_shape=jax.ShapeDtypeStruct((1, n), jnp.float32),
        scratch_shapes=[pltpu.VMEM((16, n), jnp.float32)],
        cost_estimate=pl.CostEstimate(flops=2 * nu * n * 16, bytes_accessed=2 * nu * n, transcendentals=0),
        name="weigh_tile",
    )(e, w)


def gather(x, axis):
    count = lax.axis_size(axis)
    return lax.all_to_all(jnp.broadcast_to(x[None], (count,) + x.shape), axis, 0, 0)


def butterfly(value, axis, join):
    count = lax.axis_size(axis)
    step = 1
    while step < count:
        other = lax.ppermute(value, axis, [(i, i ^ step) for i in range(count)])
        value = join(value, other)
        step *= 2
    return value


def join_logs(a, b):
    top = jnp.maximum(a, b)
    return top + jnp.log2(1.0 + jnp.exp2(jnp.minimum(a, b) - top))


def body(source_desc, target_desc, source_mass, target_mass):
    rows = lax.axis_size("row")
    cols = lax.axis_size("col")
    row = lax.axis_index("row")
    col = lax.axis_index("col")
    ns = source_mass.shape[0]
    nt = target_mass.shape[0]
    ps = ns // cols
    pt = nt // rows
    half = DAMPING * EPSILON * 0.5

    def packed(points, mass):
        return jnp.concatenate([points.reshape(-1), mass]).reshape(-1, 128)

    def unpacked(blocks, count):
        flat = blocks.reshape(blocks.shape[0], -1)
        width = flat.shape[1] // count
        points = flat[:, : count * (width - 1)].reshape(-1, width - 1)
        return points, flat[:, count * (width - 1) :].reshape(-1)

    source_lanes = gather(source_desc.T, "col").reshape(-1, ns)
    target_lanes = target_desc.T
    piece = lax.dynamic_slice_in_dim(target_desc, row * pt, pt, 0)
    piece_mass = lax.dynamic_slice_in_dim(target_mass, row * pt, pt, 0)
    target_set, target_set_mass = unpacked(gather(packed(piece, piece_mass), "col"), pt)
    piece = lax.dynamic_slice_in_dim(source_lanes, col * ps, ps, 1).T
    piece_mass = lax.dynamic_slice_in_dim(source_mass, col * ps, ps, 0)
    source_set, source_set_mass = unpacked(gather(packed(piece, piece_mass), "row"), ps)

    smass = source_mass.astype(jnp.float32)
    tmass = target_mass.astype(jnp.float32)
    slog = jnp.log(smass)
    tlog = jnp.log(tmass)

    def join_parts(a, b, logs):
        return jnp.concatenate([join_logs(a[:logs], b[:logs]), a[logs:] + b[logs:]])

    ct_part, cs_part = cross_tile(target_desc, tlog[None], source_lanes, slog[None])
    ss_plan, ss_part = self_tile(source_set, source_lanes, slog[None])
    st_plan, st_part = self_tile(target_set, target_lanes, tlog[None])
    by_col = butterfly(jnp.concatenate([cs_part[0], st_part[0]]), "col", lambda a, b: join_parts(a, b, ns))
    by_row = butterfly(jnp.concatenate([ct_part[0], ss_part[0]]), "row", lambda a, b: join_parts(a, b, nt))
    cross_source = -half * (by_col[:ns] / LOG2E - slog)
    cross_target = -half * (by_row[:nt] / LOG2E - tlog)
    st_set = -half * jnp.log(by_col[ns:])
    ss_set = -half * jnp.log(by_row[nt:])

    z = slog + cross_source / EPSILON
    w = tlog + cross_target / EPSILON
    ct_part, cs_part = cross_tile(target_desc, w[None], source_lanes, z[None])
    ss_part = weigh_tile(ss_plan, (source_set_mass.astype(jnp.float32) * jnp.exp(ss_set / EPSILON))[None])
    st_part = weigh_tile(st_plan, (target_set_mass.astype(jnp.float32) * jnp.exp(st_set / EPSILON))[None])
    ss_own = lax.dynamic_update_slice(
        jnp.zeros((ns,), jnp.float32), lax.dynamic_slice(ss_set, (row * ps,), (ps,)), (col * ps,)
    )
    st_own = lax.dynamic_update_slice(
        jnp.zeros((nt,), jnp.float32), lax.dynamic_slice(st_set, (col * pt,), (pt,)), (row * pt,)
    )
    by_col = butterfly(jnp.concatenate([cs_part[0], ss_part[0], ss_own]), "col", lambda a, b: join_parts(a, b, ns))
    by_row = butterfly(jnp.concatenate([ct_part[0], st_part[0], st_own]), "row", lambda a, b: join_parts(a, b, nt))
    cross_source = 0.5 * cross_source - half * (by_col[:ns] / LOG2E - z)
    cross_target = 0.5 * cross_target - half * (by_row[:nt] / LOG2E - w)
    self_source = 0.5 * by_col[2 * ns :] - half * jnp.log(by_col[ns : 2 * ns] / smass)
    self_target = 0.5 * by_row[2 * nt :] - half * jnp.log(by_row[nt : 2 * nt] / tmass)
    return (cross_source, cross_target, self_source, self_target)


def solution(mesh):
    return jax.shard_map(
        body,
        mesh=mesh,
        in_specs=(P("row", "col"), P("col", None), P("row"), P("col")),
        out_specs=(P("row"), P("col"), P("row"), P("col")),
        check_vma=False,
    )
```

time: 419 us -> 133 us (0.32)
  blocking collectives: 245 us -> 0 us
  matrix products: 78.8 us -> 0 us
  other arithmetic: 85.4 us -> 12.3 us
  Pallas kernels: 0 us -> 58.5 us
  starting transfers between devices: 0 us -> 26.3 us
  waiting for transfers between devices: 0 us -> 21.5 us
  local copies, waits for them, and re-layouts: 6.13 us -> 11.3 us
    all_gather x13 -> x0, blocking collectives: 245 us -> none  [the longest x8 144 us: merged(): pieces = jax.tree.map(lambda part: lax.all_gather(part, axis), value)]
    reduce_sum x36 -> x0, other arithmetic: 82.2 us -> none  [the longest x24 59.7 us: advance(): row_total = jnp.sum(jnp.exp(row_score - row_top[:, None]), axis=1)]
    dot_general x32 -> x0, matrix products: 78.8 us -> none  [advance(): lax.dot_general(piece_desc, right_desc, (((1,), (1,)), ((), ())), preferr...]
    pallas_call x0 -> x6, Pallas kernels: none -> 58.5 us  [the longest x2 26 us: cross_tile(): pl.pallas_call(cross_kernel, grid=(nt // bt,), in_specs=[pl.BlockSpec((bt...]
    all_to_all x0 -> x3, starting transfers between devices: none -> 14.8 us  [gather(): lax.all_to_all(jnp.broadcast_to(x[None], (count,) + x.shape), axis, 0, 0)]
    ppermute x0 -> x10, starting transfers between devices: none -> 11.5 us  [butterfly(): other = lax.ppermute(value, axis, [(i, i ^ step) for i in range(count)])]
    all_to_all x0 -> x3, waiting for transfers between devices: none -> 11 us  [gather(): lax.all_to_all(jnp.broadcast_to(x[None], (count,) + x.shape), axis, 0, 0)]
    ppermute x0 -> x10, waiting for transfers between devices: none -> 10.5 us  [butterfly(): other = lax.ppermute(value, axis, [(i, i ^ step) for i in range(count)])]
  transfers between devices with their start and end apart: 0 -> 13, of which waited for: 0 -> 7; matrix products, arithmetic and copies ran while one was open for 0% -> 11% of each run, Pallas kernels for 0% -> 20%
where the time goes in v1:
time: 133 us; the launch traced here: 131 us
  Pallas kernels  58.5 us (44%)
  starting transfers between devices  26.3 us (20%)
  waiting for transfers between devices  21.5 us (16%)
  other arithmetic  12.3 us (9%)
  local copies, waits for them, and re-layouts  11.3 us (8%)
    pallas_call x2, Pallas kernels, cross_tile(): pl.pallas_call(cross_kernel, grid=(nt // bt,), in_specs=[pl.BlockSpec((bt...  26 us
    pallas_call x2, Pallas kernels, self_tile(): pl.pallas_call(self_kernel, grid=(nu // bt,), in_specs=[pl.BlockSpec((bt,...  19.5 us
    all_to_all x3, starting transfers between devices, gather(): lax.all_to_all(jnp.broadcast_to(x[None], (count,) + x.shape), axis, 0, 0)  14.8 us
    pallas_call x2, Pallas kernels, weigh_tile(): pl.pallas_call(weigh_kernel, grid=(nu // bt,), in_specs=[pl.BlockSpec((bt...  13 us
    ppermute x10, starting transfers between devices, butterfly(): other = lax.ppermute(value, axis, [(i, i ^ step) for i in range(count)])  11.5 us
    all_to_all x3, waiting for transfers between devices, gather(): lax.all_to_all(jnp.broadcast_to(x[None], (count,) + x.shape), axis, 0, 0)  11 us
    ppermute x10, waiting for transfers between devices, butterfly(): other = lax.ppermute(value, axis, [(i, i ^ step) for i in range(count)])  10.5 us
    reshape x2, local copies, waits for them, and re-layouts, unpacked(): points = flat[:, :count * (width - 1)].reshape(-1, width - 1)  3.09 us
  transfers between devices with their start and end apart: 13, of which 7 were waited for; matrix products, arithmetic and copies ran while one was open for 11% of the time, Pallas kernels for 20%

profile of v1, /device:TPU:0, one launch (start us, length us, event | category | flops | bytes accessed | tf_op | source)
XLA Modules:
  0.0 130.8 jit_solution(8462944082512071480)
XLA Ops:
  0.6 1.5 %broadcast_in_dim.41 = bf16[8,8,2048]{2,1,0:T(8,128)(2,1)} broadcast(bf16[8,2048]{1,0:T(8,128)(2,1)} %bitcast.56), dimensions={1,2} | broadcast | bytes 294912 | tf_op jit(solution)/shard_map/broadcast_in_dim | solution.py:191
  2.1 7.3 %all-to-all-start = ((bf16[8,8,2048]{2,1,0:T(8,128)(2,1)}), bf16[8,8,2048]{2,1,0:T(8,128)(2,1)S(1)}, u32[]{:S(2)}, u32[]{:S(2)}) async-start(bf16[8,8,2048]{2,1,0:T(8,128)(2,1)} %broadcast_in_dim.41), calls=%async_computation | async-start | bytes 524288 | tf_op jit(solution)/shard_map/all_to_all | solution.py:191
  9.4 0.8 constant_dynamic-slice_fusion
  10.3 2.0 %copy.18.t_ref = bf16[2048,64]{1,0:T(8,128)(2,1)} copy(bf16[2048,64]{0,1:T(8,128)(2,1)} %param.5) | data formatting | bytes 524288 | tf_op args[1]
  14.0 1.3 convert_log_fusion.1
  15.3 1.3 convert_log_fusion
  16.6 1.8 %all-to-all-done = bf16[8,8,2048]{2,1,0:T(8,128)(2,1)S(1)} async-done(((bf16[8,8,2048]{2,1,0:T(8,128)(2,1)}), bf16[8,8,2048]{2,1,0:T(8,128)(2,1)S(1)}, u32[]{:S(2)}, u32[]{:S(2)}) %all-to-all-start) | async-done | bytes 262176 | tf_op jit(solution)/shard_map/all_to_all | solution.py:191
  19.2 3.3 %all-to-all-start.2 = ((bf16[4,130,128]{2,1,0:T(8,128)(2,1)}), bf16[4,130,128]{2,1,0:T(8,128)(2,1)S(1)}, u32[]{:S(2)}, u32[]{:S(2)}) async-start(bf16[4,130,128]{2,1,0:T(8,128)(2,1)} %broadcast_in_dim.46), calls=%async_computation.2 | async-start | bytes 278528 | tf_op jit(solution)/shard_map/all_to_all | solution.py:191
  22.6 13.0 %cross_tile.2 = (f32[1,2048]{1,0:T(1,128)}, f32[1,2048]{1,0:T(1,128)}) custom-call(bf16[2048,64]{1,0:T(8,128)(2,1)} %copy.18.t_ref, f32[1,2048]{1,0:T(1,128)} %bitcast.71, bf16[64,2048]{1,0:T(8,128)(2,1)} %bitcast.45, f32[1,2048]{1,0:T(1,128)} %bitcast.73), custom_call_target="tpu_custom_call" | custom-call | flops 2147483648 | bytes 1048576 | tf_op jit(solution)/shard_map/cross_tile/pallas_call | solution.py:113
  35.8 1.0 reshape.44.u_ref
  36.7 4.9 %self_tile.3 = (bf16[1024,2048]{1,0:T(8,128)(2,1)}, f32[1,1024]{1,0:T(1,128)}) custom-call(bf16[1024,64]{1,0:T(8,128)(2,1)} %reshape.44.u_ref, bf16[64,2048]{1,0:T(8,128)(2,1)} %bitcast.46, f32[1,2048]{1,0:T(1,128)} %bitcast.74), custom_call_target="tpu_custom_call" | custom-call | flops 1073741824 | bytes 4194304 | tf_op jit(solution)/shard_map/self_tile/pallas_call | solution.py:147
  42.8 0.9 broadcast_in_dim.44
  43.7 4.2 %all-to-all-start.1 = ((bf16[8,260,128]{2,1,0:T(8,128)(2,1)}), bf16[8,260,128]{2,1,0:T(8,128)(2,1)S(1)}, u32[]{:S(2)}, u32[]{:S(2)}) async-start(bf16[8,260,128]{2,1,0:T(8,128)(2,1)} %broadcast_in_dim.44), calls=%async_computation.1 | async-start | bytes 1081344 | tf_op jit(solution)/shard_map/all_to_all | solution.py:191
  49.4 1.7 %collective-permute-start.4 = (f32[3072]{0:T(1024)S(1)}, f32[3072]{0:T(1024)S(1)}, u32[]{:S(2)}, u32[]{:S(2)}) collective-permute-start(f32[3072]{0:T(1024)S(1)} %pad_maximum_fusion.9), channel_id=1, source_target_pairs={{0,16},{8,24},{16,0},{24,8},{1,17},{9,25},{17,1},{25,9},{2,18},{10... | collective-permute-start | bytes 36872 | tf_op jit(solution)/shard_map/ppermute | solution.py:198
  51.1 2.0 %collective-permute-done.4 = f32[3072]{0:T(1024)S(1)} collective-permute-done((f32[3072]{0:T(1024)S(1)}, f32[3072]{0:T(1024)S(1)}, u32[]{:S(2)}, u32[]{:S(2)}) %collective-permute-start.4) | collective-permute-done | bytes 12320 | tf_op jit(solution)/shard_map/ppermute | solution.py:198
  53.8 9.3 %all-to-all-done.1 = bf16[8,260,128]{2,1,0:T(8,128)(2,1)S(1)} async-done(((bf16[8,260,128]{2,1,0:T(8,128)(2,1)}), bf16[8,260,128]{2,1,0:T(8,128)(2,1)S(1)}, u32[]{:S(2)}, u32[]{:S(2)}) %all-to-all-start.1) | async-done | bytes 532512 | tf_op jit(solution)/shard_map/all_to_all | solution.py:191
  63.1 2.1 %reshape.41.u_ref = bf16[4096,64]{1,0:T(8,128)(2,1)} reshape(bf16[8,32768]{1,0:T(8,128)(2,1)S(1)} %slice.116) | data formatting | bytes 1048576 | tf_op jit(solution)/shard_map/reshape | solution.py:226
  65.3 14.5 %self_tile.2 = (bf16[4096,2048]{1,0:T(8,128)(2,1)}, f32[1,4096]{1,0:T(1,128)}) custom-call(bf16[4096,64]{1,0:T(8,128)(2,1)} %reshape.41.u_ref, bf16[64,2048]{1,0:T(8,128)(2,1)} %bitcast.43, f32[1,2048]{1,0:T(1,128)} %bitcast.72), custom_call_target="tpu_custom_call" | custom-call | flops 4294967296 | bytes 16777216 | tf_op jit(solution)/shard_map/self_tile/pallas_call | solution.py:147
  80.5 1.5 %collective-permute-start = (f32[6144]{0:T(1024)S(1)}, f32[6144]{0:T(1024)S(1)}, u32[]{:S(2)}, u32[]{:S(2)}) collective-permute-start(f32[6144]{0:T(1024)S(1)} %pad_maximum_fusion), channel_id=1, source_target_pairs={{0,1},{1,0},{2,3},{3,2},{4,5},{5,4},{6,7},{7,6},{8,9},{9,8},{10,11... | collective-permute-start | bytes 73736 | tf_op jit(solution)/shard_map/ppermute | solution.py:198
  82.6 1.8 %collective-permute-done = f32[6144]{0:T(1024)S(1)} collective-permute-done((f32[6144]{0:T(1024)S(1)}, f32[6144]{0:T(1024)S(1)}, u32[]{:S(2)}, u32[]{:S(2)}) %collective-permute-start) | collective-permute-done | bytes 24608 | tf_op jit(solution)/shard_map/ppermute | solution.py:198
  85.1 0.8 collective-permute-start.1
  86.1 3.3 %weigh_tile.2 = f32[1,2048]{1,0:T(1,128)} custom-call(bf16[1024,2048]{1,0:T(8,128)(2,1)} %get-tuple-element.17.e_ref, f32[1,1024]{1,0:T(1,128)} %bitcast.65), custom_call_target="tpu_custom_call" | custom-call | flops 67108864 | bytes 4194304 | tf_op jit(solution)/shard_map/weigh_tile/pallas_call | solution.py:177
  89.4 1.1 collective-permute-start.2
  90.5 3.7 %collective-permute-done.2 = f32[6144]{0:T(1024)S(1)} collective-permute-done((f32[6144]{0:T(1024)S(1)}, f32[6144]{0:T(1024)S(1)}, u32[]{:S(2)}, u32[]{:S(2)}) %collective-permute-start.2) | collective-permute-done | bytes 24608 | tf_op jit(solution)/shard_map/ppermute | solution.py:198
  94.8 13.0 %cross_tile.3 = (f32[1,2048]{1,0:T(1,128)}, f32[1,2048]{1,0:T(1,128)}) custom-call(bf16[2048,64]{1,0:T(8,128)(2,1)} %copy.18.t_ref, f32[1,2048]{1,0:T(1,128)} %bitcast.69, bf16[64,2048]{1,0:T(8,128)(2,1)} %bitcast.47, f32[1,2048]{1,0:T(1,128)} %bitcast.70), custom_call_target="tpu_custom_call" | custom-call | flops 2147483648 | bytes 1048576 | tf_op jit(solution)/shard_map/cross_tile/pallas_call | solution.py:113
  107.8 0.8 pad_maximum_fusion.3
  108.6 1.1 collective-permute-start.5
  110.3 9.7 %weigh_tile.3 = f32[1,2048]{1,0:T(1,128)} custom-call(bf16[4096,2048]{1,0:T(8,128)(2,1)} %get-tuple-element.19.e_ref, f32[1,4096]{1,0:T(1,128)} %bitcast.52), custom_call_target="tpu_custom_call" | custom-call | flops 268435456 | bytes 16777216 | tf_op jit(solution)/shard_map/weigh_tile/pallas_call | solution.py:177
  121.0 1.7 %collective-permute-start.6 = (f32[6144]{0:T(1024)S(1)}, f32[6144]{0:T(1024)S(1)}, u32[]{:S(2)}, u32[]{:S(2)}) collective-permute-start(f32[6144]{0:T(1024)S(1)} %pad_maximum_fusion.4), channel_id=1, source_target_pairs={{0,2},{1,3},{2,0},{3,1},{4,6},{5,7},{6,4},{7,5},{8,10},{9,11},{10,... | collective-permute-start | bytes 73736 | tf_op jit(solution)/shard_map/ppermute | solution.py:198
  123.4 2.0 %collective-permute-start.9 = (f32[6144]{0:T(1024)S(1)}, f32[6144]{0:T(1024)S(1)}, u32[]{:S(2)}, u32[]{:S(2)}) collective-permute-start(f32[6144]{0:T(1024)S(1)} %pad_maximum_fusion.7), channel_id=1, source_target_pairs={{0,16},{8,24},{16,0},{24,8},{1,17},{9,25},{17,1},{25,9},{2,18},{10... | collective-permute-start | bytes 73736 | tf_op jit(solution)/shard_map/ppermute | solution.py:198
  125.4 1.2 collective-permute-start.7
  127.9 2.3 %collective-permute-done.7 = f32[6144]{0:T(1024)S(1)} collective-permute-done((f32[6144]{0:T(1024)S(1)}, f32[6144]{0:T(1024)S(1)}, u32[]{:S(2)}, u32[]{:S(2)}) %collective-permute-start.7) | collective-permute-done | bytes 24608 | tf_op jit(solution)/shard_map/ppermute | solution.py:198
  (74 shorter events, 13.1 us)
Async XLA Ops:
  0.6 52.5 %copy-start.2 = (bf16[2048]{0:T(1024)(128)(2,1)S(1)}, bf16[2048]{0:T(1024)(128)(2,1)}, u32[]{:S(2)}) copy-start(bf16[2048]{0:T(1024)(128)(2,1)} %param.7) | copy-start | bytes 12292
  2.1 16.2 %all-to-all-start = ((bf16[8,8,2048]{2,1,0:T(8,128)(2,1)}), bf16[8,8,2048]{2,1,0:T(8,128)(2,1)S(1)}, u32[]{:S(2)}, u32[]{:S(2)}) async-start(bf16[8,8,2048]{2,1,0:T(8,128)(2,1)} %broadcast_in_dim.41), calls=%async_computation | async-start | bytes 524288 | tf_op jit(solution)/shard_map/all_to_all | solution.py:191
  18.3 4.3 %copy-start = (bf16[8,8,2048]{2,1,0:T(8,128)(2,1)}, bf16[8,8,2048]{2,1,0:T(8,128)(2,1)S(1)}, u32[]{:S(2)}) copy-start(bf16[8,8,2048]{2,1,0:T(8,128)(2,1)S(1)} %all-to-all-done) | copy-start | bytes 786436
  19.2 16.4 %all-to-all-start.2 = ((bf16[4,130,128]{2,1,0:T(8,128)(2,1)}), bf16[4,130,128]{2,1,0:T(8,128)(2,1)S(1)}, u32[]{:S(2)}, u32[]{:S(2)}) async-start(bf16[4,130,128]{2,1,0:T(8,128)(2,1)} %broadcast_in_dim.46), calls=%async_computation.2 | async-start | bytes 278528 | tf_op jit(solution)/shard_map/all_to_all | solution.py:191
  35.6 44.2 %copy-start.4 = (f32[1,2048]{1,0:T(1,128)S(1)}, f32[1,2048]{1,0:T(1,128)}, u32[]{:S(2)}) copy-start(f32[1,2048]{1,0:T(1,128)} %get-tuple-element.12) | copy-start | bytes 24580
  35.6 58.5 %copy-start.3 = (bf16[2048]{0:T(1024)(128)(2,1)S(1)}, bf16[2048]{0:T(1024)(128)(2,1)}, u32[]{:S(2)}) copy-start(bf16[2048]{0:T(1024)(128)(2,1)} %param.6) | copy-start | bytes 12292
  42.4 5.6 %collective-permute-start.3 = (f32[3072]{0:T(1024)S(1)}, f32[3072]{0:T(1024)S(1)}, u32[]{:S(2)}, u32[]{:S(2)}) collective-permute-start(f32[3072]{0:T(1024)S(1)} %pad_maximum_fusion.8), channel_id=1, source_target_pairs={{0,8},{8,0},{16,24},{24,16},{1,9},{9,1},{17,25},{25,17},{2,10},{10... | collective-permute-start | bytes 36872 | tf_op jit(solution)/shard_map/ppermute | solution.py:198
  43.7 19.3 %all-to-all-start.1 = ((bf16[8,260,128]{2,1,0:T(8,128)(2,1)}), bf16[8,260,128]{2,1,0:T(8,128)(2,1)S(1)}, u32[]{:S(2)}, u32[]{:S(2)}) async-start(bf16[8,260,128]{2,1,0:T(8,128)(2,1)} %broadcast_in_dim.44), calls=%async_computation.1 | async-start | bytes 1081344 | tf_op jit(solution)/shard_map/all_to_all | solution.py:191
  49.4 3.8 %collective-permute-start.4 = (f32[3072]{0:T(1024)S(1)}, f32[3072]{0:T(1024)S(1)}, u32[]{:S(2)}, u32[]{:S(2)}) collective-permute-start(f32[3072]{0:T(1024)S(1)} %pad_maximum_fusion.9), channel_id=1, source_target_pairs={{0,16},{8,24},{16,0},{24,8},{1,17},{9,25},{17,1},{25,9},{2,18},{10... | collective-permute-start | bytes 36872 | tf_op jit(solution)/shard_map/ppermute | solution.py:198
  80.5 3.8 %collective-permute-start = (f32[6144]{0:T(1024)S(1)}, f32[6144]{0:T(1024)S(1)}, u32[]{:S(2)}, u32[]{:S(2)}) collective-permute-start(f32[6144]{0:T(1024)S(1)} %pad_maximum_fusion), channel_id=1, source_target_pairs={{0,1},{1,0},{2,3},{3,2},{4,5},{5,4},{6,7},{7,6},{8,9},{9,8},{10,11... | collective-permute-start | bytes 73736 | tf_op jit(solution)/shard_map/ppermute | solution.py:198
  85.1 4.2 %collective-permute-start.1 = (f32[6144]{0:T(1024)S(1)}, f32[6144]{0:T(1024)S(1)}, u32[]{:S(2)}, u32[]{:S(2)}) collective-permute-start(f32[6144]{0:T(1024)S(1)} %pad_maximum_fusion.1), channel_id=1, source_target_pairs={{0,2},{1,3},{2,0},{3,1},{4,6},{5,7},{6,4},{7,5},{8,10},{9,11},{10,... | collective-permute-start | bytes 73736 | tf_op jit(solution)/shard_map/ppermute | solution.py:198
  89.3 31.6 %copy-start.1 = (f32[1,2048]{1,0:T(1,128)S(1)}, f32[1,2048]{1,0:T(1,128)}, u32[]{:S(2)}) copy-start(f32[1,2048]{1,0:T(1,128)} %weigh_tile.2) | copy-start | bytes 24580
  89.4 4.8 %collective-permute-start.2 = (f32[6144]{0:T(1024)S(1)}, f32[6144]{0:T(1024)S(1)}, u32[]{:S(2)}, u32[]{:S(2)}) collective-permute-start(f32[6144]{0:T(1024)S(1)} %pad_maximum_fusion.2), channel_id=1, source_target_pairs={{0,4},{1,5},{2,6},{3,7},{4,0},{5,1},{6,2},{7,3},{8,12},{9,13},{10,... | collective-permute-start | bytes 73736 | tf_op jit(solution)/shard_map/ppermute | solution.py:198
  107.8 12.4 %copy-start.5 = (f32[1,2048]{1,0:T(1,128)S(1)}, f32[1,2048]{1,0:T(1,128)}, u32[]{:S(2)}) copy-start(f32[1,2048]{1,0:T(1,128)} %get-tuple-element.18) | copy-start | bytes 24580
  107.8 13.1 %copy-start.6 = (f32[1,2048]{1,0:T(1,128)S(1)}, f32[1,2048]{1,0:T(1,128)}, u32[]{:S(2)}) copy-start(f32[1,2048]{1,0:T(1,128)} %get-tuple-element.16) | copy-start | bytes 24580
  108.6 12.3 %collective-permute-start.5 = (f32[6144]{0:T(1024)S(1)}, f32[6144]{0:T(1024)S(1)}, u32[]{:S(2)}, u32[]{:S(2)}) collective-permute-start(f32[6144]{0:T(1024)S(1)} %pad_maximum_fusion.3), channel_id=1, source_target_pairs={{0,1},{1,0},{2,3},{3,2},{4,5},{5,4},{6,7},{7,6},{8,9},{9,8},{10,11... | collective-permute-start | bytes 73736 | tf_op jit(solution)/shard_map/ppermute | solution.py:198
  120.9 1.8 %collective-permute-start.8 = (f32[6144]{0:T(1024)S(1)}, f32[6144]{0:T(1024)S(1)}, u32[]{:S(2)}, u32[]{:S(2)}) collective-permute-start(f32[6144]{0:T(1024)S(1)} %pad_maximum_fusion.6), channel_id=1, source_target_pairs={{0,8},{8,0},{16,24},{24,16},{1,9},{9,1},{17,25},{25,17},{2,10},{10... | collective-permute-start | bytes 73736 | tf_op jit(solution)/shard_map/ppermute | solution.py:198
  121.0 4.4 %collective-permute-start.6 = (f32[6144]{0:T(1024)S(1)}, f32[6144]{0:T(1024)S(1)}, u32[]{:S(2)}, u32[]{:S(2)}) collective-permute-start(f32[6144]{0:T(1024)S(1)} %pad_maximum_fusion.4), channel_id=1, source_target_pairs={{0,2},{1,3},{2,0},{3,1},{4,6},{5,7},{6,4},{7,5},{8,10},{9,11},{10,... | collective-permute-start | bytes 73736 | tf_op jit(solution)/shard_map/ppermute | solution.py:198
  123.4 3.8 %collective-permute-start.9 = (f32[6144]{0:T(1024)S(1)}, f32[6144]{0:T(1024)S(1)}, u32[]{:S(2)}, u32[]{:S(2)}) collective-permute-start(f32[6144]{0:T(1024)S(1)} %pad_maximum_fusion.7), channel_id=1, source_target_pairs={{0,16},{8,24},{16,0},{24,8},{1,17},{9,25},{17,1},{25,9},{2,18},{10... | collective-permute-start | bytes 73736 | tf_op jit(solution)/shard_map/ppermute | solution.py:198
  125.4 4.8 %collective-permute-start.7 = (f32[6144]{0:T(1024)S(1)}, f32[6144]{0:T(1024)S(1)}, u32[]{:S(2)}, u32[]{:S(2)}) collective-permute-start(f32[6144]{0:T(1024)S(1)} %pad_maximum_fusion.5), channel_id=1, source_target_pairs={{0,4},{1,5},{2,6},{3,7},{4,0},{5,1},{6,2},{7,3},{8,12},{9,13},{10,... | collective-permute-start | bytes 73736 | tf_op jit(solution)/shard_map/ppermute | solution.py:198

commit v2 on v1

v2 whole, which is shorter than its diff:
```python
import functools

import jax, jax.numpy as jnp
from jax import lax
from jax.experimental import pallas as pl
from jax.experimental.pallas import tpu as pltpu
from jax.sharding import PartitionSpec as P


EPSILON = 0.25
REACH = 1.0
DAMPING = 1.0 / (1.0 + EPSILON / REACH)

STRIP = 256
EXTRA = 16


def split3(x):
    hi = x.astype(jnp.bfloat16).astype(jnp.float32)
    rest = x - hi
    mid = rest.astype(jnp.bfloat16).astype(jnp.float32)
    return hi, mid, rest - mid


def operand(desc, weight, scale, own):
    wide = desc.astype(jnp.float32)
    bias = weight - 2.0 * jnp.sum(wide * wide, axis=0, keepdims=True)
    hi, mid, lo = split3(bias)
    row = lax.broadcasted_iota(jnp.int32, (EXTRA, wide.shape[1]), 0) - own
    other = jnp.where((row + own >= 3 - own) & (row + own < 6 - own), 1.0, 0.0)
    extra = jnp.where(row == 0, hi, jnp.where(row == 1, mid, jnp.where(row == 2, lo, other)))
    main = desc if scale == 1.0 else (scale * wide).astype(jnp.bfloat16)
    return jnp.concatenate([main, extra.astype(jnp.bfloat16)], axis=0)


def scores(lhs, rhs):
    return lax.dot_general(lhs, rhs, (((0,), (0,)), ((), ())), preferred_element_type=jnp.float32)


def to_lanes(block):
    tiles = [block[k : k + 128, :].T[0:1, :] for k in range(0, block.shape[0], 128)]
    return jnp.concatenate(tiles, axis=1)


def rows_sum_lanes(block):
    tiles = [
        jnp.sum(block[k : k + 128, :].T, axis=0, keepdims=True)
        for k in range(0, block.shape[0], 128)
    ]
    return jnp.concatenate(tiles, axis=1)


def fold_rows(x, op):
    parts = [x[k : k + 8, :] for k in range(0, x.shape[0], 8)]
    while len(parts) > 1:
        pairs = [op(parts[k], parts[k + 1]) for k in range(0, len(parts) - 1, 2)]
        parts = pairs + parts[len(pairs) * 2 :]
    return parts[0]


def fold_lanes(x, op):
    return functools.reduce(op, [x[:, k : k + 128] for k in range(0, x.shape[1], 128)])


def cross_kernel(t_ref, w_ref, s_ref, z_ref, row_ref, col_ref, rhs, fbuf, ctop, csum):
    i = pl.program_id(0)
    n = s_ref.shape[1]
    bt = t_ref.shape[1]

    @pl.when(i == 0)
    def _():
        rhs[...] = operand(s_ref[...], z_ref[...], 4.0, 0)
        ctop[...] = jnp.full(ctop.shape, -jnp.inf, jnp.float32)
        csum[...] = jnp.zeros(csum.shape, jnp.float32)

    lhs = operand(t_ref[...], w_ref[...], 1.0, 3)
    rmax = None
    for k in range(0, n, STRIP):
        f = scores(lhs, rhs[:, k : k + STRIP])
        fbuf[:, k : k + STRIP] = f
        m = fold_lanes(f, jnp.maximum)
        rmax = m if rmax is None else jnp.maximum(rmax, m)
        top = jnp.max(fold_rows(f, jnp.maximum), axis=0, keepdims=True)
        old = ctop[:, k : k + STRIP]
        new = jnp.maximum(old, top)
        csum[:, k : k + STRIP] = csum[:, k : k + STRIP] * jnp.exp(old - new)
        ctop[:, k : k + STRIP] = new
    r1 = jnp.max(rmax, axis=1, keepdims=True)
    r = jnp.broadcast_to(r1, (bt, 128))
    racc = jnp.zeros((bt, 128), jnp.float32)
    for h in range(0, n, 128):
        f = fbuf[:, h : h + 128]
        racc = racc + jnp.exp(f - r)
        e2 = jnp.exp(f - ctop[0:1, h : h + 128])
        csum[:, h : h + 128] = csum[:, h : h + 128] + fold_rows(e2, jnp.add)
    total = jnp.sum(racc, axis=1, keepdims=True)
    row_ref[...] = to_lanes(jnp.broadcast_to(r1 + jnp.log(total), (bt, 128)))

    @pl.when(i == pl.num_programs(0) - 1)
    def _():
        col_ref[...] = ctop[0:1, :] + jnp.log(jnp.sum(csum[...], axis=0, keepdims=True))


def whole(shape):
    return pl.BlockSpec(shape, lambda *i: (0,) * len(shape))


def cross_tile(t, w, s, z, block=256):
    ch, nt = t.shape
    n = s.shape[1]
    bt = min(block, nt)
    return pl.pallas_call(
        cross_kernel,
        grid=(nt // bt,),
        in_specs=[
            pl.BlockSpec((ch, bt), lambda i: (0, i)),
            pl.BlockSpec((1, bt), lambda i: (0, i)),
            whole((ch, n)),
            whole((1, n)),
        ],
        out_specs=[pl.BlockSpec((1, bt), lambda i: (0, i)), whole((1, n))],
        out_shape=[jax.ShapeDtypeStruct((1, k), jnp.float32) for k in (nt, n)],
        scratch_shapes=[
            pltpu.VMEM((ch + EXTRA, n), jnp.bfloat16),
            pltpu.VMEM((bt, n), jnp.float32),
            pltpu.VMEM((8, n), jnp.float32),
            pltpu.VMEM((8, n), jnp.float32),
        ],
        cost_estimate=pl.CostEstimate(
            flops=8 * nt * n * ch, bytes_accessed=4 * (nt + n) * ch, transcendentals=2 * nt * n
        ),
        name="cross_tile",
    )(t, w, s, z)


def self_kernel(flip, u_ref, s_ref, z_ref, row_ref, rhs):
    ch, n = s_ref.shape
    bt = u_ref.shape[2]

    @pl.when(pl.program_id(0) == 0)
    def _():
        rhs[...] = operand(s_ref[...], z_ref[...], 4.0, 0)

    lhs = operand(u_ref[0, 0:ch, :], jnp.zeros((1, bt), jnp.float32), 1.0, 3)
    racc = jnp.zeros((bt, 128), jnp.float32)
    for k in range(0, n, STRIP):
        racc = racc + fold_lanes(jnp.exp(scores(lhs, rhs[:, k : k + STRIP])), jnp.add)
    row_ref[...] = rows_sum_lanes(racc)


def again_kernel(flip, u_ref, w_ref, s_ref, col_ref, rhs, csum):
    i = pl.program_id(0)
    ch, n = s_ref.shape

    @pl.when(i == 0)
    def _():
        rhs[...] = operand(s_ref[...], jnp.zeros((1, n), jnp.float32), 4.0, 0)
        csum[...] = jnp.zeros(csum.shape, jnp.float32)

    mass = u_ref[0, ch : ch + 1, :].astype(jnp.float32)
    weight = jnp.log(mass) - 0.5 * DAMPING * jnp.log(w_ref[...])
    lhs = operand(u_ref[0, 0:ch, :], weight, 1.0, 3)
    for k in range(0, n, STRIP):
        part = fold_rows(jnp.exp(scores(lhs, rhs[:, k : k + STRIP])), jnp.add)
        csum[:, k : k + STRIP] = csum[:, k : k + STRIP] + part

    @pl.when(i == pl.num_programs(0) - 1)
    def _():
        col_ref[...] = jnp.sum(csum[...], axis=0, keepdims=True)


def self_cost(u, n):
    pairs = u.shape[0] * u.shape[2] * n
    return pl.CostEstimate(flops=4 * pairs * u.shape[1], bytes_accessed=u.size, transcendentals=pairs)


def self_tile(u, s, z, flip):
    blocks, depth, bt = u.shape
    ch, n = s.shape
    return pl.pallas_call(
        self_kernel,
        grid_spec=pltpu.PrefetchScalarGridSpec(
            num_scalar_prefetch=1,
            grid=(blocks,),
            in_specs=[
                pl.BlockSpec((1, depth, bt), lambda i, f: (i ^ f[0], 0, 0)),
                whole((ch, n)),
                whole((1, n)),
            ],
            out_specs=pl.BlockSpec((1, bt), lambda i, f: (0, i)),
            scratch_shapes=[pltpu.VMEM((ch + EXTRA, n), jnp.bfloat16)],
        ),
        out_shape=jax.ShapeDtypeStruct((1, blocks * bt), jnp.float32),
        cost_estimate=self_cost(u, n),
        name="self_tile",
    )(flip, u, s, z)


def again_tile(u, w, s, flip):
    blocks, depth, bt = u.shape
    ch, n = s.shape
    return pl.pallas_call(
        again_kernel,
        grid_spec=pltpu.PrefetchScalarGridSpec(
            num_scalar_prefetch=1,
            grid=(blocks,),
            in_specs=[
                pl.BlockSpec((1, depth, bt), lambda i, f: (i ^ f[0], 0, 0)),
                pl.BlockSpec((1, bt), lambda i, f: (0, i)),
                whole((ch, n)),
            ],
            out_specs=whole((1, n)),
            scratch_shapes=[
                pltpu.VMEM((ch + EXTRA, n), jnp.bfloat16),
                pltpu.VMEM((8, n), jnp.float32),
            ],
        ),
        out_shape=jax.ShapeDtypeStruct((1, n), jnp.float32),
        cost_estimate=self_cost(u, n),
        name="again_tile",
    )(flip, u, w, s)


def gather(x, axis):
    count = lax.axis_size(axis)
    return lax.all_to_all(jnp.broadcast_to(x[None], (count,) + x.shape), axis, 0, 0)


def collect(x, axis):
    count = lax.axis_size(axis)
    return [x] + [
        lax.ppermute(x, axis, [(i, i ^ k) for i in range(count)]) for k in range(1, count)
    ]


def tree(parts, op):
    while len(parts) > 1:
        parts = [op(parts[k], parts[k + 1]) for k in range(0, len(parts), 2)]
    return parts[0]


def log_sum(parts):
    top = tree(parts, jnp.maximum)
    return top + jnp.log(tree([jnp.exp(part - top) for part in parts], jnp.add))


def body(source_desc, target_desc, source_mass, target_mass):
    rows = lax.axis_size("row")
    cols = lax.axis_size("col")
    row = lax.axis_index("row")
    col = lax.axis_index("col")
    ns = source_mass.shape[0]
    nt = target_mass.shape[0]
    ps = ns // cols
    pt = nt // rows
    half = DAMPING * EPSILON * 0.5

    source_mass = source_mass[None]
    target_mass = target_mass[None]
    target_lanes = target_desc.T
    source_lanes = gather(source_desc.T, "col").reshape(-1, ns)
    piece = jnp.concatenate([target_lanes, target_mass], axis=0)
    piece = lax.dynamic_slice_in_dim(piece, row * pt, pt, 1)
    target_set = gather(piece, "col")
    piece = jnp.concatenate([source_lanes, source_mass], axis=0)
    piece = lax.dynamic_slice_in_dim(piece, col * ps, ps, 1)
    source_set = jnp.stack(collect(piece, "row"))
    flip = row.astype(jnp.int32)[None]
    level = jnp.zeros((1,), jnp.int32)

    smass = source_mass.astype(jnp.float32)
    tmass = target_mass.astype(jnp.float32)
    slog = jnp.log(smass)
    tlog = jnp.log(tmass)

    ct, cs = cross_tile(target_lanes, tlog, source_lanes, slog)
    ss = self_tile(source_set, source_lanes, slog, flip)
    st = self_tile(target_set, target_lanes, tlog, level)
    by_row = collect(jnp.concatenate([ct, ss], axis=1), "row")
    ct = log_sum([part[:, :nt] for part in by_row])
    ss = tree([part[:, nt:] for part in by_row], jnp.add)
    by_col = gather(jnp.concatenate([cs, st], axis=1), "col")
    cs = log_sum([part[:, :ns] for part in by_col])
    st = tree([part[:, ns:] for part in by_col], jnp.add)
    cross_source = -half * (cs - slog)
    cross_target = -half * (ct - tlog)
    z = slog + cross_source / EPSILON
    w = tlog + cross_target / EPSILON
    ct, cs = cross_tile(target_lanes, w, source_lanes, z)
    ss_again = again_tile(source_set, ss, source_lanes, flip)
    st_again = again_tile(target_set, st, target_lanes, level)

    ss_mine = -half * jnp.log(lax.dynamic_slice_in_dim(ss, row * ps, ps, 1))
    st_mine = -half * jnp.log(lax.dynamic_slice_in_dim(st, col * pt, pt, 1))
    by_col = gather(jnp.concatenate([cs, ss_again, ss_mine], axis=1), "col")
    by_row = collect(jnp.concatenate([ct, st_again, st_mine], axis=1), "row")
    cs = log_sum([part[:, :ns] for part in by_col])
    ss_again = tree([part[:, ns : 2 * ns] for part in by_col], jnp.add)
    ss = by_col[:, :, 2 * ns :].reshape(1, ns)
    ct = log_sum([part[:, :nt] for part in by_row])
    st_again = tree([part[:, nt : 2 * nt] for part in by_row], jnp.add)
    st = jnp.zeros((1, nt), jnp.float32)
    for k, part in enumerate(by_row):
        st = lax.dynamic_update_slice(st, part[:, 2 * nt :], (0, (row ^ k) * pt))
    cross_source = 0.5 * cross_source - half * (cs - z)
    cross_target = 0.5 * cross_target - half * (ct - w)
    self_source = 0.5 * ss - half * jnp.log(ss_again)
    self_target = 0.5 * st - half * jnp.log(st_again)
    return (cross_source[0], cross_target[0], self_source[0], self_target[0])


def solution(mesh):
    return jax.shard_map(
        body,
        mesh=mesh,
        in_specs=(P("row", "col"), P("col", None), P("row"), P("col")),
        out_specs=(P("row"), P("col"), P("row"), P("col")),
        check_vma=False,
    )
```

time: 133 us -> 115 us (0.86)
  Pallas kernels: 58.5 us -> 47.9 us
  other arithmetic: 12.3 us -> 7.79 us
  local copies, waits for them, and re-layouts: 11.3 us -> 7.43 us
  waiting for transfers between devices: 21.5 us -> 23.4 us
    pallas_call x6, Pallas kernels: 58.5 us -> 47.9 us  [the longest x2 22.8 us: cross_tile(): pl.pallas_call(cross_kernel, grid=(nt // bt,), in_specs=[pl.BlockSpec((ch...]
    all_to_all x3 -> x4, waiting for transfers between devices: 11 us -> 20.2 us  [gather(): lax.all_to_all(jnp.broadcast_to(x[None], (count,) + x.shape), axis, 0, 0)]
    ppermute x10 -> x9, waiting for transfers between devices: 10.5 us -> 3.19 us  [collect(): lax.ppermute(x, axis, [(i, i ^ k) for i in range(count)])]
    ppermute x10 -> x9, starting transfers between devices: 11.5 us -> 5.74 us  [collect(): lax.ppermute(x, axis, [(i, i ^ k) for i in range(count)])]
    all_to_all x3 -> x4, starting transfers between devices: 14.8 us -> 20.5 us  [gather(): lax.all_to_all(jnp.broadcast_to(x[None], (count,) + x.shape), axis, 0, 0)]
    reshape x4 -> x0, local copies, waits for them, and re-layouts: 3.31 us -> none  [the longest x2 3.09 us: unpacked(): points = flat[:, :count * (width - 1)].reshape(-1, width - 1)]
    add x14 -> x2, other arithmetic: 2.9 us -> 0.07 us  [tree(): parts = [op(parts[k], parts[k + 1]) for k in range(0, len(parts), 2)]]
    dynamic_slice x4 -> x0, local copies, waits for them, and re-layouts: 2.48 us -> none  [the longest x2 0.96 us: body(): piece = lax.dynamic_slice_in_dim(target_desc, row * pt, pt, 0)]
  transfers between devices with their start and end apart: 13 -> 13, of which waited for: 7 -> 5; matrix products, arithmetic and copies ran while one was open for 11% -> 5% of each run, Pallas kernels for 20% -> 17%
where the time goes in v2:
time: 115 us; the launch traced here: 114 us
  Pallas kernels  47.9 us (42%)
  starting transfers between devices  26.2 us (23%)
  waiting for transfers between devices  23.4 us (20%)
  other arithmetic  7.79 us (7%)
  local copies, waits for them, and re-layouts  7.43 us (6%)
    pallas_call x2, Pallas kernels, cross_tile(): pl.pallas_call(cross_kernel, grid=(nt // bt,), in_specs=[pl.BlockSpec((ch...  22.8 us
    all_to_all x4, starting transfers between devices, gather(): lax.all_to_all(jnp.broadcast_to(x[None], (count,) + x.shape), axis, 0, 0)  20.5 us
    all_to_all x4, waiting for transfers between devices, gather(): lax.all_to_all(jnp.broadcast_to(x[None], (count,) + x.shape), axis, 0, 0)  20.2 us
    pallas_call x2, Pallas kernels, self_tile(): pl.pallas_call(self_kernel, grid_spec=pltpu.PrefetchScalarGridSpec(num_sc...  12.8 us
    pallas_call x2, Pallas kernels, again_tile(): pl.pallas_call(again_kernel, grid_spec=pltpu.PrefetchScalarGridSpec(num_s...  12.3 us
    ppermute x9, starting transfers between devices, collect(): lax.ppermute(x, axis, [(i, i ^ k) for i in range(count)])  5.74 us
    broadcast_in_dim x4, local copies, waits for them, and re-layouts, gather(): jnp.broadcast_to(x[None], (count,) + x.shape)  3.88 us
    unnamed x32, local copies, waits for them, and re-layouts  3.47 us
  transfers between devices with their start and end apart: 13, of which 5 were waited for; matrix products, arithmetic and copies ran while one was open for 5% of the time, Pallas kernels for 17%

profile of v2, /device:TPU:0, one launch (start us, length us, event | category | flops | bytes accessed | tf_op | source)
XLA Modules:
  0.0 113.7 jit_solution(18441703865117554510)
XLA Ops:
  0.6 1.5 %broadcast_in_dim.40 = bf16[8,8,2048]{2,1,0:T(8,128)(2,1)} broadcast(bf16[8,2048]{1,0:T(8,128)(2,1)} %bitcast.72), dimensions={1,2} | broadcast | bytes 294912 | tf_op jit(solution)/shard_map/broadcast_in_dim | solution.py:226
  2.1 7.4 %all-to-all-start = ((bf16[8,8,2048]{2,1,0:T(8,128)(2,1)}), bf16[8,8,2048]{2,1,0:T(8,128)(2,1)S(1)}, u32[]{:S(2)}, u32[]{:S(2)}) async-start(bf16[8,8,2048]{2,1,0:T(8,128)(2,1)} %broadcast_in_dim.40), calls=%async_computation | async-start | bytes 524288 | tf_op jit(solution)/shard_map/all_to_all | solution.py:226
  9.5 0.7 copy-done.10
  12.2 6.3 %all-to-all-done = bf16[8,8,2048]{2,1,0:T(8,128)(2,1)S(1)} async-done(((bf16[8,8,2048]{2,1,0:T(8,128)(2,1)}), bf16[8,8,2048]{2,1,0:T(8,128)(2,1)S(1)}, u32[]{:S(2)}, u32[]{:S(2)}) %all-to-all-start) | async-done | bytes 262176 | tf_op jit(solution)/shard_map/all_to_all | solution.py:226
  18.4 0.9 broadcast_in_dim.42
  19.4 3.6 %all-to-all-start.1 = ((bf16[8,65,512]{2,1,0:T(8,128)(2,1)}), bf16[8,65,512]{2,1,0:T(8,128)(2,1)S(1)}, u32[]{:S(2)}, u32[]{:S(2)}) async-start(bf16[8,65,512]{2,1,0:T(8,128)(2,1)} %broadcast_in_dim.42), calls=%async_computation.1 | async-start | bytes 1179648 | tf_op jit(solution)/shard_map/all_to_all | solution.py:226
  23.0 1.6 %collective-permute-start.1 = (bf16[65,256]{1,0:T(8,128)(2,1)S(1)}, bf16[65,256]{1,0:T(8,128)(2,1)S(1)}, u32[]{:S(2)}, u32[]{:S(2)}) collective-permute-start(bf16[65,256]{1,0:T(8,128)(2,1)S(1)} %fusion.1), channel_id=1, source_target_pairs={{0,16},{8,24},{16,0},{24,8},{1,17},{9,25},{17,1},{25,9},{2,18},{10... | collective-permute-start | bytes 99848 | tf_op jit(solution)/shard_map/ppermute | solution.py:232
  24.9 11.4 %cross_tile.2 = (f32[1,2048]{1,0:T(1,128)}, f32[1,2048]{1,0:T(1,128)}) custom-call(bf16[64,2048]{1,0:T(8,128)(2,1)} %bitcast.55, f32[1,2048]{1,0:T(1,128)} %bitcast.61, bf16[64,2048]{1,0:T(8,128)(2,1)} %bitcast.50, f32[1,2048]{1,0:T(1,128)} %bitcast.65), custom_call_target="tpu_custom_call" | custom-call | flops 2147483648 | bytes 1048576 | tf_op jit(solution)/shard_map/cross_tile/pallas_call | solution.py:112
  36.4 0.7 pad_maximum_fusion.u_ref
  37.1 4.2 %self_tile.3 = f32[1,1024]{1,0:T(1,128)} custom-call(s32[1]{0:T(128)} %bitcast.14.flip, bf16[4,65,256]{2,1,0:T(8,128)(2,1)} %pad_maximum_fusion.u_ref, bf16[64,2048]{1,0:T(8,128)(2,1)} %bitcast.51, f32[1,2048]{1,0:T(1,128)} %bitcast.66), custom_call_target="tpu_custom_call" | custom-call | flops 545259520 | bytes 66560 | tf_op jit(solution)/shard_map/self_tile/pallas_call | solution.py:180
  41.3 0.7 pad_maximum_fusion.3
  42.4 1.5 %collective-permute-start.4 = (f32[1,3072]{1,0:T(1,128)S(1)}, f32[1,3072]{1,0:T(1,128)S(1)}, u32[]{:S(2)}, u32[]{:S(2)}) collective-permute-start(f32[1,3072]{1,0:T(1,128)S(1)} %pad_maximum_fusion.3), channel_id=1, source_target_pairs={{0,16},{8,24},{16,0},{24,8},{1,17},{9,25},{17,1},{25,9},{2,18},{10... | collective-permute-start | bytes 36872 | tf_op jit(solution)/shard_map/ppermute | solution.py:232
  43.9 2.2 %collective-permute-done.4 = f32[1,3072]{1,0:T(1,128)S(1)} collective-permute-done((f32[1,3072]{1,0:T(1,128)S(1)}, f32[1,3072]{1,0:T(1,128)S(1)}, u32[]{:S(2)}, u32[]{:S(2)}) %collective-permute-start.4) | collective-permute-done | bytes 12320 | tf_op jit(solution)/shard_map/ppermute | solution.py:232
  46.1 1.0 collective-permute-done.5
  47.2 0.8 copy-done.2
  48.0 8.6 %self_tile.2 = f32[1,4096]{1,0:T(1,128)} custom-call(s32[1]{0:T(128)} %constant.18.clone.1.flip, bf16[8,65,512]{2,1,0:T(8,128)(2,1)} %copy-done.2, bf16[64,2048]{1,0:T(8,128)(2,1)} %bitcast.56, f32[1,2048]{1,0:T(1,128)} %bitcast.62), custom_call_target="tpu_custom_call" | custom-call | flops 2181038080 | bytes 266240 | tf_op jit(solution)/shard_map/self_tile/pallas_call | solution.py:180
  56.6 0.7 pad_maximum_fusion.1
  57.3 0.8 broadcast_in_dim.44
  58.1 6.1 %all-to-all-start.2 = ((f32[8,1,6144]{2,1,0:T(1,128)}), f32[8,1,6144]{2,1,0:T(1,128)S(1)}, u32[]{:S(2)}, u32[]{:S(2)}) async-start(f32[8,1,6144]{2,1,0:T(1,128)} %broadcast_in_dim.44), calls=%async_computation.2 | async-start | bytes 393216 | tf_op jit(solution)/shard_map/all_to_all | solution.py:226
  64.9 7.6 %all-to-all-done.2 = f32[8,1,6144]{2,1,0:T(1,128)S(1)} async-done(((f32[8,1,6144]{2,1,0:T(1,128)}), f32[8,1,6144]{2,1,0:T(1,128)S(1)}, u32[]{:S(2)}, u32[]{:S(2)}) %all-to-all-start.2) | async-done | bytes 196640 | tf_op jit(solution)/shard_map/all_to_all | solution.py:226
  73.2 0.7 multiply_add_fusion
  73.9 11.4 %cross_tile.3 = (f32[1,2048]{1,0:T(1,128)}, f32[1,2048]{1,0:T(1,128)}) custom-call(bf16[64,2048]{1,0:T(8,128)(2,1)} %bitcast.57, f32[1,2048]{1,0:T(1,128)} %get-tuple-element.16.w_ref, bf16[64,2048]{1,0:T(8,128)(2,1)} %bitcast.52, f32[1,2048]{1,0:T(1,128)} %get-tuple-element.14.z_ref), custom_call_target="tpu_custom_call" | custom-call | flops 2147483648 | bytes 1048576 | tf_op jit(solution)/shard_map/cross_tile/pallas_call | solution.py:112
  85.3 8.3 %again_tile.3 = f32[1,2048]{1,0:T(1,128)} custom-call(s32[1]{0:T(128)} %constant.18.clone.1.flip, bf16[8,65,512]{2,1,0:T(8,128)(2,1)} %copy-done.2, f32[1,4096]{1,0:T(1,128)} %copy-done.9, bf16[64,2048]{1,0:T(8,128)(2,1)} %bitcast.58), custom_call_target="tpu_custom_call" | custom-call | flops 2181038080 | bytes 266240 | tf_op jit(solution)/shard_map/again_tile/pallas_call | solution.py:202
  93.6 0.7 pad_maximum_fusion.2
  94.4 4.0 %again_tile.2 = f32[1,2048]{1,0:T(1,128)} custom-call(s32[1]{0:T(128)} %bitcast.14.flip, bf16[4,65,256]{2,1,0:T(8,128)(2,1)} %pad_maximum_fusion.u_ref, f32[1,1024]{1,0:T(1,128)} %copy-done.15, bf16[64,2048]{1,0:T(8,128)(2,1)} %bitcast.53), custom_call_target="tpu_custom_call" | custom-call | flops 545259520 | bytes 66560 | tf_op jit(solution)/shard_map/again_tile/pallas_call | solution.py:202
  99.0 1.3 %collective-permute-start.8 = (f32[1,4608]{1,0:T(1,128)S(1)}, f32[1,4608]{1,0:T(1,128)S(1)}, u32[]{:S(2)}, u32[]{:S(2)}) collective-permute-start(f32[1,4608]{1,0:T(1,128)S(1)} %pad_maximum_fusion.2), channel_id=1, source_target_pairs={{0,24},{8,16},{16,8},{24,0},{1,25},{9,17},{17,9},{25,1},{2,26},{10... | collective-permute-start | bytes 55304 | tf_op jit(solution)/shard_map/ppermute | solution.py:232
  100.2 0.7 maximum_reduce_fusion
  101.0 0.7 broadcast_in_dim.48
  101.7 3.4 %all-to-all-start.3 = ((f32[8,1,4352]{2,1,0:T(1,128)}), f32[8,1,4352]{2,1,0:T(1,128)S(1)}, u32[]{:S(2)}, u32[]{:S(2)}) async-start(f32[8,1,4352]{2,1,0:T(1,128)} %broadcast_in_dim.48), calls=%async_computation.3 | async-start | bytes 278528 | tf_op jit(solution)/shard_map/all_to_all | solution.py:226
  105.8 0.7 multiply_subtract_fusion
  106.5 6.4 %all-to-all-done.3 = f32[8,1,4352]{2,1,0:T(1,128)S(1)} async-done(((f32[8,1,4352]{2,1,0:T(1,128)}), f32[8,1,4352]{2,1,0:T(1,128)S(1)}, u32[]{:S(2)}, u32[]{:S(2)}) %all-to-all-start.3) | async-done | bytes 139296 | tf_op jit(solution)/shard_map/all_to_all | solution.py:226
  112.9 0.8 multiply_subtract_fusion.1
  (63 shorter events, 5.5 us)
Async XLA Ops:
  2.1 8.1 %copy-start.3 = (bf16[2048,64]{0,1:T(8,128)(2,1)S(1)}, bf16[2048,64]{0,1:T(8,128)(2,1)}, u32[]{:S(2)}) copy-start(bf16[2048,64]{0,1:T(8,128)(2,1)} %param.5) | copy-start | bytes 786436
  2.1 16.3 %all-to-all-start = ((bf16[8,8,2048]{2,1,0:T(8,128)(2,1)}), bf16[8,8,2048]{2,1,0:T(8,128)(2,1)S(1)}, u32[]{:S(2)}, u32[]{:S(2)}) async-start(bf16[8,8,2048]{2,1,0:T(8,128)(2,1)} %broadcast_in_dim.40), calls=%async_computation | async-start | bytes 524288 | tf_op jit(solution)/shard_map/all_to_all | solution.py:226
  9.5 0.7 copy-start.10
  10.2 0.7 copy-start.11
  18.4 4.5 %copy-start = (bf16[8,8,2048]{2,1,0:T(8,128)(2,1)}, bf16[8,8,2048]{2,1,0:T(8,128)(2,1)S(1)}, u32[]{:S(2)}) copy-start(bf16[8,8,2048]{2,1,0:T(8,128)(2,1)S(1)} %all-to-all-done) | copy-start | bytes 786436
  19.4 27.8 %all-to-all-start.1 = ((bf16[8,65,512]{2,1,0:T(8,128)(2,1)}), bf16[8,65,512]{2,1,0:T(8,128)(2,1)S(1)}, u32[]{:S(2)}, u32[]{:S(2)}) async-start(bf16[8,65,512]{2,1,0:T(8,128)(2,1)} %broadcast_in_dim.42), calls=%async_computation.1 | async-start | bytes 1179648 | tf_op jit(solution)/shard_map/all_to_all | solution.py:226
  23.0 13.4 %collective-permute-start = (bf16[65,256]{1,0:T(8,128)(2,1)S(1)}, bf16[65,256]{1,0:T(8,128)(2,1)S(1)}, u32[]{:S(2)}, u32[]{:S(2)}) collective-permute-start(bf16[65,256]{1,0:T(8,128)(2,1)S(1)} %fusion.1), channel_id=1, source_target_pairs={{0,8},{8,0},{16,24},{24,16},{1,9},{9,1},{17,25},{25,17},{2,10},{10... | collective-permute-start | bytes 99848 | tf_op jit(solution)/shard_map/ppermute | solution.py:232
  23.0 13.3 %collective-permute-start.1 = (bf16[65,256]{1,0:T(8,128)(2,1)S(1)}, bf16[65,256]{1,0:T(8,128)(2,1)S(1)}, u32[]{:S(2)}, u32[]{:S(2)}) collective-permute-start(bf16[65,256]{1,0:T(8,128)(2,1)S(1)} %fusion.1), channel_id=1, source_target_pairs={{0,16},{8,24},{16,0},{24,8},{1,17},{9,25},{17,1},{25,9},{2,18},{10... | collective-permute-start | bytes 99848 | tf_op jit(solution)/shard_map/ppermute | solution.py:232
  24.6 11.7 %collective-permute-start.2 = (bf16[65,256]{1,0:T(8,128)(2,1)S(1)}, bf16[65,256]{1,0:T(8,128)(2,1)S(1)}, u32[]{:S(2)}, u32[]{:S(2)}) collective-permute-start(bf16[65,256]{1,0:T(8,128)(2,1)S(1)} %fusion.1), channel_id=1, source_target_pairs={{0,24},{8,16},{16,8},{24,0},{1,25},{9,17},{17,9},{25,1},{2,26},{10... | collective-permute-start | bytes 99848 | tf_op jit(solution)/shard_map/ppermute | solution.py:232
  24.9 11.4 %copy-start.1 = (bf16[8,8,2048]{2,1,0:T(8,128)(2,1)S(1)}, bf16[8,8,2048]{2,1,0:T(8,128)(2,1)}, u32[]{:S(2)}) copy-start(bf16[8,8,2048]{2,1,0:T(8,128)(2,1)} %copy-done) | copy-start | bytes 786436
  37.1 4.2 %copy-start.6 = (f32[1,2048]{1,0:T(1,128)S(1)}, f32[1,2048]{1,0:T(1,128)}, u32[]{:S(2)}) copy-start(f32[1,2048]{1,0:T(1,128)} %get-tuple-element.9) | copy-start | bytes 24580
  42.0 1.9 %collective-permute-start.3 = (f32[1,3072]{1,0:T(1,128)S(1)}, f32[1,3072]{1,0:T(1,128)S(1)}, u32[]{:S(2)}, u32[]{:S(2)}) collective-permute-start(f32[1,3072]{1,0:T(1,128)S(1)} %pad_maximum_fusion.3), channel_id=1, source_target_pairs={{0,8},{8,0},{16,24},{24,16},{1,9},{9,1},{17,25},{25,17},{2,10},{10... | collective-permute-start | bytes 36872 | tf_op jit(solution)/shard_map/ppermute | solution.py:232
  42.4 3.7 %collective-permute-start.4 = (f32[1,3072]{1,0:T(1,128)S(1)}, f32[1,3072]{1,0:T(1,128)S(1)}, u32[]{:S(2)}, u32[]{:S(2)}) collective-permute-start(f32[1,3072]{1,0:T(1,128)S(1)} %pad_maximum_fusion.3), channel_id=1, source_target_pairs={{0,16},{8,24},{16,0},{24,8},{1,17},{9,25},{17,1},{25,9},{2,18},{10... | collective-permute-start | bytes 36872 | tf_op jit(solution)/shard_map/ppermute | solution.py:232
  43.9 3.2 %collective-permute-start.5 = (f32[1,3072]{1,0:T(1,128)S(1)}, f32[1,3072]{1,0:T(1,128)S(1)}, u32[]{:S(2)}, u32[]{:S(2)}) collective-permute-start(f32[1,3072]{1,0:T(1,128)S(1)} %pad_maximum_fusion.3), channel_id=1, source_target_pairs={{0,24},{8,16},{16,8},{24,0},{1,25},{9,17},{17,9},{25,1},{2,26},{10... | collective-permute-start | bytes 36872 | tf_op jit(solution)/shard_map/ppermute | solution.py:232
  43.9 3.2 %copy-start.12 = (f32[1,1024]{1,0:T(1,128)S(1)}, f32[1,1024]{1,0:T(1,128)}, u32[]{:S(2)}) copy-start(f32[1,1024]{1,0:T(1,128)} %self_tile.3) | copy-start | bytes 12292
  47.1 9.5 %copy-start.15 = (f32[1,1024]{1,0:T(1,128)}, f32[1,1024]{1,0:T(1,128)S(1)}, u32[]{:S(2)}) copy-start(f32[1,1024]{1,0:T(1,128)S(1)} %fusion.9.w_ref) | copy-start | bytes 12292
  47.1 9.5 %copy-start.14 = (f32[1,2048]{1,0:T(1,128)S(1)}, f32[1,2048]{1,0:T(1,128)}, u32[]{:S(2)}) copy-start(f32[1,2048]{1,0:T(1,128)} %get-tuple-element.8) | copy-start | bytes 24580
  47.2 0.8 copy-start.2
  58.1 6.1 %copy-start.4 = (f32[2048]{0:T(1024)S(1)}, f32[2048]{0:T(1024)}, u32[]{:S(2)}) copy-start(f32[2048]{0:T(1024)} %convert_log_fusion.1) | copy-start | bytes 24580
  58.1 14.3 %all-to-all-start.2 = ((f32[8,1,6144]{2,1,0:T(1,128)}), f32[8,1,6144]{2,1,0:T(1,128)S(1)}, u32[]{:S(2)}, u32[]{:S(2)}) async-start(f32[8,1,6144]{2,1,0:T(1,128)} %broadcast_in_dim.44), calls=%async_computation.2 | async-start | bytes 393216 | tf_op jit(solution)/shard_map/all_to_all | solution.py:226
  72.5 0.7 copy-start.5
  73.2 12.1 %copy-start.9 = (f32[1,4096]{1,0:T(1,128)}, f32[1,4096]{1,0:T(1,128)S(1)}, u32[]{:S(2)}) copy-start(f32[1,4096]{1,0:T(1,128)S(1)} %fusion.3.w_ref) | copy-start | bytes 49156
  85.3 8.3 %copy-start.7 = (f32[1,2048]{1,0:T(1,128)S(1)}, f32[1,2048]{1,0:T(1,128)}, u32[]{:S(2)}) copy-start(f32[1,2048]{1,0:T(1,128)} %get-tuple-element.11) | copy-start | bytes 24580
  94.3 5.9 %copy-start.13 = (f32[1,2048]{1,0:T(1,128)S(1)}, f32[1,2048]{1,0:T(1,128)}, u32[]{:S(2)}) copy-start(f32[1,2048]{1,0:T(1,128)} %get-tuple-element.10) | copy-start | bytes 24580
  94.3 10.8 %collective-permute-start.6 = (f32[1,4608]{1,0:T(1,128)S(1)}, f32[1,4608]{1,0:T(1,128)S(1)}, u32[]{:S(2)}, u32[]{:S(2)}) collective-permute-start(f32[1,4608]{1,0:T(1,128)S(1)} %pad_maximum_fusion.2), channel_id=1, source_target_pairs={{0,8},{8,0},{16,24},{24,16},{1,9},{9,1},{17,25},{25,17},{2,10},{10... | collective-permute-start | bytes 55304 | tf_op jit(solution)/shard_map/ppermute | solution.py:232
  98.4 6.7 %collective-permute-start.7 = (f32[1,4608]{1,0:T(1,128)S(1)}, f32[1,4608]{1,0:T(1,128)S(1)}, u32[]{:S(2)}, u32[]{:S(2)}) collective-permute-start(f32[1,4608]{1,0:T(1,128)S(1)} %pad_maximum_fusion.2), channel_id=1, source_target_pairs={{0,16},{8,24},{16,0},{24,8},{1,17},{9,25},{17,1},{25,9},{2,18},{10... | collective-permute-start | bytes 55304 | tf_op jit(solution)/shard_map/ppermute | solution.py:232
  99.0 6.2 %collective-permute-start.8 = (f32[1,4608]{1,0:T(1,128)S(1)}, f32[1,4608]{1,0:T(1,128)S(1)}, u32[]{:S(2)}, u32[]{:S(2)}) collective-permute-start(f32[1,4608]{1,0:T(1,128)S(1)} %pad_maximum_fusion.2), channel_id=1, source_target_pairs={{0,24},{8,16},{16,8},{24,0},{1,25},{9,17},{17,9},{25,1},{2,26},{10... | collective-permute-start | bytes 55304 | tf_op jit(solution)/shard_map/ppermute | solution.py:232
  101.7 11.2 %all-to-all-start.3 = ((f32[8,1,4352]{2,1,0:T(1,128)}), f32[8,1,4352]{2,1,0:T(1,128)S(1)}, u32[]{:S(2)}, u32[]{:S(2)}) async-start(f32[8,1,4352]{2,1,0:T(1,128)} %broadcast_in_dim.48), calls=%async_computation.3 | async-start | bytes 278528 | tf_op jit(solution)/shard_map/all_to_all | solution.py:226
  105.1 0.7 copy-start.8

commit v3 on v2

v3 whole, which is shorter than its diff:
```python
import functools
import math

import jax, jax.numpy as jnp
from jax import lax
from jax.experimental import pallas as pl
from jax.experimental.pallas import tpu as pltpu
from jax.sharding import PartitionSpec as P


EPSILON = 0.25
REACH = 1.0
DAMPING = 1.0 / (1.0 + EPSILON / REACH)

STRIP = 256
EXTRA = 16
GROUP = 1024


def split3(x):
    hi = x.astype(jnp.bfloat16).astype(jnp.float32)
    rest = x - hi
    mid = rest.astype(jnp.bfloat16).astype(jnp.float32)
    return hi, mid, rest - mid


def operand(desc, weight, scale, own):
    wide = desc.astype(jnp.float32)
    bias = weight - 2.0 * jnp.sum(wide * wide, axis=0, keepdims=True)
    hi, mid, lo = split3(bias)
    row = lax.broadcasted_iota(jnp.int32, (EXTRA, wide.shape[1]), 0) - own
    other = jnp.where((row + own >= 3 - own) & (row + own < 6 - own), 1.0, 0.0)
    extra = jnp.where(row == 0, hi, jnp.where(row == 1, mid, jnp.where(row == 2, lo, other)))
    main = desc if scale == 1.0 else (scale * wide).astype(jnp.bfloat16)
    return jnp.concatenate([main, extra.astype(jnp.bfloat16)], axis=0)


def scores(lhs, rhs):
    return lax.dot_general(lhs, rhs, (((0,), (0,)), ((), ())), preferred_element_type=jnp.float32)


def to_lanes(block):
    tiles = [block[k : k + 128, :].T[0:1, :] for k in range(0, block.shape[0], 128)]
    return jnp.concatenate(tiles, axis=1)


def rows_sum_lanes(block):
    tiles = [
        jnp.sum(block[k : k + 128, :].T, axis=0, keepdims=True)
        for k in range(0, block.shape[0], 128)
    ]
    return jnp.concatenate(tiles, axis=1)


def fold_rows(x, op):
    parts = [x[k : k + 8, :] for k in range(0, x.shape[0], 8)]
    while len(parts) > 1:
        pairs = [op(parts[k], parts[k + 1]) for k in range(0, len(parts) - 1, 2)]
        parts = pairs + parts[len(pairs) * 2 :]
    return parts[0]


def fold_lanes(x, op):
    return functools.reduce(op, [x[:, k : k + 128] for k in range(0, x.shape[1], 128)])


def whole(shape):
    return pl.BlockSpec(shape, lambda *i: (0,) * len(shape))


def damped(log_mass, log_total):
    return log_mass - 0.5 * DAMPING * (log_total - log_mass)


def tree(parts, op):
    while len(parts) > 1:
        parts = [op(parts[k], parts[k + 1]) for k in range(0, len(parts), 2)]
    return parts[0]


def log_sum(parts):
    top = tree(parts, jnp.maximum)
    return top + jnp.log(tree([jnp.exp(part - top) for part in parts], jnp.add))


def start_cross(s, z, rhs, ctop, csum):
    rhs[...] = operand(s, z, 4.0, 0)
    ctop[...] = jnp.full(ctop.shape, -jnp.inf, jnp.float32)
    csum[...] = jnp.zeros(csum.shape, jnp.float32)


def cross_block(t, w, rhs, fbuf, ctop, csum):
    n = rhs.shape[1]
    bt = t.shape[1]
    lhs = operand(t, w, 1.0, 3)
    rmax = None
    for k in range(0, n, STRIP):
        f = scores(lhs, rhs[:, k : k + STRIP])
        fbuf[:, k : k + STRIP] = f
        m = fold_lanes(f, jnp.maximum)
        rmax = m if rmax is None else jnp.maximum(rmax, m)
        top = jnp.max(fold_rows(f, jnp.maximum), axis=0, keepdims=True)
        old = ctop[:, k : k + STRIP]
        new = jnp.maximum(old, top)
        csum[:, k : k + STRIP] = csum[:, k : k + STRIP] * jnp.exp(old - new)
        ctop[:, k : k + STRIP] = new
    r1 = jnp.max(rmax, axis=1, keepdims=True)
    r = jnp.broadcast_to(r1, (bt, 128))
    racc = jnp.zeros((bt, 128), jnp.float32)
    for h in range(0, n, 128):
        f = fbuf[:, h : h + 128]
        racc = racc + jnp.exp(f - r)
        e2 = jnp.exp(f - ctop[0:1, h : h + 128])
        csum[:, h : h + 128] = csum[:, h : h + 128] + fold_rows(e2, jnp.add)
    total = jnp.sum(racc, axis=1, keepdims=True)
    return to_lanes(jnp.broadcast_to(r1 + jnp.log(total), (bt, 128)))


def col_logs(ctop, csum):
    return ctop[0:1, :] + jnp.log(jnp.sum(csum[...], axis=0, keepdims=True))


def last_step():
    return pl.program_id(0) == pl.num_programs(0) - 1


def cross_kernel(t_ref, w_ref, s_ref, z_ref, row_ref, col_ref, *scratch):
    rhs, _, ctop, csum = scratch

    @pl.when(pl.program_id(0) == 0)
    def _():
        start_cross(s_ref[...], z_ref[...], rhs, ctop, csum)

    row_ref[...] = cross_block(t_ref[...], w_ref[...], *scratch)

    @pl.when(last_step())
    def _():
        col_ref[...] = col_logs(ctop, csum)


def cross_scratch(ch, bt, n):
    return [
        pltpu.VMEM((ch + EXTRA, n), jnp.bfloat16),
        pltpu.VMEM((bt, n), jnp.float32),
        pltpu.VMEM((8, n), jnp.float32),
        pltpu.VMEM((8, n), jnp.float32),
    ]


def cross_cost(nt, n, ch):
    return pl.CostEstimate(
        flops=8 * nt * n * ch, bytes_accessed=4 * (nt + n) * ch, transcendentals=2 * nt * n
    )


def cross_tile(t, w, s, z):
    ch, nt = t.shape
    n = s.shape[1]
    bt = math.gcd(GROUP, nt)
    lanes = pl.BlockSpec((1, bt), lambda i: (0, i))
    return pl.pallas_call(
        cross_kernel,
        grid=(nt // bt,),
        in_specs=[pl.BlockSpec((ch, bt), lambda i: (0, i)), lanes, whole((ch, n)), whole((1, n))],
        out_specs=[lanes, whole((1, n))],
        out_shape=[jax.ShapeDtypeStruct((1, k), jnp.float32) for k in (nt, n)],
        scratch_shapes=cross_scratch(ch, bt, n),
        cost_estimate=cross_cost(nt, n, ch),
        name="cross_tile",
    )(t, w, s, z)


def cross_again_kernel(count, t_ref, tl_ref, s_ref, sl_ref, cols_ref, more_ref, *refs):
    parts = refs[:count]
    row_ref, w_ref, z_ref, col_ref = refs[count : count + 4]
    scratch = refs[count + 4 :]
    rhs, _, ctop, csum = scratch
    n = s_ref.shape[1]

    @pl.when(pl.program_id(0) == 0)
    def _():
        cs = log_sum([cols_ref[k, :, 0:n] for k in range(cols_ref.shape[0])])
        z = damped(sl_ref[...], cs)
        z_ref[...] = z
        start_cross(s_ref[...], z, rhs, ctop, csum)

    w = damped(tl_ref[...], log_sum([part[0] for part in parts]))
    w_ref[...] = w
    row_ref[...] = cross_block(t_ref[...], w, *scratch)

    @pl.when(last_step())
    def _():
        logs = col_logs(ctop, csum)
        for k in range(col_ref.shape[0]):
            col_ref[k, :, 0:n] = logs
            col_ref[k, :, n:] = more_ref[...]


def cross_again(t, tlog, s, slog, by_col, by_row, more):
    ch, nt = t.shape
    n = s.shape[1]
    bt = math.gcd(GROUP, nt)
    lanes = pl.BlockSpec((1, bt), lambda i: (0, i))
    copies = by_col.shape[0]
    shape = (copies, 1, n + more.shape[1])
    return pl.pallas_call(
        functools.partial(cross_again_kernel, len(by_row)),
        grid=(nt // bt,),
        in_specs=[
            pl.BlockSpec((ch, bt), lambda i: (0, i)),
            lanes,
            whole((ch, n)),
            whole((1, n)),
            whole(by_col.shape),
            whole(more.shape),
        ]
        + [pl.BlockSpec((1, 1, bt), lambda i: (0, 0, i))] * len(by_row),
        out_specs=[lanes, lanes, whole((1, n)), whole(shape)],
        out_shape=[jax.ShapeDtypeStruct(k, jnp.float32) for k in ((1, nt), (1, nt), (1, n), shape)],
        scratch_shapes=cross_scratch(ch, bt, n),
        cost_estimate=cross_cost(nt, n, ch),
        name="cross_again",
    )(t, tlog, s, slog, by_col, more, *by_row)


def points(flip, u_ref, ch):
    group = u_ref.shape[0]
    order = [k ^ (flip[0] & (group - 1)) for k in range(group)]
    return [jnp.concatenate([u_ref[k, a:b, :] for k in order], axis=1) for a, b in ((0, ch), (ch, ch + 1))]


def self_kernel(flip, u_ref, s_ref, z_ref, more_ref, out_ref, rhs):
    i = pl.program_id(0)
    ch, n = s_ref.shape
    extra = more_ref.shape[1]

    @pl.when(i == 0)
    def _():
        rhs[...] = operand(s_ref[...], z_ref[...], 4.0, 0)
        for k in range(out_ref.shape[0]):
            out_ref[k, :, 0:extra] = more_ref[...]

    desc, _ = points(flip, u_ref, ch)
    bt = desc.shape[1]
    lhs = operand(desc, jnp.zeros((1, bt), jnp.float32), 1.0, 3)
    racc = jnp.zeros((bt, 128), jnp.float32)
    for k in range(0, n, STRIP):
        racc = racc + fold_lanes(jnp.exp(scores(lhs, rhs[:, k : k + STRIP])), jnp.add)
    sums = rows_sum_lanes(racc)
    start = pl.multiple_of(extra + i * bt, 128)
    for k in range(out_ref.shape[0]):
        out_ref[k, :, pl.ds(start, bt)] = sums


def self_cost(u, n):
    pairs = u.shape[0] * u.shape[2] * n
    return pl.CostEstimate(flops=4 * pairs * u.shape[1], bytes_accessed=u.size, transcendentals=pairs)


def grouped(u):
    blocks, depth, bt = u.shape
    group = math.gcd(blocks, max(1, GROUP // bt))
    return group, pl.BlockSpec((group, depth, bt), lambda i, f: (i ^ (f[0] // group), 0, 0))


def self_tile(u, s, z, flip, more, copies):
    blocks, _, bt = u.shape
    ch, n = s.shape
    group, block = grouped(u)
    shape = (copies, 1, more.shape[1] + blocks * bt)
    return pl.pallas_call(
        self_kernel,
        grid_spec=pltpu.PrefetchScalarGridSpec(
            num_scalar_prefetch=1,
            grid=(blocks // group,),
            in_specs=[block, whole((ch, n)), whole((1, n)), whole(more.shape)],
            out_specs=whole(shape),
            scratch_shapes=[pltpu.VMEM((ch + EXTRA, n), jnp.bfloat16)],
        ),
        out_shape=jax.ShapeDtypeStruct(shape, jnp.float32),
        cost_estimate=self_cost(u, n),
        name="self_tile",
    )(flip, u, s, z, more)


def again_kernel(skip, ahead, flip, u_ref, s_ref, more_ref, *refs):
    parts, (out_ref, rhs, csum, sums) = refs[:-4], refs[-4:]
    i = pl.program_id(0)
    ch, n = s_ref.shape
    extra = more_ref.shape[1] if ahead else 0
    own = out_ref.shape[2] - extra - n

    @pl.when(i == 0)
    def _():
        rhs[...] = operand(s_ref[...], jnp.zeros((1, n), jnp.float32), 4.0, 0)
        csum[...] = jnp.zeros(csum.shape, jnp.float32)
        pieces = [part[k, :, skip:] for part in parts for k in range(part.shape[0])]
        sums[...] = jnp.log(tree(pieces, jnp.add))
        if ahead:
            out_ref[0, :, 0:extra] = more_ref[...]

    desc, mass = points(flip, u_ref, ch)
    bt = desc.shape[1]
    logs = sums[:, pl.ds(pl.multiple_of(i * bt, 128), bt)]
    weight = jnp.log(mass.astype(jnp.float32)) - 0.5 * DAMPING * logs
    lhs = operand(desc, weight, 1.0, 3)
    for k in range(0, n, STRIP):
        part = fold_rows(jnp.exp(scores(lhs, rhs[:, k : k + STRIP])), jnp.add)
        csum[:, k : k + STRIP] = csum[:, k : k + STRIP] + part

    @pl.when(last_step())
    def _():
        out_ref[0, :, extra : extra + n] = jnp.sum(csum[...], axis=0, keepdims=True)
        mine = sums[:, pl.ds(pl.multiple_of(flip[0] * own, 128), own)]
        out_ref[0, :, extra + n :] = (-0.5 * DAMPING * EPSILON) * mine


def again_tile(u, s, flip, parts, skip, own, more=None):
    blocks, _, bt = u.shape
    ch, n = s.shape
    group, block = grouped(u)
    ahead = more is not None
    if not ahead:
        more = jnp.zeros((1, 128), jnp.float32)
    shape = (1, 1, (more.shape[1] if ahead else 0) + n + own)
    return pl.pallas_call(
        functools.partial(again_kernel, skip, ahead),
        grid_spec=pltpu.PrefetchScalarGridSpec(
            num_scalar_prefetch=1,
            grid=(blocks // group,),
            in_specs=[block, whole((ch, n)), whole(more.shape)] + [whole(part.shape) for part in parts],
            out_specs=whole(shape),
            scratch_shapes=[
                pltpu.VMEM((ch + EXTRA, n), jnp.bfloat16),
                pltpu.VMEM((8, n), jnp.float32),
                pltpu.VMEM((1, blocks * bt), jnp.float32),
            ],
        ),
        out_shape=jax.ShapeDtypeStruct(shape, jnp.float32),
        cost_estimate=self_cost(u, n),
        name="again_tile",
    )(flip, u, s, more, *parts)


def collect(x, axis):
    count = lax.axis_size(axis)
    return [x] + [
        lax.ppermute(x, axis, [(i, i ^ k) for i in range(count)]) for k in range(1, count)
    ]


def near(x, axis):
    count = lax.axis_size(axis)
    return jnp.stack([x, lax.ppermute(x, axis, [(i, i ^ 1) for i in range(count)])])


def far(pair, axis):
    count = lax.axis_size(axis)
    parts = [
        lax.ppermute(pair, axis, [(i, i ^ k) for i in range(count)]) for k in range(2, count, 2)
    ]
    return jnp.concatenate([pair] + parts, axis=0)


def swap(x, axis):
    return lax.all_to_all(x, axis, 0, 0)


def body(source_desc, target_desc, source_mass, target_mass):
    rows = lax.axis_size("row")
    cols = lax.axis_size("col")
    row = lax.axis_index("row")
    col = lax.axis_index("col")
    ns = source_mass.shape[0]
    nt = target_mass.shape[0]
    ps = ns // cols
    pt = nt // rows
    half = DAMPING * EPSILON * 0.5

    source_mass = source_mass[None]
    target_mass = target_mass[None]
    target_lanes = target_desc.T
    blocks = target_lanes.reshape(cols, -1, nt)
    target_swapped = jnp.concatenate(
        [lax.dynamic_index_in_dim(blocks, col ^ k, 0, False) for k in range(cols)], axis=0
    )
    piece = jnp.concatenate([target_lanes, target_mass], axis=0)
    piece = lax.dynamic_slice_in_dim(piece, row * pt, pt, 1)
    pair = near(source_desc.T, "col")
    target_pair = near(piece, "col")
    source_lanes = far(pair, "col").reshape(-1, ns)
    target_set = far(target_pair, "col")
    piece = jnp.concatenate([source_lanes, source_mass], axis=0)
    piece = lax.dynamic_slice_in_dim(piece, col * ps, ps, 1)
    source_set = jnp.stack(collect(piece, "row"))
    flip = row.astype(jnp.int32)[None]
    turn = col.astype(jnp.int32)[None]

    smass = source_mass.astype(jnp.float32)
    tmass = target_mass.astype(jnp.float32)
    slog = jnp.log(smass)
    tlog = jnp.log(tmass)

    ct, cs = cross_tile(target_swapped, tlog, source_lanes, slog)
    sums = self_tile(source_set, source_lanes, slog, flip, ct, 1)
    by_row = collect(sums, "row")
    sums = self_tile(target_set, target_lanes, tlog, turn, cs, cols)
    by_col = swap(sums, "col")
    more = again_tile(source_set, source_lanes, flip, by_row, nt, ps)
    ct, w, z, sums = cross_again(target_swapped, tlog, source_lanes, slog, by_col, by_row, more[0])
    last_col = swap(sums, "col")
    sums = again_tile(target_set, target_lanes, turn, [by_col], ns, pt, ct)
    last_row = [part[0] for part in collect(sums, "row")]

    cs = log_sum([part[:, :ns] for part in last_col])
    ss_again = tree([part[:, ns : 2 * ns] for part in last_col], jnp.add)
    ss = last_col[:, :, 2 * ns :].reshape(1, ns)
    ct = log_sum([part[:, :nt] for part in last_row])
    st_again = tree([part[:, nt : 2 * nt] for part in last_row], jnp.add)
    st = jnp.zeros((1, nt), jnp.float32)
    for k, part in enumerate(last_row):
        st = lax.dynamic_update_slice(st, part[:, 2 * nt :], (0, (row ^ k) * pt))
    cross_source = 0.5 * EPSILON * (z - slog) - half * (cs - z)
    cross_target = 0.5 * EPSILON * (w - tlog) - half * (ct - w)
    self_source = 0.5 * ss - half * jnp.log(ss_again)
    self_target = 0.5 * st - half * jnp.log(st_again)
    return (cross_source[0], cross_target[0], self_source[0], self_target[0])


def solution(mesh):
    return jax.shard_map(
        body,
        mesh=mesh,
        in_specs=(P("row", "col"), P("col", None), P("row"), P("col")),
        out_specs=(P("row"), P("col"), P("row"), P("col")),
        check_vma=False,
    )
```

time: 115 us -> 94.9 us (0.83)
  waiting for transfers between devices: 23.4 us -> 13.8 us
  Pallas kernels: 47.9 us -> 40.1 us
  other arithmetic: 7.79 us -> 4.37 us
  starting transfers between devices: 26.2 us -> 29.1 us
  local copies, waits for them, and re-layouts: 7.43 us -> 5.75 us
    all_to_all x4 -> x2, waiting for transfers between devices: 20.2 us -> 6.3 us  [swap(): return lax.all_to_all(x, axis, 0, 0)]
    pallas_call x2 -> x1, Pallas kernels: 22.8 us -> 9.46 us  [cross_tile(): pl.pallas_call(cross_kernel, grid=(nt // bt,), in_specs=[pl.BlockSpec((ch...]
    ppermute x0 -> x8, starting transfers between devices: none -> 12.3 us  [the longest x6 9.23 us: far(): lax.ppermute(pair, axis, [(i, i ^ k) for i in range(count)])]
    all_to_all x4 -> x2, starting transfers between devices: 20.5 us -> 11.1 us  [swap(): return lax.all_to_all(x, axis, 0, 0)]
    pallas_call x2 -> x3, Pallas kernels: 12.3 us -> 20 us  [the longest x2 10.3 us: again_tile(): pl.pallas_call(functools.partial(again_kernel, skip, ahead), grid_spec=pl...]
    broadcast_in_dim x4 -> x1, local copies, waits for them, and re-layouts: 3.88 us -> 0.51 us  [again_tile(): more = jnp.zeros((1, 128), jnp.float32)]
    concatenate x5 -> x0, other arithmetic: 2.91 us -> none  [the longest x1 0.75 us: body(): by_col = gather(jnp.concatenate([cs, ss_again, ss_mine], axis=1), 'col')]
    ppermute x0 -> x8, waiting for transfers between devices: none -> 2.26 us  [the longest x6 2.26 us: far(): lax.ppermute(pair, axis, [(i, i ^ k) for i in range(count)])]
  transfers between devices with their start and end apart: 13 -> 19, of which waited for: 5 -> 6; matrix products, arithmetic and copies ran while one was open for 5% -> 5% of each run, Pallas kernels for 17% -> 16%
where the time goes in v3:
time: 94.9 us; the launch traced here: 94.2 us
  Pallas kernels  40.1 us (42%)
  starting transfers between devices  29.1 us (31%)
  waiting for transfers between devices  13.8 us (15%)
  local copies, waits for them, and re-layouts  5.75 us (6%)
  other arithmetic  4.37 us (5%)
  between operations  1.03 us (1%)
    all_to_all x2, starting transfers between devices, swap(): return lax.all_to_all(x, axis, 0, 0)  11.1 us
    pallas_call x2, Pallas kernels, self_tile(): pl.pallas_call(self_kernel, grid_spec=pltpu.PrefetchScalarGridSpec(num_sc...  10.7 us
    pallas_call x2, Pallas kernels, again_tile(): pl.pallas_call(functools.partial(again_kernel, skip, ahead), grid_spec=pl...  10.3 us
    pallas_call x1, Pallas kernels, cross_again(): pl.pallas_call(functools.partial(cross_again_kernel, len(by_row)), grid=(...  9.73 us
    pallas_call x1, Pallas kernels, cross_tile(): pl.pallas_call(cross_kernel, grid=(nt // bt,), in_specs=[pl.BlockSpec((ch...  9.46 us
    ppermute x6, starting transfers between devices, far(): lax.ppermute(pair, axis, [(i, i ^ k) for i in range(count)])  9.23 us
    all_to_all x2, waiting for transfers between devices, swap(): return lax.all_to_all(x, axis, 0, 0)  6.3 us
    ppermute x9, starting transfers between devices, collect(): lax.ppermute(x, axis, [(i, i ^ k) for i in range(count)])  5.7 us
  transfers between devices with their start and end apart: 19, of which 6 were waited for; matrix products, arithmetic and copies ran while one was open for 5% of the time, Pallas kernels for 16%

profile of v3, /device:TPU:0, one launch (start us, length us, event | category | flops | bytes accessed | tf_op | source)
XLA Modules:
  0.0 94.2 jit_solution(439606762478869999)
XLA Ops:
  0.6 3.0 %collective-permute-start = (bf16[8,2048]{1,0:T(8,128)(2,1)}, bf16[8,2048]{1,0:T(8,128)(2,1)S(1)}, u32[]{:S(2)}, u32[]{:S(2)}) collective-permute-start(bf16[8,2048]{1,0:T(8,128)(2,1)} %bitcast.84), channel_id=1, source_target_pairs={{0,1},{1,0},{2,3},{3,2},{4,5},{5,4},{6,7},{7,6},{8,9},{9,8},{10,11... | collective-permute-start | bytes 98312 | tf_op jit(solution)/shard_map/ppermute | solution.py:354
  3.7 0.7 copy-done.8
  4.4 0.9 constant_dynamic-update-slice_fusion.17
  6.2 0.7 copy-done.9
  6.9 0.7 convert_log_fusion
  7.6 2.1 %collective-permute-start.1 = (bf16[2,8,2048]{2,1,0:T(8,128)(2,1)S(1)}, bf16[2,8,2048]{2,1,0:T(8,128)(2,1)S(1)}, u32[]{:S(2)}, u32[]{:S(2)}) collective-permute-start(bf16[2,8,2048]{2,1,0:T(8,128)(2,1)S(1)} %pad_maximum_fusion.2), channel_id=1, source_target_pairs={{0,2},{1,3},{2,0},{3,1},{4,6},{5,7},{6,4},{7,5},{8,10},{9,11},{10,... | collective-permute-start | bytes 196616 | tf_op jit(solution)/shard_map/ppermute | solution.py:360
  9.7 2.6 %collective-permute-start.2 = (bf16[2,8,2048]{2,1,0:T(8,128)(2,1)S(1)}, bf16[2,8,2048]{2,1,0:T(8,128)(2,1)S(1)}, u32[]{:S(2)}, u32[]{:S(2)}) collective-permute-start(bf16[2,8,2048]{2,1,0:T(8,128)(2,1)S(1)} %pad_maximum_fusion.2), channel_id=1, source_target_pairs={{0,4},{1,5},{2,6},{3,7},{4,0},{5,1},{6,2},{7,3},{8,12},{9,13},{10,... | collective-permute-start | bytes 196616 | tf_op jit(solution)/shard_map/ppermute | solution.py:360
  12.3 1.0 %collective-permute-start.5 = (bf16[2,65,512]{2,1,0:T(8,128)(2,1)S(1)}, bf16[2,65,512]{2,1,0:T(8,128)(2,1)S(1)}, u32[]{:S(2)}, u32[]{:S(2)}) collective-permute-start(bf16[2,65,512]{2,1,0:T(8,128)(2,1)S(1)} %pad_maximum_fusion), channel_id=1, source_target_pairs={{0,2},{1,3},{2,0},{3,1},{4,6},{5,7},{6,4},{7,5},{8,10},{9,11},{10,... | collective-permute-start | bytes 399368 | tf_op jit(solution)/shard_map/ppermute | solution.py:360
  13.3 3.5 %collective-permute-start.6 = (bf16[2,65,512]{2,1,0:T(8,128)(2,1)S(1)}, bf16[2,65,512]{2,1,0:T(8,128)(2,1)S(1)}, u32[]{:S(2)}, u32[]{:S(2)}) collective-permute-start(bf16[2,65,512]{2,1,0:T(8,128)(2,1)S(1)} %pad_maximum_fusion), channel_id=1, source_target_pairs={{0,4},{1,5},{2,6},{3,7},{4,0},{5,1},{6,2},{7,3},{8,12},{9,13},{10,... | collective-permute-start | bytes 399368 | tf_op jit(solution)/shard_map/ppermute | solution.py:360
  16.9 2.2 %collective-permute-done.3 = bf16[2,8,2048]{2,1,0:T(8,128)(2,1)S(1)} collective-permute-done((bf16[2,8,2048]{2,1,0:T(8,128)(2,1)S(1)}, bf16[2,8,2048]{2,1,0:T(8,128)(2,1)S(1)}, u32[]{:S(2)}, u32[]{:S(2)}) %collective-permute-start.3) | collective-permute-done | bytes 65568 | tf_op jit(solution)/shard_map/ppermute | solution.py:360
  19.2 0.7 copy-done
  19.9 9.5 %cross_tile.1 = (f32[1,2048]{1,0:T(1,128)}, f32[1,2048]{1,0:T(1,128)}) custom-call(bf16[64,2048]{1,0:T(8,128)(2,1)} %copy-done.13, f32[1,2048]{1,0:T(1,128)} %bitcast.90, bf16[64,2048]{1,0:T(8,128)(2,1)} %bitcast.65, f32[1,2048]{1,0:T(1,128)} %bitcast.94), custom_call_target="tpu_custom_call" | custom-call | flops 2147483648 | bytes 1048576 | tf_op jit(solution)/shard_map/cross_tile/pallas_call | solution.py:161
  29.4 0.8 copy-done.10
  30.2 7.6 %self_tile.2 = f32[8,1,6144]{2,1,0:T(1,128)} custom-call(s32[1]{0:T(128)} %bitcast.18.flip, bf16[8,65,512]{2,1,0:T(8,128)(2,1)} %copy-done.10, bf16[64,2048]{1,0:T(8,128)(2,1)} %bitcast.72, f32[1,2048]{1,0:T(1,128)} %bitcast.91, f32[1,2048]{1,0:T(1,128)} %get-tuple-element.10.more_ref), custom_call_target="tpu_custom_call" | custom-call | flops 2181038080 | bytes 266240 | tf_op jit(solution)/shard_map/self_tile/pallas_call | solution.py:271
  37.8 5.0 %all-to-all-start = ((f32[8,1,6144]{2,1,0:T(1,128)}), f32[8,1,6144]{2,1,0:T(1,128)S(1)}, u32[]{:S(2)}, u32[]{:S(2)}) async-start(f32[8,1,6144]{2,1,0:T(1,128)} %self_tile.2), calls=%async_computation | async-start | bytes 393216 | tf_op jit(solution)/shard_map/all_to_all | solution.py:366
  42.9 1.6 %collective-permute-start.9 = (bf16[65,256]{1,0:T(8,128)(2,1)S(1)}, bf16[65,256]{1,0:T(8,128)(2,1)S(1)}, u32[]{:S(2)}, u32[]{:S(2)}) collective-permute-start(bf16[65,256]{1,0:T(8,128)(2,1)S(1)} %fusion.1), channel_id=1, source_target_pairs={{0,16},{8,24},{16,0},{24,8},{1,17},{9,25},{17,1},{25,9},{2,18},{10... | collective-permute-start | bytes 99848 | tf_op jit(solution)/shard_map/ppermute | solution.py:348
  44.8 1.8 %collective-permute-done.10 = bf16[65,256]{1,0:T(8,128)(2,1)S(1)} collective-permute-done((bf16[65,256]{1,0:T(8,128)(2,1)S(1)}, bf16[65,256]{1,0:T(8,128)(2,1)S(1)}, u32[]{:S(2)}, u32[]{:S(2)}) %collective-permute-start.10) | collective-permute-done | bytes 33312 | tf_op jit(solution)/shard_map/ppermute | solution.py:348
  47.1 0.7 pad_maximum_fusion.1.u_ref
  47.8 3.1 %self_tile.3.refs_0_ = f32[1,1,3072]{2,1,0:T(1,128)} custom-call(s32[1]{0:T(128)} %bitcast.21.flip, bf16[4,65,256]{2,1,0:T(8,128)(2,1)} %pad_maximum_fusion.1.u_ref, bf16[64,2048]{1,0:T(8,128)(2,1)} %bitcast.66, f32[1,2048]{1,0:T(1,128)} %bitcast.95, f32[1,2048]{1,0:T(1,128)} %get-tuple-element.11.more_ref), custom_call_target="tpu_custom_call" | custom-call | flops 545259520 | bytes 66560 | tf_op jit(solution)/shard_map/self_tile/pallas_call | solution.py:271
  51.4 1.0 %collective-permute-start.12 = (f32[1,1,3072]{2,1,0:T(1,128)}, f32[1,1,3072]{2,1,0:T(1,128)S(1)}, u32[]{:S(2)}, u32[]{:S(2)}) collective-permute-start(f32[1,1,3072]{2,1,0:T(1,128)} %self_tile.3.refs_0_), channel_id=1, source_target_pairs={{0,16},{8,24},{16,0},{24,8},{1,17},{9,25},{17,1},{25,9},{2,18},{10... | collective-permute-start | bytes 36872 | tf_op jit(solution)/shard_map/ppermute | solution.py:348
  52.7 2.5 %collective-permute-done.12.refs_2_ = f32[1,1,3072]{2,1,0:T(1,128)S(1)} collective-permute-done((f32[1,1,3072]{2,1,0:T(1,128)}, f32[1,1,3072]{2,1,0:T(1,128)S(1)}, u32[]{:S(2)}, u32[]{:S(2)}) %collective-permute-start.12) | collective-permute-done | bytes 12320 | tf_op jit(solution)/shard_map/ppermute | solution.py:348
  56.2 3.0 %again_tile.2 = f32[1,1,2304]{2,1,0:T(1,128)} custom-call(s32[1]{0:T(128)} %bitcast.21.flip, bf16[4,65,256]{2,1,0:T(8,128)(2,1)} %pad_maximum_fusion.1.u_ref, bf16[64,2048]{1,0:T(8,128)(2,1)} %bitcast.67, f32[1,128]{1,0:T(1,128)} %broadcast_in_dim.22.more_ref, f32[1,1,3072]{2,1,0:T(1,128)} %self_tile.3.refs_0_, f32[1,1,3072]{2,1,0:T(1,128)} %copy-done.14, ...), custom_call_target="tpu_custom_call" | custom-call | flops 545259520 | bytes 66560 | tf_op jit(solution)/shard_map/again_tile/pallas_call | solution.py:326
  59.2 0.7 copy-done.3
  59.9 9.7 %cross_again.1 = (f32[1,2048]{1,0:T(1,128)}, f32[1,2048]{1,0:T(1,128)}, f32[1,2048]{1,0:T(1,128)}, f32[8,1,4352]{2,1,0:T(1,128)}) custom-call(bf16[64,2048]{1,0:T(8,128)(2,1)} %copy-done.13, f32[1,2048]{1,0:T(1,128)} %bitcast.92, bf16[64,2048]{1,0:T(8,128)(2,1)} %bitcast.68, f32[1,2048]{1,0:T(1,128)} %bitcast.96, f32[8,1,6144]{2,1,0:T(1,128)} %copy-done.3, ...), custom_call_target="tpu_custom_call" | custom-call | flops 2147483648 | bytes 1048576 | tf_op jit(solution)/shard_map/cross_again/pallas_call | solution.py:206
  69.7 7.3 %again_tile.3 = f32[1,1,4608]{2,1,0:T(1,128)} custom-call(s32[1]{0:T(128)} %bitcast.18.flip, bf16[8,65,512]{2,1,0:T(8,128)(2,1)} %copy-done.10, bf16[64,2048]{1,0:T(8,128)(2,1)} %bitcast.73, f32[1,2048]{1,0:T(1,128)} %get-tuple-element.15.more_ref, f32[8,1,6144]{2,1,0:T(1,128)} %copy-done.3), custom_call_target="tpu_custom_call" | custom-call | flops 2181038080 | bytes 266240 | tf_op jit(solution)/shard_map/again_tile/pallas_call | solution.py:326
  77.2 0.9 collective-permute-start.15
  78.1 0.7 collective-permute-start.16
  78.8 6.1 %all-to-all-start.1 = ((f32[8,1,4352]{2,1,0:T(1,128)}), f32[8,1,4352]{2,1,0:T(1,128)S(1)}, u32[]{:S(2)}, u32[]{:S(2)}) async-start(f32[8,1,4352]{2,1,0:T(1,128)} %get-tuple-element.13), calls=%async_computation.1 | async-start | bytes 278528 | tf_op jit(solution)/shard_map/all_to_all | solution.py:366
  85.7 0.7 multiply_subtract_fusion
  86.4 6.3 %all-to-all-done.1 = f32[8,1,4352]{2,1,0:T(1,128)S(1)} async-done(((f32[8,1,4352]{2,1,0:T(1,128)}), f32[8,1,4352]{2,1,0:T(1,128)S(1)}, u32[]{:S(2)}, u32[]{:S(2)}) %all-to-all-start.1) | async-done | bytes 139296 | tf_op jit(solution)/shard_map/all_to_all | solution.py:366
  92.8 0.7 copy-done.12
  93.5 0.7 multiply_subtract_fusion.1
  (83 shorter events, 4.8 us)
Async XLA Ops:
  0.6 6.9 %collective-permute-start = (bf16[8,2048]{1,0:T(8,128)(2,1)}, bf16[8,2048]{1,0:T(8,128)(2,1)S(1)}, u32[]{:S(2)}, u32[]{:S(2)}) collective-permute-start(bf16[8,2048]{1,0:T(8,128)(2,1)} %bitcast.84), channel_id=1, source_target_pairs={{0,1},{1,0},{2,3},{3,2},{4,5},{5,4},{6,7},{7,6},{8,9},{9,8},{10,11... | collective-permute-start | bytes 98312 | tf_op jit(solution)/shard_map/ppermute | solution.py:354
  4.4 1.7 %copy-start.2 = (bf16[2048,64]{0,1:T(8,128)(2,1)S(1)}, bf16[2048,64]{0,1:T(8,128)(2,1)}, u32[]{:S(2)}) copy-start(bf16[2048,64]{0,1:T(8,128)(2,1)} %param.5) | copy-start | bytes 786436
  5.3 0.8 copy-start.4
  5.3 7.0 %collective-permute-start.4 = (bf16[65,512]{1,0:T(8,128)(2,1)S(1)}, bf16[65,512]{1,0:T(8,128)(2,1)S(1)}, u32[]{:S(2)}, u32[]{:S(2)}) collective-permute-start(bf16[65,512]{1,0:T(8,128)(2,1)S(1)} %get-tuple-element.17), channel_id=1, source_target_pairs={{0,1},{1,0},{2,3},{3,2},{4,5},{5,4},{6,7},{7,6},{8,9},{9,8},{10,11... | collective-permute-start | bytes 199688 | tf_op jit(solution)/shard_map/ppermute | solution.py:354
  6.9 5.4 %copy-start.13 = (bf16[64,2048]{1,0:T(8,128)(2,1)}, bf16[64,2048]{1,0:T(8,128)(2,1)S(1)}, u32[]{:S(2)}) copy-start(bf16[64,2048]{1,0:T(8,128)(2,1)S(1)} %constant_dynamic-update-slice_fusion.t_ref) | copy-start | bytes 786436
  7.6 9.2 %collective-permute-start.1 = (bf16[2,8,2048]{2,1,0:T(8,128)(2,1)S(1)}, bf16[2,8,2048]{2,1,0:T(8,128)(2,1)S(1)}, u32[]{:S(2)}, u32[]{:S(2)}) collective-permute-start(bf16[2,8,2048]{2,1,0:T(8,128)(2,1)S(1)} %pad_maximum_fusion.2), channel_id=1, source_target_pairs={{0,2},{1,3},{2,0},{3,1},{4,6},{5,7},{6,4},{7,5},{8,10},{9,11},{10,... | collective-permute-start | bytes 196616 | tf_op jit(solution)/shard_map/ppermute | solution.py:360
  9.7 7.2 %collective-permute-start.2 = (bf16[2,8,2048]{2,1,0:T(8,128)(2,1)S(1)}, bf16[2,8,2048]{2,1,0:T(8,128)(2,1)S(1)}, u32[]{:S(2)}, u32[]{:S(2)}) collective-permute-start(bf16[2,8,2048]{2,1,0:T(8,128)(2,1)S(1)} %pad_maximum_fusion.2), channel_id=1, source_target_pairs={{0,4},{1,5},{2,6},{3,7},{4,0},{5,1},{6,2},{7,3},{8,12},{9,13},{10,... | collective-permute-start | bytes 196616 | tf_op jit(solution)/shard_map/ppermute | solution.py:360
  12.3 6.9 %collective-permute-start.3 = (bf16[2,8,2048]{2,1,0:T(8,128)(2,1)S(1)}, bf16[2,8,2048]{2,1,0:T(8,128)(2,1)S(1)}, u32[]{:S(2)}, u32[]{:S(2)}) collective-permute-start(bf16[2,8,2048]{2,1,0:T(8,128)(2,1)S(1)} %pad_maximum_fusion.2), channel_id=1, source_target_pairs={{0,6},{1,7},{2,4},{3,5},{4,2},{5,3},{6,0},{7,1},{8,14},{9,15},{10,... | collective-permute-start | bytes 196616 | tf_op jit(solution)/shard_map/ppermute | solution.py:360
  12.3 17.0 %collective-permute-start.5 = (bf16[2,65,512]{2,1,0:T(8,128)(2,1)S(1)}, bf16[2,65,512]{2,1,0:T(8,128)(2,1)S(1)}, u32[]{:S(2)}, u32[]{:S(2)}) collective-permute-start(bf16[2,65,512]{2,1,0:T(8,128)(2,1)S(1)} %pad_maximum_fusion), channel_id=1, source_target_pairs={{0,2},{1,3},{2,0},{3,1},{4,6},{5,7},{6,4},{7,5},{8,10},{9,11},{10,... | collective-permute-start | bytes 399368 | tf_op jit(solution)/shard_map/ppermute | solution.py:360
  13.3 16.1 %collective-permute-start.6 = (bf16[2,65,512]{2,1,0:T(8,128)(2,1)S(1)}, bf16[2,65,512]{2,1,0:T(8,128)(2,1)S(1)}, u32[]{:S(2)}, u32[]{:S(2)}) collective-permute-start(bf16[2,65,512]{2,1,0:T(8,128)(2,1)S(1)} %pad_maximum_fusion), channel_id=1, source_target_pairs={{0,4},{1,5},{2,6},{3,7},{4,0},{5,1},{6,2},{7,3},{8,12},{9,13},{10,... | collective-permute-start | bytes 399368 | tf_op jit(solution)/shard_map/ppermute | solution.py:360
  16.8 12.6 %collective-permute-start.7 = (bf16[2,65,512]{2,1,0:T(8,128)(2,1)S(1)}, bf16[2,65,512]{2,1,0:T(8,128)(2,1)S(1)}, u32[]{:S(2)}, u32[]{:S(2)}) collective-permute-start(bf16[2,65,512]{2,1,0:T(8,128)(2,1)S(1)} %pad_maximum_fusion), channel_id=1, source_target_pairs={{0,6},{1,7},{2,4},{3,5},{4,2},{5,3},{6,0},{7,1},{8,14},{9,15},{10,... | collective-permute-start | bytes 399368 | tf_op jit(solution)/shard_map/ppermute | solution.py:360
  19.2 0.7 copy-start
  29.4 0.8 copy-start.10
  37.8 5.0 %copy-start.1 = (bf16[8,8,2048]{2,1,0:T(8,128)(2,1)S(1)}, bf16[8,8,2048]{2,1,0:T(8,128)(2,1)}, u32[]{:S(2)}) copy-start(bf16[8,8,2048]{2,1,0:T(8,128)(2,1)} %copy-done) | copy-start | bytes 786436
  37.8 21.4 %all-to-all-start = ((f32[8,1,6144]{2,1,0:T(1,128)}), f32[8,1,6144]{2,1,0:T(1,128)S(1)}, u32[]{:S(2)}, u32[]{:S(2)}) async-start(f32[8,1,6144]{2,1,0:T(1,128)} %self_tile.2), calls=%async_computation | async-start | bytes 393216 | tf_op jit(solution)/shard_map/all_to_all | solution.py:366
  42.8 3.8 %collective-permute-start.10 = (bf16[65,256]{1,0:T(8,128)(2,1)S(1)}, bf16[65,256]{1,0:T(8,128)(2,1)S(1)}, u32[]{:S(2)}, u32[]{:S(2)}) collective-permute-start(bf16[65,256]{1,0:T(8,128)(2,1)S(1)} %fusion.1), channel_id=1, source_target_pairs={{0,24},{8,16},{16,8},{24,0},{1,25},{9,17},{17,9},{25,1},{2,26},{10... | collective-permute-start | bytes 99848 | tf_op jit(solution)/shard_map/ppermute | solution.py:348
  42.9 4.2 %collective-permute-start.9 = (bf16[65,256]{1,0:T(8,128)(2,1)S(1)}, bf16[65,256]{1,0:T(8,128)(2,1)S(1)}, u32[]{:S(2)}, u32[]{:S(2)}) collective-permute-start(bf16[65,256]{1,0:T(8,128)(2,1)S(1)} %fusion.1), channel_id=1, source_target_pairs={{0,16},{8,24},{16,0},{24,8},{1,17},{9,25},{17,1},{25,9},{2,18},{10... | collective-permute-start | bytes 99848 | tf_op jit(solution)/shard_map/ppermute | solution.py:348
  44.5 2.6 %collective-permute-start.8 = (bf16[65,256]{1,0:T(8,128)(2,1)S(1)}, bf16[65,256]{1,0:T(8,128)(2,1)S(1)}, u32[]{:S(2)}, u32[]{:S(2)}) collective-permute-start(bf16[65,256]{1,0:T(8,128)(2,1)S(1)} %fusion.1), channel_id=1, source_target_pairs={{0,8},{8,0},{16,24},{24,16},{1,9},{9,1},{17,25},{25,17},{2,10},{10... | collective-permute-start | bytes 99848 | tf_op jit(solution)/shard_map/ppermute | solution.py:348
  50.8 1.9 %collective-permute-start.11 = (f32[1,1,3072]{2,1,0:T(1,128)}, f32[1,1,3072]{2,1,0:T(1,128)S(1)}, u32[]{:S(2)}, u32[]{:S(2)}) collective-permute-start(f32[1,1,3072]{2,1,0:T(1,128)} %self_tile.3.refs_0_), channel_id=1, source_target_pairs={{0,8},{8,0},{16,24},{24,16},{1,9},{9,1},{17,25},{25,17},{2,10},{10... | collective-permute-start | bytes 36872 | tf_op jit(solution)/shard_map/ppermute | solution.py:348
  51.4 3.9 %collective-permute-start.12 = (f32[1,1,3072]{2,1,0:T(1,128)}, f32[1,1,3072]{2,1,0:T(1,128)S(1)}, u32[]{:S(2)}, u32[]{:S(2)}) collective-permute-start(f32[1,1,3072]{2,1,0:T(1,128)} %self_tile.3.refs_0_), channel_id=1, source_target_pairs={{0,16},{8,24},{16,0},{24,8},{1,17},{9,25},{17,1},{25,9},{2,18},{10... | collective-permute-start | bytes 36872 | tf_op jit(solution)/shard_map/ppermute | solution.py:348
  52.3 3.3 %collective-permute-start.13 = (f32[1,1,3072]{2,1,0:T(1,128)}, f32[1,1,3072]{2,1,0:T(1,128)S(1)}, u32[]{:S(2)}, u32[]{:S(2)}) collective-permute-start(f32[1,1,3072]{2,1,0:T(1,128)} %self_tile.3.refs_0_), channel_id=1, source_target_pairs={{0,24},{8,16},{16,8},{24,0},{1,25},{9,17},{17,9},{25,1},{2,26},{10... | collective-permute-start | bytes 36872 | tf_op jit(solution)/shard_map/ppermute | solution.py:348
  52.7 3.4 %copy-start.14 = (f32[1,1,3072]{2,1,0:T(1,128)}, f32[1,1,3072]{2,1,0:T(1,128)S(1)}, u32[]{:S(2)}) copy-start(f32[1,1,3072]{2,1,0:T(1,128)S(1)} %collective-permute-done.11.refs_1_) | copy-start | bytes 36868
  55.3 0.9 copy-start.15
  77.0 8.0 %collective-permute-start.14 = (f32[1,1,4608]{2,1,0:T(1,128)}, f32[1,1,4608]{2,1,0:T(1,128)S(1)}, u32[]{:S(2)}, u32[]{:S(2)}) collective-permute-start(f32[1,1,4608]{2,1,0:T(1,128)} %again_tile.3), channel_id=1, source_target_pairs={{0,8},{8,0},{16,24},{24,16},{1,9},{9,1},{17,25},{25,17},{2,10},{10... | collective-permute-start | bytes 55304 | tf_op jit(solution)/shard_map/ppermute | solution.py:348
  77.2 7.8 %collective-permute-start.15 = (f32[1,1,4608]{2,1,0:T(1,128)}, f32[1,1,4608]{2,1,0:T(1,128)S(1)}, u32[]{:S(2)}, u32[]{:S(2)}) collective-permute-start(f32[1,1,4608]{2,1,0:T(1,128)} %again_tile.3), channel_id=1, source_target_pairs={{0,16},{8,24},{16,0},{24,8},{1,17},{9,25},{17,1},{25,9},{2,18},{10... | collective-permute-start | bytes 55304 | tf_op jit(solution)/shard_map/ppermute | solution.py:348
  78.1 7.0 %collective-permute-start.16 = (f32[1,1,4608]{2,1,0:T(1,128)}, f32[1,1,4608]{2,1,0:T(1,128)S(1)}, u32[]{:S(2)}, u32[]{:S(2)}) collective-permute-start(f32[1,1,4608]{2,1,0:T(1,128)} %again_tile.3), channel_id=1, source_target_pairs={{0,24},{8,16},{16,8},{24,0},{1,25},{9,17},{17,9},{25,1},{2,26},{10... | collective-permute-start | bytes 55304 | tf_op jit(solution)/shard_map/ppermute | solution.py:348
  78.8 6.1 %copy-start.7 = (f32[1,1,4608]{2,1,0:T(1,128)S(1)}, f32[1,1,4608]{2,1,0:T(1,128)}, u32[]{:S(2)}) copy-start(f32[1,1,4608]{2,1,0:T(1,128)} %again_tile.3) | copy-start | bytes 55300
  78.8 13.9 %all-to-all-start.1 = ((f32[8,1,4352]{2,1,0:T(1,128)}), f32[8,1,4352]{2,1,0:T(1,128)S(1)}, u32[]{:S(2)}, u32[]{:S(2)}) async-start(f32[8,1,4352]{2,1,0:T(1,128)} %get-tuple-element.13), calls=%async_computation.1 | async-start | bytes 278528 | tf_op jit(solution)/shard_map/all_to_all | solution.py:366
  85.0 0.7 copy-start.11
  85.0 0.7 copy-start.5
  92.7 0.7 copy-start.12
  92.8 0.7 copy-start.6
  (4 other events, 2.6 us)

commit v4 on v3

--- a/solution.py
+++ b/solution.py
@@ -15,6 +15,7 @@
 STRIP = 256
 EXTRA = 16
 GROUP = 1024
+LIMIT = 16 * 2**20
 
 
 def split3(x):
@@ -26,6 +27,7 @@
 
 def operand(desc, weight, scale, own):
     wide = desc.astype(jnp.float32)
+    desc = desc.astype(jnp.bfloat16)
     bias = weight - 2.0 * jnp.sum(wide * wide, axis=0, keepdims=True)
     hi, mid, lo = split3(bias)
     row = lax.broadcasted_iota(jnp.int32, (EXTRA, wide.shape[1]), 0) - own
@@ -124,14 +126,23 @@
     return pl.program_id(0) == pl.num_programs(0) - 1
 
 
-def cross_kernel(t_ref, w_ref, s_ref, z_ref, row_ref, col_ref, *scratch):
+def log_of(mass):
+    return jnp.log(mass.astype(jnp.float32))
+
+
+def swapped(turn, t_ref):
+    count = t_ref.shape[0]
+    return jnp.concatenate([t_ref[k ^ turn[0]].astype(jnp.float32) for k in range(count)], axis=0)
+
+
+def cross_kernel(turn, t_ref, w_ref, s_ref, z_ref, row_ref, col_ref, *scratch):
     rhs, _, ctop, csum = scratch
 
     @pl.when(pl.program_id(0) == 0)
     def _():
-        start_cross(s_ref[...], z_ref[...], rhs, ctop, csum)
-
-    row_ref[...] = cross_block(t_ref[...], w_ref[...], *scratch)
+        start_cross(s_ref[...], log_of(z_ref[...]), rhs, ctop, csum)
+
+    row_ref[...] = cross_block(swapped(turn, t_ref), log_of(w_ref[...]), *scratch)
 
     @pl.when(last_step())
     def _():
@@ -153,40 +164,49 @@
     )
 
 
-def cross_tile(t, w, s, z):
-    ch, nt = t.shape
+def cross_tile(turn, t, w, s, z):
+    count, ch, nt = t.shape
+    ch = ch * count
     n = s.shape[1]
     bt = math.gcd(GROUP, nt)
-    lanes = pl.BlockSpec((1, bt), lambda i: (0, i))
+    lanes = pl.BlockSpec((1, bt), lambda i, f: (0, i))
     return pl.pallas_call(
         cross_kernel,
-        grid=(nt // bt,),
-        in_specs=[pl.BlockSpec((ch, bt), lambda i: (0, i)), lanes, whole((ch, n)), whole((1, n))],
-        out_specs=[lanes, whole((1, n))],
+        grid_spec=pltpu.PrefetchScalarGridSpec(
+            num_scalar_prefetch=1,
+            grid=(nt // bt,),
+            in_specs=[
+                pl.BlockSpec((count, ch // count, bt), lambda i, f: (0, 0, i)),
+                lanes,
+                whole((ch, n)),
+                whole((1, n)),
+            ],
+            out_specs=[lanes, whole((1, n))],
+            scratch_shapes=cross_scratch(ch, bt, n),
+        ),
         out_shape=[jax.ShapeDtypeStruct((1, k), jnp.float32) for k in (nt, n)],
-        scratch_shapes=cross_scratch(ch, bt, n),
         cost_estimate=cross_cost(nt, n, ch),
+        compiler_params=pltpu.CompilerParams(vmem_limit_bytes=LIMIT),
         name="cross_tile",
-    )(t, w, s, z)
-
-
-def cross_again_kernel(count, t_ref, tl_ref, s_ref, sl_ref, cols_ref, more_ref, *refs):
-    parts = refs[:count]
-    row_ref, w_ref, z_ref, col_ref = refs[count : count + 4]
-    scratch = refs[count + 4 :]
+    )(turn, t, w, s, z)
+
+
+def cross_again_kernel(count, width, turn, t_ref, tm_ref, s_ref, sm_ref, more_ref, *refs):
+    parts, cols = refs[:count], refs[count : count + width]
+    row_ref, w_ref, z_ref, col_ref = refs[count + width : count + width + 4]
+    scratch = refs[count + width + 4 :]
     rhs, _, ctop, csum = scratch
     n = s_ref.shape[1]
 
     @pl.when(pl.program_id(0) == 0)
     def _():
-        cs = log_sum([cols_ref[k, :, 0:n] for k in range(cols_ref.shape[0])])
-        z = damped(sl_ref[...], cs)
+        z = damped(log_of(sm_ref[...]), log_sum([part[:, 0:n] for part in cols]))
         z_ref[...] = z
         start_cross(s_ref[...], z, rhs, ctop, csum)
 
-    w = damped(tl_ref[...], log_sum([part[0] for part in parts]))
+    w = damped(log_of(tm_ref[...]), log_sum([part[0] for part in parts]))
     w_ref[...] = w
-    row_ref[...] = cross_block(t_ref[...], w, *scratch)
+    row_ref[...] = cross_block(swapped(turn, t_ref), w, *scratch)
 
     @pl.when(last_step())
     def _():
@@ -196,31 +216,35 @@
             col_ref[k, :, n:] = more_ref[...]
 
 
-def cross_again(t, tlog, s, slog, by_col, by_row, more):
-    ch, nt = t.shape
+def cross_again(turn, t, tmass, s, smass, by_col, by_row, more):
+    count, ch, nt = t.shape
+    ch = ch * count
     n = s.shape[1]
     bt = math.gcd(GROUP, nt)
-    lanes = pl.BlockSpec((1, bt), lambda i: (0, i))
-    copies = by_col.shape[0]
-    shape = (copies, 1, n + more.shape[1])
+    lanes = pl.BlockSpec((1, bt), lambda i, f: (0, i))
+    shape = (count, 1, n + more.shape[1])
     return pl.pallas_call(
-        functools.partial(cross_again_kernel, len(by_row)),
-        grid=(nt // bt,),
-        in_specs=[
-            pl.BlockSpec((ch, bt), lambda i: (0, i)),
-            lanes,
-            whole((ch, n)),
-            whole((1, n)),
-            whole(by_col.shape),
-            whole(more.shape),
-        ]
-        + [pl.BlockSpec((1, 1, bt), lambda i: (0, 0, i))] * len(by_row),
-        out_specs=[lanes, lanes, whole((1, n)), whole(shape)],
+        functools.partial(cross_again_kernel, len(by_row), len(by_col)),
+        grid_spec=pltpu.PrefetchScalarGridSpec(
+            num_scalar_prefetch=1,
+            grid=(nt // bt,),
+            in_specs=[
+                pl.BlockSpec((count, ch // count, bt), lambda i, f: (0, 0, i)),
+                lanes,
+                whole((ch, n)),
+                whole((1, n)),
+                whole(more.shape),
+            ]
+            + [pl.BlockSpec((1, 1, bt), lambda i, f: (0, 0, i))] * len(by_row)
+            + [whole(part.shape) for part in by_col],
+            out_specs=[lanes, lanes, whole((1, n)), whole(shape)],
+            scratch_shapes=cross_scratch(ch, bt, n),
+        ),
         out_shape=[jax.ShapeDtypeStruct(k, jnp.float32) for k in ((1, nt), (1, nt), (1, n), shape)],
-        scratch_shapes=cross_scratch(ch, bt, n),
         cost_estimate=cross_cost(nt, n, ch),
+        compiler_params=pltpu.CompilerParams(vmem_limit_bytes=LIMIT),
         name="cross_again",
-    )(t, tlog, s, slog, by_col, more, *by_row)
+    )(turn, t, tmass, s, smass, more, *by_row, *by_col)
 
 
 def points(flip, u_ref, ch):
@@ -229,14 +253,14 @@
     return [jnp.concatenate([u_ref[k, a:b, :] for k in order], axis=1) for a, b in ((0, ch), (ch, ch + 1))]
 
 
-def self_kernel(flip, u_ref, s_ref, z_ref, more_ref, out_ref, rhs):
+def self_kernel(flip, u_ref, s_ref, z_ref, more_ref, out_ref, plan_ref, rhs):
     i = pl.program_id(0)
     ch, n = s_ref.shape
     extra = more_ref.shape[1]
 
     @pl.when(i == 0)
     def _():
-        rhs[...] = operand(s_ref[...], z_ref[...], 4.0, 0)
+        rhs[...] = operand(s_ref[...], log_of(z_ref[...]), 4.0, 0)
         for k in range(out_ref.shape[0]):
             out_ref[k, :, 0:extra] = more_ref[...]
 
@@ -244,8 +268,11 @@
     bt = desc.shape[1]
     lhs = operand(desc, jnp.zeros((1, bt), jnp.float32), 1.0, 3)
     racc = jnp.zeros((bt, 128), jnp.float32)
+    here = pl.ds(pl.multiple_of(i * bt, bt), bt)
     for k in range(0, n, STRIP):
-        racc = racc + fold_lanes(jnp.exp(scores(lhs, rhs[:, k : k + STRIP])), jnp.add)
+        plan = jnp.exp(scores(lhs, rhs[:, k : k + STRIP]))
+        racc = racc + fold_lanes(plan, jnp.add)
+        plan_ref[here, k : k + STRIP] = plan.astype(jnp.bfloat16)
     sums = rows_sum_lanes(racc)
     start = pl.multiple_of(extra + i * bt, 128)
     for k in range(out_ref.shape[0]):
@@ -274,78 +301,72 @@
             num_scalar_prefetch=1,
             grid=(blocks // group,),
             in_specs=[block, whole((ch, n)), whole((1, n)), whole(more.shape)],
-            out_specs=whole(shape),
+            out_specs=[whole(shape), pl.BlockSpec(memory_space=pltpu.VMEM)],
             scratch_shapes=[pltpu.VMEM((ch + EXTRA, n), jnp.bfloat16)],
         ),
-        out_shape=jax.ShapeDtypeStruct(shape, jnp.float32),
+        out_shape=[
+            jax.ShapeDtypeStruct(shape, jnp.float32),
+            jax.ShapeDtypeStruct((blocks * bt, n), jnp.bfloat16),
+        ],
+        compiler_params=pltpu.CompilerParams(vmem_limit_bytes=LIMIT),
         cost_estimate=self_cost(u, n),
         name="self_tile",
     )(flip, u, s, z, more)
 
 
-def again_kernel(skip, ahead, flip, u_ref, s_ref, more_ref, *refs):
-    parts, (out_ref, rhs, csum, sums) = refs[:-4], refs[-4:]
-    i = pl.program_id(0)
-    ch, n = s_ref.shape
+def again_kernel(skip, ahead, place, own, flip, u_ref, z_ref, plan_ref, more_ref, *refs):
+    parts, out_ref = refs[:-1], refs[-1]
+    rows, n = plan_ref.shape
     extra = more_ref.shape[1] if ahead else 0
-    own = out_ref.shape[2] - extra - n
-
-    @pl.when(i == 0)
-    def _():
-        rhs[...] = operand(s_ref[...], jnp.zeros((1, n), jnp.float32), 4.0, 0)
-        csum[...] = jnp.zeros(csum.shape, jnp.float32)
-        pieces = [part[k, :, skip:] for part in parts for k in range(part.shape[0])]
-        sums[...] = jnp.log(tree(pieces, jnp.add))
-        if ahead:
-            out_ref[0, :, 0:extra] = more_ref[...]
-
-    desc, mass = points(flip, u_ref, ch)
-    bt = desc.shape[1]
-    logs = sums[:, pl.ds(pl.multiple_of(i * bt, 128), bt)]
-    weight = jnp.log(mass.astype(jnp.float32)) - 0.5 * DAMPING * logs
-    lhs = operand(desc, weight, 1.0, 3)
-    for k in range(0, n, STRIP):
-        part = fold_rows(jnp.exp(scores(lhs, rhs[:, k : k + STRIP])), jnp.add)
-        csum[:, k : k + STRIP] = csum[:, k : k + STRIP] + part
-
-    @pl.when(last_step())
-    def _():
-        out_ref[0, :, extra : extra + n] = jnp.sum(csum[...], axis=0, keepdims=True)
-        mine = sums[:, pl.ds(pl.multiple_of(flip[0] * own, 128), own)]
-        out_ref[0, :, extra + n :] = (-0.5 * DAMPING * EPSILON) * mine
-
-
-def again_tile(u, s, flip, parts, skip, own, more=None):
-    blocks, _, bt = u.shape
-    ch, n = s.shape
-    group, block = grouped(u)
+    sums = jnp.log(tree([part[:, skip:] if len(part.shape) == 2 else part[0, :, skip:] for part in parts], jnp.add))
+    if ahead:
+        out_ref[0, :, 0:extra] = more_ref[...]
+    blocks, depth, _ = u_ref.shape
+    masses = [u_ref[k ^ flip[0], depth - 1 : depth, :] for k in range(blocks)]
+    mass = jnp.concatenate(masses, axis=1).astype(jnp.float32)
+    weight = mass * jnp.exp(-0.5 * DAMPING * sums)
+    hi, mid, lo = split3(weight)
+    row = lax.broadcasted_iota(jnp.int32, (EXTRA, rows), 0)
+    lhs = jnp.where(row == 0, hi, jnp.where(row == 1, mid, jnp.where(row == 2, lo, 0.0)))
+    lhs = lhs.astype(jnp.bfloat16)
+    for k in range(0, n, 512):
+        acc = jnp.dot(lhs, plan_ref[:, k : k + 512], preferred_element_type=jnp.float32)
+        total = jnp.sum(acc, axis=0, keepdims=True) / z_ref[:, k : k + 512].astype(jnp.float32)
+        out_ref[0, :, extra + k : extra + k + 512] = total
+    last = extra + n
+    if place:
+        out_ref[0, :, last:] = jnp.zeros((1, out_ref.shape[2] - last), jnp.float32)
+        last = pl.multiple_of(last + flip[1] * own, 128)
+    for k in range(rows // own):
+
+        @pl.when(flip[0] == k)
+        def _():
+            mine = (-0.5 * DAMPING * EPSILON) * sums[:, k * own : (k + 1) * own]
+            out_ref[0, :, pl.ds(last, own)] = mine
+
+
+def again_tile(u, z, plan, flip, parts, skip, own, more=None, place=False):
+    rows, n = plan.shape
     ahead = more is not None
     if not ahead:
         more = jnp.zeros((1, 128), jnp.float32)
-    shape = (1, 1, (more.shape[1] if ahead else 0) + n + own)
+    shape = (1, 1, (more.shape[1] if ahead else 0) + n + (n if place else own))
+    vmem = pl.BlockSpec(memory_space=pltpu.VMEM)
     return pl.pallas_call(
-        functools.partial(again_kernel, skip, ahead),
-        grid_spec=pltpu.PrefetchScalarGridSpec(
-            num_scalar_prefetch=1,
-            grid=(blocks // group,),
-            in_specs=[block, whole((ch, n)), whole(more.shape)] + [whole(part.shape) for part in parts],
-            out_specs=whole(shape),
-            scratch_shapes=[
-                pltpu.VMEM((ch + EXTRA, n), jnp.bfloat16),
-                pltpu.VMEM((8, n), jnp.float32),
-                pltpu.VMEM((1, blocks * bt), jnp.float32),
-            ],
-        ),
+        functools.partial(again_kernel, skip, ahead, place, own),
+        in_specs=[pl.BlockSpec(memory_space=pltpu.SMEM)] + [vmem] * (4 + len(parts)),
+        out_specs=vmem,
         out_shape=jax.ShapeDtypeStruct(shape, jnp.float32),
-        cost_estimate=self_cost(u, n),
+        compiler_params=pltpu.CompilerParams(vmem_limit_bytes=LIMIT),
+        cost_estimate=pl.CostEstimate(flops=32 * rows * n, bytes_accessed=2 * rows * n, transcendentals=0),
         name="again_tile",
-    )(flip, u, s, more, *parts)
-
-
-def collect(x, axis):
+    )(flip, u, z, plan, more, *parts)
+
+
+def collect(x, axis, step=1):
     count = lax.axis_size(axis)
     return [x] + [
-        lax.ppermute(x, axis, [(i, i ^ k) for i in range(count)]) for k in range(1, count)
+        lax.ppermute(x, axis, [(i, i ^ k) for i in range(count)]) for k in range(step, count, step)
     ]
 
 
@@ -380,10 +401,7 @@
     source_mass = source_mass[None]
     target_mass = target_mass[None]
     target_lanes = target_desc.T
-    blocks = target_lanes.reshape(cols, -1, nt)
-    target_swapped = jnp.concatenate(
-        [lax.dynamic_index_in_dim(blocks, col ^ k, 0, False) for k in range(cols)], axis=0
-    )
+    target_blocks = target_lanes.reshape(cols, -1, nt)
     piece = jnp.concatenate([target_lanes, target_mass], axis=0)
     piece = lax.dynamic_slice_in_dim(piece, row * pt, pt, 1)
     pair = near(source_desc.T, "col")
@@ -395,34 +413,38 @@
     source_set = jnp.stack(collect(piece, "row"))
     flip = row.astype(jnp.int32)[None]
     turn = col.astype(jnp.int32)[None]
-
-    smass = source_mass.astype(jnp.float32)
-    tmass = target_mass.astype(jnp.float32)
-    slog = jnp.log(smass)
-    tlog = jnp.log(tmass)
-
-    ct, cs = cross_tile(target_swapped, tlog, source_lanes, slog)
-    sums = self_tile(source_set, source_lanes, slog, flip, ct, 1)
-    by_row = collect(sums, "row")
-    sums = self_tile(target_set, target_lanes, tlog, turn, cs, cols)
-    by_col = swap(sums, "col")
-    more = again_tile(source_set, source_lanes, flip, by_row, nt, ps)
-    ct, w, z, sums = cross_again(target_swapped, tlog, source_lanes, slog, by_col, by_row, more[0])
+    spot = jnp.stack([col, row]).astype(jnp.int32)
+
+    ct, cs = cross_tile(turn, target_blocks, target_mass, source_lanes, source_mass)
+    sums, target_plan = self_tile(target_set, target_lanes, target_mass, turn, cs, 1)
+    sums = sums[0]
+    other = lax.ppermute(sums, "col", [(i, i ^ 1) for i in range(cols)])
+    logs = lax.broadcasted_iota(jnp.int32, sums.shape, 1) < ns
+    sums = jnp.where(logs, log_sum([sums, other]), sums + other)
+    row_sums, source_plan = self_tile(source_set, source_lanes, source_mass, flip, ct, 1)
+    by_row = collect(row_sums, "row")
+    by_col = collect(sums, "col", 2)
+    more = again_tile(source_set, source_mass, source_plan, flip, by_row, nt, ps)
+    ct, w, z, sums = cross_again(
+        turn, target_blocks, target_mass, source_lanes, source_mass, by_col, by_row, more[0]
+    )
     last_col = swap(sums, "col")
-    sums = again_tile(target_set, target_lanes, turn, [by_col], ns, pt, ct)
+    sums = again_tile(
+        target_set, target_mass, target_plan, spot, by_col, ns, pt, ct, True
+    )
     last_row = [part[0] for part in collect(sums, "row")]
 
+    slog = jnp.log(source_mass.astype(jnp.float32))
+    tlog = jnp.log(target_mass.astype(jnp.float32))
     cs = log_sum([part[:, :ns] for part in last_col])
     ss_again = tree([part[:, ns : 2 * ns] for part in last_col], jnp.add)
     ss = last_col[:, :, 2 * ns :].reshape(1, ns)
+    cross_source = 0.5 * EPSILON * (z - slog) - half * (cs - z)
+    self_source = 0.5 * ss - half * jnp.log(ss_again)
     ct = log_sum([part[:, :nt] for part in last_row])
     st_again = tree([part[:, nt : 2 * nt] for part in last_row], jnp.add)
-    st = jnp.zeros((1, nt), jnp.float32)
-    for k, part in enumerate(last_row):
-        st = lax.dynamic_update_slice(st, part[:, 2 * nt :], (0, (row ^ k) * pt))
-    cross_source = 0.5 * EPSILON * (z - slog) - half * (cs - z)
+    st = tree([part[:, 2 * nt :] for part in last_row], jnp.add)
     cross_target = 0.5 * EPSILON * (w - tlog) - half * (ct - w)
-    self_source = 0.5 * ss - half * jnp.log(ss_again)
     self_target = 0.5 * st - half * jnp.log(st_again)
     return (cross_source[0], cross_target[0], self_source[0], self_target[0])
 

time: 94.9 us -> 84.2 us (0.89)
  Pallas kernels: 40.1 us -> 27.5 us
  waiting for transfers between devices: 13.8 us -> 18.7 us
  local copies, waits for them, and re-layouts: 5.75 us -> 3.19 us
    pallas_call x4, Pallas kernels: 29.5 us -> 20.2 us  [the longest x1 8.52 us: cross_again(): pl.pallas_call(functools.partial(cross_again_kernel, len(by_row), len(by_...]
    all_to_all x2 -> x1, starting transfers between devices: 11.1 us -> 3.39 us  [swap(): return lax.all_to_all(x, axis, 0, 0)]
    ppermute x6, waiting for transfers between devices: 2.26 us -> 8.86 us  [far(): lax.ppermute(pair, axis, [(i, i ^ k) for i in range(count)])]
    ppermute x9 -> x12, starting transfers between devices: 5.7 us -> 10.9 us  [collect(): lax.ppermute(x, axis, [(i, i ^ k) for i in range(count)])]
    unnamed x48 -> x13, local copies, waits for them, and re-layouts: 5.12 us -> 1.77 us
    pallas_call x2, Pallas kernels: 10.7 us -> 7.33 us  [self_tile(): pl.pallas_call(self_kernel, grid_spec=pltpu.PrefetchScalarGridSpec(num_sc...]
    ppermute x9 -> x12, waiting for transfers between devices: 5.24 us -> 3.12 us  [collect(): lax.ppermute(x, axis, [(i, i ^ k) for i in range(count)])]
    ppermute x0 -> x1, starting transfers between devices: none -> 1.56 us  [body(): other = lax.ppermute(sums, 'col', [(i, i ^ 1) for i in range(cols)])]
  transfers between devices with their start and end apart: 19 -> 22, of which waited for: 6 -> 5; matrix products, arithmetic and copies ran while one was open for 5% -> 6% of each run, Pallas kernels for 16% -> 12%
where the time goes in v4:
time: 84.2 us; the launch traced here: 83.7 us
  starting transfers between devices  29.4 us (35%)
  Pallas kernels  27.5 us (33%)
  waiting for transfers between devices  18.7 us (22%)
  other arithmetic  3.96 us (5%)
  local copies, waits for them, and re-layouts  3.19 us (4%)
  between operations  0.88 us (1%)
    ppermute x12, starting transfers between devices, collect(): lax.ppermute(x, axis, [(i, i ^ k) for i in range(count)])  10.9 us
    ppermute x6, starting transfers between devices, far(): lax.ppermute(pair, axis, [(i, i ^ k) for i in range(count)])  10.5 us
    ppermute x6, waiting for transfers between devices, far(): lax.ppermute(pair, axis, [(i, i ^ k) for i in range(count)])  8.86 us
    pallas_call x1, Pallas kernels, cross_again(): pl.pallas_call(functools.partial(cross_again_kernel, len(by_row), len(by_...  8.52 us
    pallas_call x1, Pallas kernels, cross_tile(): pl.pallas_call(cross_kernel, grid_spec=pltpu.PrefetchScalarGridSpec(num_s...  7.86 us
    pallas_call x2, Pallas kernels, self_tile(): pl.pallas_call(self_kernel, grid_spec=pltpu.PrefetchScalarGridSpec(num_sc...  7.33 us
    all_to_all x1, waiting for transfers between devices, swap(): return lax.all_to_all(x, axis, 0, 0)  6.76 us
    pallas_call x2, Pallas kernels, again_tile(): pl.pallas_call(functools.partial(again_kernel, skip, ahead, place, own),...  3.77 us
  transfers between devices with their start and end apart: 22, of which 5 were waited for; matrix products, arithmetic and copies ran while one was open for 6% of the time, Pallas kernels for 12%

profile of v4, /device:TPU:0, one launch (start us, length us, event | category | flops | bytes accessed | tf_op | source)
XLA Modules:
  0.0 83.7 jit_solution(14727396395600881908)
XLA Ops:
  0.6 3.0 %collective-permute-start = (bf16[8,2048]{1,0:T(8,128)(2,1)}, bf16[8,2048]{1,0:T(8,128)(2,1)S(1)}, u32[]{:S(2)}, u32[]{:S(2)}) collective-permute-start(bf16[8,2048]{1,0:T(8,128)(2,1)} %bitcast.65), channel_id=1, source_target_pairs={{0,1},{1,0},{2,3},{3,2},{4,5},{5,4},{6,7},{7,6},{8,9},{9,8},{10,11... | collective-permute-start | bytes 98312 | tf_op jit(solution)/shard_map/ppermute | solution.py:375
  4.4 0.8 %constant_dynamic-update-slice_fusion.9 = (bf16[8,65,512]{2,1,0:T(8,128)(2,1)S(1)}, bf16[65,512]{1,0:T(8,128)(2,1)S(1)}) fusion(s32[]{:T(128)S(6)} %select_n.11, bf16[1,2048]{1,0:T(2,128)(2,1)S(1)} %broadcast_in_dim.16.w_ref.z_ref.tm_ref, bf16[64,2048]{1,0:T(8,128)(2,1)} %bitcast.56), kind=kLoop, calls=%fused_computation.21 | loop fusion | flops 133119 | bytes 413700
  5.3 0.8 constant_dynamic-update-slice_fusion.4
  6.7 0.7 broadcast_in_dim.17.z_ref.sm_ref
  7.5 0.8 pad_maximum_fusion.2
  8.2 2.1 %collective-permute-start.1 = (bf16[2,8,2048]{2,1,0:T(8,128)(2,1)S(1)}, bf16[2,8,2048]{2,1,0:T(8,128)(2,1)S(1)}, u32[]{:S(2)}, u32[]{:S(2)}) collective-permute-start(bf16[2,8,2048]{2,1,0:T(8,128)(2,1)S(1)} %pad_maximum_fusion.2), channel_id=1, source_target_pairs={{0,2},{1,3},{2,0},{3,1},{4,6},{5,7},{6,4},{7,5},{8,10},{9,11},{10,... | collective-permute-start | bytes 196616 | tf_op jit(solution)/shard_map/ppermute | solution.py:381
  10.3 2.6 %collective-permute-start.2 = (bf16[2,8,2048]{2,1,0:T(8,128)(2,1)S(1)}, bf16[2,8,2048]{2,1,0:T(8,128)(2,1)S(1)}, u32[]{:S(2)}, u32[]{:S(2)}) collective-permute-start(bf16[2,8,2048]{2,1,0:T(8,128)(2,1)S(1)} %pad_maximum_fusion.2), channel_id=1, source_target_pairs={{0,4},{1,5},{2,6},{3,7},{4,0},{5,1},{6,2},{7,3},{8,12},{9,13},{10,... | collective-permute-start | bytes 196616 | tf_op jit(solution)/shard_map/ppermute | solution.py:381
  12.9 1.0 %collective-permute-start.11 = (bf16[2,65,512]{2,1,0:T(8,128)(2,1)S(1)}, bf16[2,65,512]{2,1,0:T(8,128)(2,1)S(1)}, u32[]{:S(2)}, u32[]{:S(2)}) collective-permute-start(bf16[2,65,512]{2,1,0:T(8,128)(2,1)S(1)} %pad_maximum_fusion.1), channel_id=1, source_target_pairs={{0,2},{1,3},{2,0},{3,1},{4,6},{5,7},{6,4},{7,5},{8,10},{9,11},{10,... | collective-permute-start | bytes 399368 | tf_op jit(solution)/shard_map/ppermute | solution.py:381
  13.9 3.5 %collective-permute-start.12 = (bf16[2,65,512]{2,1,0:T(8,128)(2,1)S(1)}, bf16[2,65,512]{2,1,0:T(8,128)(2,1)S(1)}, u32[]{:S(2)}, u32[]{:S(2)}) collective-permute-start(bf16[2,65,512]{2,1,0:T(8,128)(2,1)S(1)} %pad_maximum_fusion.1), channel_id=1, source_target_pairs={{0,4},{1,5},{2,6},{3,7},{4,0},{5,1},{6,2},{7,3},{8,12},{9,13},{10,... | collective-permute-start | bytes 399368 | tf_op jit(solution)/shard_map/ppermute | solution.py:381
  17.4 2.3 %collective-permute-done.3 = bf16[2,8,2048]{2,1,0:T(8,128)(2,1)S(1)} collective-permute-done((bf16[2,8,2048]{2,1,0:T(8,128)(2,1)S(1)}, bf16[2,8,2048]{2,1,0:T(8,128)(2,1)S(1)}, u32[]{:S(2)}, u32[]{:S(2)}) %collective-permute-start.3) | collective-permute-done | bytes 65568 | tf_op jit(solution)/shard_map/ppermute | solution.py:381
  19.9 1.6 %collective-permute-start.5 = (bf16[65,256]{1,0:T(8,128)(2,1)S(1)}, bf16[65,256]{1,0:T(8,128)(2,1)S(1)}, u32[]{:S(2)}, u32[]{:S(2)}) collective-permute-start(bf16[65,256]{1,0:T(8,128)(2,1)S(1)} %fusion.1), channel_id=1, source_target_pairs={{0,16},{8,24},{16,0},{24,8},{1,17},{9,25},{17,1},{25,9},{2,18},{10... | collective-permute-start | bytes 99848 | tf_op jit(solution)/shard_map/ppermute | solution.py:369
  21.7 0.9 %copy-done = bf16[2048,64]{0,1:T(8,128)(2,1)S(1)} copy-done((bf16[2048,64]{0,1:T(8,128)(2,1)S(1)}, bf16[2048,64]{0,1:T(8,128)(2,1)}, u32[]{:S(2)}) %copy-start) | copy-done | bytes 262168
  22.7 7.9 %cross_tile.1 = (f32[1,2048]{1,0:T(1,128)S(1)}, f32[1,2048]{1,0:T(1,128)S(1)}) custom-call(s32[1]{0:T(128)} %bitcast.turn.flip, bf16[8,8,2048]{2,1,0:T(8,128)(2,1)S(1)} %bitcast.57, bf16[1,2048]{1,0:T(2,128)(2,1)S(1)} %broadcast_in_dim.16.w_ref.z_ref.tm_ref, bf16[64,2048]{1,0:T(8,128)(2,1)S(1)} %bitcast.52, bf16[1,2048]{1,0:T(2,128)(2,1)S(1)} %broadcast_in_dim.17.z_ref.sm_ref), custom_call_target="tpu_custom_call" | custom-call | flops 2147483648 | bytes 1048576 | tf_op jit(solution)/shard_map/cross_tile/pallas_call | solution.py:173
  30.6 1.4 %collective-permute-start.13 = (bf16[2,65,512]{2,1,0:T(8,128)(2,1)S(1)}, bf16[2,65,512]{2,1,0:T(8,128)(2,1)S(1)}, u32[]{:S(2)}, u32[]{:S(2)}) collective-permute-start(bf16[2,65,512]{2,1,0:T(8,128)(2,1)S(1)} %pad_maximum_fusion.1), channel_id=1, source_target_pairs={{0,6},{1,7},{2,4},{3,5},{4,2},{5,3},{6,0},{7,1},{8,14},{9,15},{10,... | collective-permute-start | bytes 399368 | tf_op jit(solution)/shard_map/ppermute | solution.py:381
  32.0 6.5 %collective-permute-done.13 = bf16[2,65,512]{2,1,0:T(8,128)(2,1)S(1)} collective-permute-done((bf16[2,65,512]{2,1,0:T(8,128)(2,1)S(1)}, bf16[2,65,512]{2,1,0:T(8,128)(2,1)S(1)}, u32[]{:S(2)}, u32[]{:S(2)}) %collective-permute-start.13) | collective-permute-done | bytes 133152 | tf_op jit(solution)/shard_map/ppermute | solution.py:381
  38.6 5.9 %self_tile.3 = (f32[1,1,6144]{2,1,0:T(1,128)S(1)}, bf16[4096,2048]{1,0:T(8,128)(2,1)S(1)}) custom-call(s32[1]{0:T(128)} %bitcast.turn.flip, bf16[8,65,512]{2,1,0:T(8,128)(2,1)S(1)} %constant_dynamic-update-slice_fusion.5.u_ref, bf16[64,2048]{1,0:T(8,128)(2,1)S(1)} %bitcast.58, bf16[1,2048]{1,0:T(2,128)(2,1)S(1)} %broadcast_in_dim.16.w_ref.z_ref.tm_ref, ...), custom_call_target="tpu_custom_call" | custom-call | flops 2181038080 | bytes 266240 | tf_op jit(solution)/shard_map/self_tile/pallas_call | solution.py:298
  44.4 1.6 %collective-permute-start.14 = (f32[1,6144]{1,0:T(1,128)S(1)}, f32[1,6144]{1,0:T(1,128)S(1)}, u32[]{:S(2)}, u32[]{:S(2)}) collective-permute-start(f32[1,6144]{1,0:T(1,128)S(1)} %bitcast.61), channel_id=1, source_target_pairs={{0,1},{1,0},{2,3},{3,2},{4,5},{5,4},{6,7},{7,6},{8,9},{9,8},{10,11... | collective-permute-start | bytes 73736 | tf_op jit(solution)/shard_map/ppermute | solution.py:421
  46.0 1.5 %self_tile.2 = (f32[1,1,3072]{2,1,0:T(1,128)S(1)}, bf16[1024,2048]{1,0:T(8,128)(2,1)S(1)}) custom-call(s32[1]{0:T(128)} %bitcast.8.flip, bf16[4,65,256]{2,1,0:T(8,128)(2,1)S(1)} %pad_maximum_fusion.u_ref, bf16[64,2048]{1,0:T(8,128)(2,1)S(1)} %bitcast.54, bf16[1,2048]{1,0:T(2,128)(2,1)S(1)} %broadcast_in_dim.17.z_ref.sm_ref, ...), custom_call_target="tpu_custom_call" | custom-call | flops 545259520 | bytes 66560 | tf_op jit(solution)/shard_map/self_tile/pallas_call | solution.py:298
  47.5 1.3 %collective-permute-start.8 = (f32[1,1,3072]{2,1,0:T(1,128)S(1)}, f32[1,1,3072]{2,1,0:T(1,128)S(1)}, u32[]{:S(2)}, u32[]{:S(2)}) collective-permute-start(f32[1,1,3072]{2,1,0:T(1,128)S(1)} %get-tuple-element.16.refs_0_), channel_id=1, source_target_pairs={{0,16},{8,24},{16,0},{24,8},{1,17},{9,25},{17,1},{25,9},{2,18},{10... | collective-permute-start | bytes 36872 | tf_op jit(solution)/shard_map/ppermute | solution.py:369
  49.4 2.7 %collective-permute-start.15 = (f32[1,6144]{1,0:T(1,128)S(1)}, f32[1,6144]{1,0:T(1,128)S(1)}, u32[]{:S(2)}, u32[]{:S(2)}) collective-permute-start(f32[1,6144]{1,0:T(1,128)S(1)} %compare_select_fusion.refs_4_.refs_0_), channel_id=1, source_target_pairs={{0,2},{1,3},{2,0},{3,1},{4,6},{5,7},{6,4},{7,5},{8,10},{9,11},{10,... | collective-permute-start | bytes 73736 | tf_op jit(solution)/shard_map/ppermute | solution.py:369
  52.1 0.9 %collective-permute-start.16 = (f32[1,6144]{1,0:T(1,128)S(1)}, f32[1,6144]{1,0:T(1,128)S(1)}, u32[]{:S(2)}, u32[]{:S(2)}) collective-permute-start(f32[1,6144]{1,0:T(1,128)S(1)} %compare_select_fusion.refs_4_.refs_0_), channel_id=1, source_target_pairs={{0,4},{1,5},{2,6},{3,7},{4,0},{5,1},{6,2},{7,3},{8,12},{9,13},{10,... | collective-permute-start | bytes 73736 | tf_op jit(solution)/shard_map/ppermute | solution.py:369
  53.0 1.5 %collective-permute-start.17 = (f32[1,6144]{1,0:T(1,128)S(1)}, f32[1,6144]{1,0:T(1,128)S(1)}, u32[]{:S(2)}, u32[]{:S(2)}) collective-permute-start(f32[1,6144]{1,0:T(1,128)S(1)} %compare_select_fusion.refs_4_.refs_0_), channel_id=1, source_target_pairs={{0,6},{1,7},{2,4},{3,5},{4,2},{5,3},{6,0},{7,1},{8,14},{9,15},{10,... | collective-permute-start | bytes 73736 | tf_op jit(solution)/shard_map/ppermute | solution.py:369
  54.6 0.9 %again_tile.2 = f32[1,1,2304]{2,1,0:T(1,128)S(1)} custom-call(s32[1]{0:T(128)} %bitcast.8.flip, bf16[4,65,256]{2,1,0:T(8,128)(2,1)S(1)} %pad_maximum_fusion.u_ref, bf16[1,2048]{1,0:T(2,128)(2,1)S(1)} %broadcast_in_dim.17.z_ref.sm_ref, bf16[1024,2048]{1,0:T(8,128)(2,1)S(1)} %get-tuple-element.15.plan_ref, f32[1,128]{1,0:T(1,128)S(1)} %broadcast_in_dim.19.more_ref, ...), custom_call_target="tpu_custom_call" | custom-call | flops 67108864 | bytes 4194304 | tf_op jit(solution)/shard_map/again_tile/pallas_call | solution.py:355
  55.6 1.3 %collective-permute-done.16.refs_6_.refs_2_ = f32[1,6144]{1,0:T(1,128)S(1)} collective-permute-done((f32[1,6144]{1,0:T(1,128)S(1)}, f32[1,6144]{1,0:T(1,128)S(1)}, u32[]{:S(2)}, u32[]{:S(2)}) %collective-permute-start.16) | collective-permute-done | bytes 24608 | tf_op jit(solution)/shard_map/ppermute | solution.py:369
  56.9 1.8 %collective-permute-done.17.refs_7_.refs_3_ = f32[1,6144]{1,0:T(1,128)S(1)} collective-permute-done((f32[1,6144]{1,0:T(1,128)S(1)}, f32[1,6144]{1,0:T(1,128)S(1)}, u32[]{:S(2)}, u32[]{:S(2)}) %collective-permute-start.17) | collective-permute-done | bytes 24608 | tf_op jit(solution)/shard_map/ppermute | solution.py:369
  58.7 8.5 %cross_again.1 = (f32[1,2048]{1,0:T(1,128)S(1)}, f32[1,2048]{1,0:T(1,128)S(1)}, f32[1,2048]{1,0:T(1,128)S(1)}, f32[8,1,4352]{2,1,0:T(1,128)}) custom-call(s32[1]{0:T(128)} %bitcast.turn.flip, bf16[8,8,2048]{2,1,0:T(8,128)(2,1)S(1)} %bitcast.59, bf16[1,2048]{1,0:T(2,128)(2,1)S(1)} %broadcast_in_dim.16.w_ref.z_ref.tm_ref, bf16[64,2048]{1,0:T(8,128)(2,1)S(1)} %bitcast.55, ...), custom_call_target="tpu_custom_call" | custom-call | flops 2147483648 | bytes 1048576 | tf_op jit(solution)/shard_map/cross_again/pallas_call | solution.py:226
  67.2 2.9 %again_tile.3 = f32[1,1,6144]{2,1,0:T(1,128)S(1)} custom-call(s32[2]{0:T(128)S(1)} %pad_add_fusion.flip, bf16[8,65,512]{2,1,0:T(8,128)(2,1)S(1)} %constant_dynamic-update-slice_fusion.5.u_ref, bf16[1,2048]{1,0:T(2,128)(2,1)S(1)} %broadcast_in_dim.16.w_ref.z_ref.tm_ref, bf16[4096,2048]{1,0:T(8,128)(2,1)S(1)} %get-tuple-element.22.plan_ref, ...), custom_call_target="tpu_custom_call" | custom-call | flops 268435456 | bytes 16777216 | tf_op jit(solution)/shard_map/again_tile/pallas_call | solution.py:355
  70.2 1.3 %collective-permute-start.19 = (f32[1,1,6144]{2,1,0:T(1,128)S(1)}, f32[1,1,6144]{2,1,0:T(1,128)S(1)}, u32[]{:S(2)}, u32[]{:S(2)}) collective-permute-start(f32[1,1,6144]{2,1,0:T(1,128)S(1)} %again_tile.3), channel_id=1, source_target_pairs={{0,16},{8,24},{16,0},{24,8},{1,17},{9,25},{17,1},{25,9},{2,18},{10... | collective-permute-start | bytes 73736 | tf_op jit(solution)/shard_map/ppermute | solution.py:369
  72.0 3.4 %all-to-all-start = ((f32[8,1,4352]{2,1,0:T(1,128)}), f32[8,1,4352]{2,1,0:T(1,128)S(1)}, u32[]{:S(2)}, u32[]{:S(2)}) async-start(f32[8,1,4352]{2,1,0:T(1,128)} %get-tuple-element.20), calls=%async_computation | async-start | bytes 278528 | tf_op jit(solution)/shard_map/all_to_all | solution.py:387
  75.4 0.7 multiply_subtract_fusion
  76.1 6.8 %all-to-all-done = f32[8,1,4352]{2,1,0:T(1,128)S(1)} async-done(((f32[8,1,4352]{2,1,0:T(1,128)}), f32[8,1,4352]{2,1,0:T(1,128)S(1)}, u32[]{:S(2)}, u32[]{:S(2)}) %all-to-all-start) | async-done | bytes 139296 | tf_op jit(solution)/shard_map/all_to_all | solution.py:387
  82.9 0.7 multiply_subtract_fusion.1
  (50 shorter events, 3.3 us)
Async XLA Ops:
  0.6 6.8 %collective-permute-start = (bf16[8,2048]{1,0:T(8,128)(2,1)}, bf16[8,2048]{1,0:T(8,128)(2,1)S(1)}, u32[]{:S(2)}, u32[]{:S(2)}) collective-permute-start(bf16[8,2048]{1,0:T(8,128)(2,1)} %bitcast.65), channel_id=1, source_target_pairs={{0,1},{1,0},{2,3},{3,2},{4,5},{5,4},{6,7},{7,6},{8,9},{9,8},{10,11... | collective-permute-start | bytes 98312 | tf_op jit(solution)/shard_map/ppermute | solution.py:375
  5.2 7.7 %collective-permute-start.10 = (bf16[65,512]{1,0:T(8,128)(2,1)S(1)}, bf16[65,512]{1,0:T(8,128)(2,1)S(1)}, u32[]{:S(2)}, u32[]{:S(2)}) collective-permute-start(bf16[65,512]{1,0:T(8,128)(2,1)S(1)} %get-tuple-element.25), channel_id=1, source_target_pairs={{0,1},{1,0},{2,3},{3,2},{4,5},{5,4},{6,7},{7,6},{8,9},{9,8},{10,11... | collective-permute-start | bytes 199688 | tf_op jit(solution)/shard_map/ppermute | solution.py:375
  8.2 9.2 %collective-permute-start.1 = (bf16[2,8,2048]{2,1,0:T(8,128)(2,1)S(1)}, bf16[2,8,2048]{2,1,0:T(8,128)(2,1)S(1)}, u32[]{:S(2)}, u32[]{:S(2)}) collective-permute-start(bf16[2,8,2048]{2,1,0:T(8,128)(2,1)S(1)} %pad_maximum_fusion.2), channel_id=1, source_target_pairs={{0,2},{1,3},{2,0},{3,1},{4,6},{5,7},{6,4},{7,5},{8,10},{9,11},{10,... | collective-permute-start | bytes 196616 | tf_op jit(solution)/shard_map/ppermute | solution.py:381
  10.3 7.1 %collective-permute-start.2 = (bf16[2,8,2048]{2,1,0:T(8,128)(2,1)S(1)}, bf16[2,8,2048]{2,1,0:T(8,128)(2,1)S(1)}, u32[]{:S(2)}, u32[]{:S(2)}) collective-permute-start(bf16[2,8,2048]{2,1,0:T(8,128)(2,1)S(1)} %pad_maximum_fusion.2), channel_id=1, source_target_pairs={{0,4},{1,5},{2,6},{3,7},{4,0},{5,1},{6,2},{7,3},{8,12},{9,13},{10,... | collective-permute-start | bytes 196616 | tf_op jit(solution)/shard_map/ppermute | solution.py:381
  12.9 6.9 %collective-permute-start.3 = (bf16[2,8,2048]{2,1,0:T(8,128)(2,1)S(1)}, bf16[2,8,2048]{2,1,0:T(8,128)(2,1)S(1)}, u32[]{:S(2)}, u32[]{:S(2)}) collective-permute-start(bf16[2,8,2048]{2,1,0:T(8,128)(2,1)S(1)} %pad_maximum_fusion.2), channel_id=1, source_target_pairs={{0,6},{1,7},{2,4},{3,5},{4,2},{5,3},{6,0},{7,1},{8,14},{9,15},{10,... | collective-permute-start | bytes 196616 | tf_op jit(solution)/shard_map/ppermute | solution.py:381
  12.9 19.0 %collective-permute-start.11 = (bf16[2,65,512]{2,1,0:T(8,128)(2,1)S(1)}, bf16[2,65,512]{2,1,0:T(8,128)(2,1)S(1)}, u32[]{:S(2)}, u32[]{:S(2)}) collective-permute-start(bf16[2,65,512]{2,1,0:T(8,128)(2,1)S(1)} %pad_maximum_fusion.1), channel_id=1, source_target_pairs={{0,2},{1,3},{2,0},{3,1},{4,6},{5,7},{6,4},{7,5},{8,10},{9,11},{10,... | collective-permute-start | bytes 399368 | tf_op jit(solution)/shard_map/ppermute | solution.py:381
  13.9 18.1 %collective-permute-start.12 = (bf16[2,65,512]{2,1,0:T(8,128)(2,1)S(1)}, bf16[2,65,512]{2,1,0:T(8,128)(2,1)S(1)}, u32[]{:S(2)}, u32[]{:S(2)}) collective-permute-start(bf16[2,65,512]{2,1,0:T(8,128)(2,1)S(1)} %pad_maximum_fusion.1), channel_id=1, source_target_pairs={{0,4},{1,5},{2,6},{3,7},{4,0},{5,1},{6,2},{7,3},{8,12},{9,13},{10,... | collective-permute-start | bytes 399368 | tf_op jit(solution)/shard_map/ppermute | solution.py:381
  19.8 10.8 %collective-permute-start.6 = (bf16[65,256]{1,0:T(8,128)(2,1)S(1)}, bf16[65,256]{1,0:T(8,128)(2,1)S(1)}, u32[]{:S(2)}, u32[]{:S(2)}) collective-permute-start(bf16[65,256]{1,0:T(8,128)(2,1)S(1)} %fusion.1), channel_id=1, source_target_pairs={{0,24},{8,16},{16,8},{24,0},{1,25},{9,17},{17,9},{25,1},{2,26},{10... | collective-permute-start | bytes 99848 | tf_op jit(solution)/shard_map/ppermute | solution.py:369
  19.9 12.1 %collective-permute-start.5 = (bf16[65,256]{1,0:T(8,128)(2,1)S(1)}, bf16[65,256]{1,0:T(8,128)(2,1)S(1)}, u32[]{:S(2)}, u32[]{:S(2)}) collective-permute-start(bf16[65,256]{1,0:T(8,128)(2,1)S(1)} %fusion.1), channel_id=1, source_target_pairs={{0,16},{8,24},{16,0},{24,8},{1,17},{9,25},{17,1},{25,9},{2,18},{10... | collective-permute-start | bytes 99848 | tf_op jit(solution)/shard_map/ppermute | solution.py:369
  21.5 10.5 %collective-permute-start.4 = (bf16[65,256]{1,0:T(8,128)(2,1)S(1)}, bf16[65,256]{1,0:T(8,128)(2,1)S(1)}, u32[]{:S(2)}, u32[]{:S(2)}) collective-permute-start(bf16[65,256]{1,0:T(8,128)(2,1)S(1)} %fusion.1), channel_id=1, source_target_pairs={{0,8},{8,0},{16,24},{24,16},{1,9},{9,1},{17,25},{25,17},{2,10},{10... | collective-permute-start | bytes 99848 | tf_op jit(solution)/shard_map/ppermute | solution.py:369
  21.7 0.9 %copy-start = (bf16[2048,64]{0,1:T(8,128)(2,1)S(1)}, bf16[2048,64]{0,1:T(8,128)(2,1)}, u32[]{:S(2)}) copy-start(bf16[2048,64]{0,1:T(8,128)(2,1)} %param.5) | copy-start | bytes 786436
  30.5 28.1 %copy-start.1 = (bf16[2048,64]{0,1:T(8,128)(2,1)S(1)}, bf16[2048,64]{0,1:T(8,128)(2,1)}, u32[]{:S(2)}) copy-start(bf16[2048,64]{0,1:T(8,128)(2,1)} %param.5) | copy-start | bytes 786436
  30.6 8.0 %collective-permute-start.13 = (bf16[2,65,512]{2,1,0:T(8,128)(2,1)S(1)}, bf16[2,65,512]{2,1,0:T(8,128)(2,1)S(1)}, u32[]{:S(2)}, u32[]{:S(2)}) collective-permute-start(bf16[2,65,512]{2,1,0:T(8,128)(2,1)S(1)} %pad_maximum_fusion.1), channel_id=1, source_target_pairs={{0,6},{1,7},{2,4},{3,5},{4,2},{5,3},{6,0},{7,1},{8,14},{9,15},{10,... | collective-permute-start | bytes 399368 | tf_op jit(solution)/shard_map/ppermute | solution.py:381
  44.4 5.0 %collective-permute-start.14 = (f32[1,6144]{1,0:T(1,128)S(1)}, f32[1,6144]{1,0:T(1,128)S(1)}, u32[]{:S(2)}, u32[]{:S(2)}) collective-permute-start(f32[1,6144]{1,0:T(1,128)S(1)} %bitcast.61), channel_id=1, source_target_pairs={{0,1},{1,0},{2,3},{3,2},{4,5},{5,4},{6,7},{7,6},{8,9},{9,8},{10,11... | collective-permute-start | bytes 73736 | tf_op jit(solution)/shard_map/ppermute | solution.py:421
  47.5 5.6 %collective-permute-start.7 = (f32[1,1,3072]{2,1,0:T(1,128)S(1)}, f32[1,1,3072]{2,1,0:T(1,128)S(1)}, u32[]{:S(2)}, u32[]{:S(2)}) collective-permute-start(f32[1,1,3072]{2,1,0:T(1,128)S(1)} %get-tuple-element.16.refs_0_), channel_id=1, source_target_pairs={{0,8},{8,0},{16,24},{24,16},{1,9},{9,1},{17,25},{25,17},{2,10},{10... | collective-permute-start | bytes 36872 | tf_op jit(solution)/shard_map/ppermute | solution.py:369
  47.5 7.1 %collective-permute-start.8 = (f32[1,1,3072]{2,1,0:T(1,128)S(1)}, f32[1,1,3072]{2,1,0:T(1,128)S(1)}, u32[]{:S(2)}, u32[]{:S(2)}) collective-permute-start(f32[1,1,3072]{2,1,0:T(1,128)S(1)} %get-tuple-element.16.refs_0_), channel_id=1, source_target_pairs={{0,16},{8,24},{16,0},{24,8},{1,17},{9,25},{17,1},{25,9},{2,18},{10... | collective-permute-start | bytes 36872 | tf_op jit(solution)/shard_map/ppermute | solution.py:369
  48.9 5.8 %collective-permute-start.9 = (f32[1,1,3072]{2,1,0:T(1,128)S(1)}, f32[1,1,3072]{2,1,0:T(1,128)S(1)}, u32[]{:S(2)}, u32[]{:S(2)}) collective-permute-start(f32[1,1,3072]{2,1,0:T(1,128)S(1)} %get-tuple-element.16.refs_0_), channel_id=1, source_target_pairs={{0,24},{8,16},{16,8},{24,0},{1,25},{9,17},{17,9},{25,1},{2,26},{10... | collective-permute-start | bytes 36872 | tf_op jit(solution)/shard_map/ppermute | solution.py:369
  49.4 6.1 %collective-permute-start.15 = (f32[1,6144]{1,0:T(1,128)S(1)}, f32[1,6144]{1,0:T(1,128)S(1)}, u32[]{:S(2)}, u32[]{:S(2)}) collective-permute-start(f32[1,6144]{1,0:T(1,128)S(1)} %compare_select_fusion.refs_4_.refs_0_), channel_id=1, source_target_pairs={{0,2},{1,3},{2,0},{3,1},{4,6},{5,7},{6,4},{7,5},{8,10},{9,11},{10,... | collective-permute-start | bytes 73736 | tf_op jit(solution)/shard_map/ppermute | solution.py:369
  52.1 4.8 %collective-permute-start.16 = (f32[1,6144]{1,0:T(1,128)S(1)}, f32[1,6144]{1,0:T(1,128)S(1)}, u32[]{:S(2)}, u32[]{:S(2)}) collective-permute-start(f32[1,6144]{1,0:T(1,128)S(1)} %compare_select_fusion.refs_4_.refs_0_), channel_id=1, source_target_pairs={{0,4},{1,5},{2,6},{3,7},{4,0},{5,1},{6,2},{7,3},{8,12},{9,13},{10,... | collective-permute-start | bytes 73736 | tf_op jit(solution)/shard_map/ppermute | solution.py:369
  53.0 5.6 %collective-permute-start.17 = (f32[1,6144]{1,0:T(1,128)S(1)}, f32[1,6144]{1,0:T(1,128)S(1)}, u32[]{:S(2)}, u32[]{:S(2)}) collective-permute-start(f32[1,6144]{1,0:T(1,128)S(1)} %compare_select_fusion.refs_4_.refs_0_), channel_id=1, source_target_pairs={{0,6},{1,7},{2,4},{3,5},{4,2},{5,3},{6,0},{7,1},{8,14},{9,15},{10,... | collective-permute-start | bytes 73736 | tf_op jit(solution)/shard_map/ppermute | solution.py:369
  55.5 16.5 %copy-start.2 = (bf16[2048]{0:T(1024)(128)(2,1)S(1)}, bf16[2048]{0:T(1024)(128)(2,1)}, u32[]{:S(2)}) copy-start(bf16[2048]{0:T(1024)(128)(2,1)} %param.7) | copy-start | bytes 12292
  70.1 5.3 %collective-permute-start.20 = (f32[1,1,6144]{2,1,0:T(1,128)S(1)}, f32[1,1,6144]{2,1,0:T(1,128)S(1)}, u32[]{:S(2)}, u32[]{:S(2)}) collective-permute-start(f32[1,1,6144]{2,1,0:T(1,128)S(1)} %again_tile.3), channel_id=1, source_target_pairs={{0,24},{8,16},{16,8},{24,0},{1,25},{9,17},{17,9},{25,1},{2,26},{10... | collective-permute-start | bytes 73736 | tf_op jit(solution)/shard_map/ppermute | solution.py:369
  70.2 5.3 %collective-permute-start.19 = (f32[1,1,6144]{2,1,0:T(1,128)S(1)}, f32[1,1,6144]{2,1,0:T(1,128)S(1)}, u32[]{:S(2)}, u32[]{:S(2)}) collective-permute-start(f32[1,1,6144]{2,1,0:T(1,128)S(1)} %again_tile.3), channel_id=1, source_target_pairs={{0,16},{8,24},{16,0},{24,8},{1,17},{9,25},{17,1},{25,9},{2,18},{10... | collective-permute-start | bytes 73736 | tf_op jit(solution)/shard_map/ppermute | solution.py:369
  71.5 3.9 %collective-permute-start.18 = (f32[1,1,6144]{2,1,0:T(1,128)S(1)}, f32[1,1,6144]{2,1,0:T(1,128)S(1)}, u32[]{:S(2)}, u32[]{:S(2)}) collective-permute-start(f32[1,1,6144]{2,1,0:T(1,128)S(1)} %again_tile.3), channel_id=1, source_target_pairs={{0,8},{8,0},{16,24},{24,16},{1,9},{9,1},{17,25},{25,17},{2,10},{10... | collective-permute-start | bytes 73736 | tf_op jit(solution)/shard_map/ppermute | solution.py:369
  72.0 10.9 %all-to-all-start = ((f32[8,1,4352]{2,1,0:T(1,128)}), f32[8,1,4352]{2,1,0:T(1,128)S(1)}, u32[]{:S(2)}, u32[]{:S(2)}) async-start(f32[8,1,4352]{2,1,0:T(1,128)} %get-tuple-element.20), calls=%async_computation | async-start | bytes 278528 | tf_op jit(solution)/shard_map/all_to_all | solution.py:387

commit v5 on v4

--- a/solution.py
+++ b/solution.py
@@ -72,6 +72,10 @@
 
 def damped(log_mass, log_total):
     return log_mass - 0.5 * DAMPING * (log_total - log_mass)
+
+
+def kept(log_mass, weight):
+    return 0.5 * EPSILON * (weight - log_mass + DAMPING * weight)
 
 
 def tree(parts, op):
@@ -191,7 +195,7 @@
     )(turn, t, w, s, z)
 
 
-def cross_again_kernel(count, width, turn, t_ref, tm_ref, s_ref, sm_ref, more_ref, *refs):
+def cross_again_kernel(count, width, turn, t_ref, tm_ref, s_ref, sm_ref, more_ref, rest_ref, *refs):
     parts, cols = refs[:count], refs[count : count + width]
     row_ref, w_ref, z_ref, col_ref = refs[count + width : count + width + 4]
     scratch = refs[count + width + 4 :]
@@ -200,29 +204,35 @@
 
     @pl.when(pl.program_id(0) == 0)
     def _():
-        z = damped(log_of(sm_ref[...]), log_sum([part[:, 0:n] for part in cols]))
-        z_ref[...] = z
+        log_mass = log_of(sm_ref[...])
+        z = damped(log_mass, log_sum([part[:, 0:n] for part in cols]))
+        z_ref[...] = kept(log_mass, z)
         start_cross(s_ref[...], z, rhs, ctop, csum)
 
-    w = damped(log_of(tm_ref[...]), log_sum([part[0] for part in parts]))
-    w_ref[...] = w
-    row_ref[...] = cross_block(swapped(turn, t_ref), w, *scratch)
+    log_mass = log_of(tm_ref[...])
+    w = damped(log_mass, log_sum([part[0] for part in parts]))
+    w_ref[...] = kept(log_mass, w)
+    bt = w.shape[1]
+    here = pl.ds(pl.multiple_of(pl.program_id(0) * bt, 128), bt)
+    row_ref[0, :, here] = cross_block(swapped(turn, t_ref), w, *scratch)
 
     @pl.when(last_step())
     def _():
+        row_ref[0, :, row_ref.shape[2] - rest_ref.shape[1] :] = rest_ref[...]
         logs = col_logs(ctop, csum)
         for k in range(col_ref.shape[0]):
             col_ref[k, :, 0:n] = logs
             col_ref[k, :, n:] = more_ref[...]
 
 
-def cross_again(turn, t, tmass, s, smass, by_col, by_row, more):
+def cross_again(turn, t, tmass, s, smass, by_col, by_row, more, rest):
     count, ch, nt = t.shape
     ch = ch * count
     n = s.shape[1]
     bt = math.gcd(GROUP, nt)
     lanes = pl.BlockSpec((1, bt), lambda i, f: (0, i))
     shape = (count, 1, n + more.shape[1])
+    long = (1, 1, nt + rest.shape[1])
     return pl.pallas_call(
         functools.partial(cross_again_kernel, len(by_row), len(by_col)),
         grid_spec=pltpu.PrefetchScalarGridSpec(
@@ -234,17 +244,18 @@
                 whole((ch, n)),
                 whole((1, n)),
                 whole(more.shape),
+                whole(rest.shape),
             ]
             + [pl.BlockSpec((1, 1, bt), lambda i, f: (0, 0, i))] * len(by_row)
             + [whole(part.shape) for part in by_col],
-            out_specs=[lanes, lanes, whole((1, n)), whole(shape)],
+            out_specs=[whole(long), lanes, whole((1, n)), whole(shape)],
             scratch_shapes=cross_scratch(ch, bt, n),
         ),
-        out_shape=[jax.ShapeDtypeStruct(k, jnp.float32) for k in ((1, nt), (1, nt), (1, n), shape)],
+        out_shape=[jax.ShapeDtypeStruct(k, jnp.float32) for k in (long, (1, nt), (1, n), shape)],
         cost_estimate=cross_cost(nt, n, ch),
         compiler_params=pltpu.CompilerParams(vmem_limit_bytes=LIMIT),
         name="cross_again",
-    )(turn, t, tmass, s, smass, more, *by_row, *by_col)
+    )(turn, t, tmass, s, smass, more, rest, *by_row, *by_col)
 
 
 def points(flip, u_ref, ch):
@@ -370,17 +381,15 @@
     ]
 
 
-def near(x, axis):
+def send(x, axis, step):
     count = lax.axis_size(axis)
-    return jnp.stack([x, lax.ppermute(x, axis, [(i, i ^ 1) for i in range(count)])])
-
-
-def far(pair, axis):
+    return lax.ppermute(x, axis, [(i, i ^ step) for i in range(count)])
+
+
+def gather(x, axis):
     count = lax.axis_size(axis)
-    parts = [
-        lax.ppermute(pair, axis, [(i, i ^ k) for i in range(count)]) for k in range(2, count, 2)
-    ]
-    return jnp.concatenate([pair] + parts, axis=0)
+    pair = jnp.stack([x, send(x, axis, 1)])
+    return jnp.concatenate([pair] + [send(pair, axis, k) for k in range(2, count, 2)])
 
 
 def swap(x, axis):
@@ -398,16 +407,14 @@
     pt = nt // rows
     half = DAMPING * EPSILON * 0.5
 
+    target_lanes = target_desc.T
+    target_blocks = target_lanes.reshape(cols, -1, nt)
+    source_lanes = gather(source_desc.T, "col").reshape(-1, ns)
+    piece = jnp.concatenate([target_lanes, target_mass[None]], axis=0)
+    piece = lax.dynamic_slice_in_dim(piece, row * pt, pt, 1)
+    target_set = gather(piece, "col")
     source_mass = source_mass[None]
     target_mass = target_mass[None]
-    target_lanes = target_desc.T
-    target_blocks = target_lanes.reshape(cols, -1, nt)
-    piece = jnp.concatenate([target_lanes, target_mass], axis=0)
-    piece = lax.dynamic_slice_in_dim(piece, row * pt, pt, 1)
-    pair = near(source_desc.T, "col")
-    target_pair = near(piece, "col")
-    source_lanes = far(pair, "col").reshape(-1, ns)
-    target_set = far(target_pair, "col")
     piece = jnp.concatenate([source_lanes, source_mass], axis=0)
     piece = lax.dynamic_slice_in_dim(piece, col * ps, ps, 1)
     source_set = jnp.stack(collect(piece, "row"))
@@ -425,26 +432,32 @@
     by_row = collect(row_sums, "row")
     by_col = collect(sums, "col", 2)
     more = again_tile(source_set, source_mass, source_plan, flip, by_row, nt, ps)
-    ct, w, z, sums = cross_again(
-        turn, target_blocks, target_mass, source_lanes, source_mass, by_col, by_row, more[0]
+    again = again_tile(
+        target_set, target_mass, target_plan, spot, by_col, ns, pt, place=True
+    )
+    row_sums, base_target, base_source, sums = cross_again(
+        turn,
+        target_blocks,
+        target_mass,
+        source_lanes,
+        source_mass,
+        by_col,
+        by_row,
+        more[0],
+        again[0],
     )
     last_col = swap(sums, "col")
-    sums = again_tile(
-        target_set, target_mass, target_plan, spot, by_col, ns, pt, ct, True
-    )
-    last_row = [part[0] for part in collect(sums, "row")]
-
-    slog = jnp.log(source_mass.astype(jnp.float32))
-    tlog = jnp.log(target_mass.astype(jnp.float32))
+    last_row = [part[0] for part in collect(row_sums, "row")]
+
     cs = log_sum([part[:, :ns] for part in last_col])
     ss_again = tree([part[:, ns : 2 * ns] for part in last_col], jnp.add)
     ss = last_col[:, :, 2 * ns :].reshape(1, ns)
-    cross_source = 0.5 * EPSILON * (z - slog) - half * (cs - z)
+    cross_source = base_source - half * cs
     self_source = 0.5 * ss - half * jnp.log(ss_again)
     ct = log_sum([part[:, :nt] for part in last_row])
     st_again = tree([part[:, nt : 2 * nt] for part in last_row], jnp.add)
     st = tree([part[:, 2 * nt :] for part in last_row], jnp.add)
-    cross_target = 0.5 * EPSILON * (w - tlog) - half * (ct - w)
+    cross_target = base_target - half * ct
     self_target = 0.5 * st - half * jnp.log(st_again)
     return (cross_source[0], cross_target[0], self_source[0], self_target[0])
 

time: 84.2 us -> 85.5 us (1.015)
  waiting for transfers between devices: 18.7 us -> 20.8 us
    ppermute x8, waiting for transfers between devices: 8.87 us -> 11.5 us  [send(): return lax.ppermute(x, axis, [(i, i ^ step) for i in range(count)])]
    all_to_all x1, starting transfers between devices: 3.39 us -> 4.51 us  [swap(): return lax.all_to_all(x, axis, 0, 0)]
    ppermute x1, starting transfers between devices: 1.56 us -> 0.65 us  [body(): other = lax.ppermute(sums, 'col', [(i, i ^ 1) for i in range(cols)])]
    unnamed x13 -> x11, local copies, waits for them, and re-layouts: 1.77 us -> 1.8 us
  transfers between devices with their start and end apart: 22 -> 22, of which waited for: 5 -> 6; matrix products, arithmetic and copies ran while one was open for 6% -> 4% of each run, Pallas kernels for 12% -> 12%
where the time goes in v5:
time: 85.5 us; the launch traced here: 85 us
  starting transfers between devices  29.4 us (34%)
  Pallas kernels  27.5 us (32%)
  waiting for transfers between devices  20.8 us (24%)
  other arithmetic  3.25 us (4%)
  local copies, waits for them, and re-layouts  3.21 us (4%)
  between operations  0.86 us (1%)
    ppermute x8, starting transfers between devices, send(): return lax.ppermute(x, axis, [(i, i ^ step) for i in range(count)])  13.1 us
    ppermute x8, waiting for transfers between devices, send(): return lax.ppermute(x, axis, [(i, i ^ step) for i in range(count)])  11.5 us
    ppermute x12, starting transfers between devices, collect(): lax.ppermute(x, axis, [(i, i ^ k) for i in range(count)])  11.1 us
    pallas_call x1, Pallas kernels, cross_again(): pl.pallas_call(functools.partial(cross_again_kernel, len(by_row), len(by_...  8.55 us
    pallas_call x1, Pallas kernels, cross_tile(): pl.pallas_call(cross_kernel, grid_spec=pltpu.PrefetchScalarGridSpec(num_s...  7.85 us
    pallas_call x2, Pallas kernels, self_tile(): pl.pallas_call(self_kernel, grid_spec=pltpu.PrefetchScalarGridSpec(num_sc...  7.33 us
    all_to_all x1, waiting for transfers between devices, swap(): return lax.all_to_all(x, axis, 0, 0)  6.82 us
    all_to_all x1, starting transfers between devices, swap(): return lax.all_to_all(x, axis, 0, 0)  4.51 us
  transfers between devices with their start and end apart: 22, of which 6 were waited for; matrix products, arithmetic and copies ran while one was open for 4% of the time, Pallas kernels for 12%

profile of v5, /device:TPU:0, one launch (start us, length us, event | category | flops | bytes accessed | tf_op | source)
XLA Modules:
  0.0 85.0 jit_solution(9748712509191046530)
XLA Ops:
  0.6 0.7 broadcast_in_dim.14.w_ref.z_ref.tm_ref
  1.3 0.8 constant_dynamic-update-slice_fusion.9
  2.2 3.0 %collective-permute-start.10 = (bf16[65,512]{1,0:T(8,128)(2,1)S(1)}, bf16[65,512]{1,0:T(8,128)(2,1)S(1)}, u32[]{:S(2)}, u32[]{:S(2)}) collective-permute-start(bf16[65,512]{1,0:T(8,128)(2,1)S(1)} %get-tuple-element.25), channel_id=1, source_target_pairs={{0,1},{1,0},{2,3},{3,2},{4,5},{5,4},{6,7},{7,6},{8,9},{9,8},{10,11... | collective-permute-start | bytes 199688 | tf_op jit(solution)/shard_map/ppermute | solution.py:386
  5.3 0.8 constant_dynamic-update-slice_fusion.4
  6.1 0.7 broadcast_in_dim.15.z_ref.sm_ref
  6.8 2.6 %collective-permute-done = bf16[8,2048]{1,0:T(8,128)(2,1)S(1)} collective-permute-done((bf16[8,2048]{1,0:T(8,128)(2,1)}, bf16[8,2048]{1,0:T(8,128)(2,1)S(1)}, u32[]{:S(2)}, u32[]{:S(2)}) %collective-permute-start) | collective-permute-done | bytes 32800 | tf_op jit(solution)/shard_map/ppermute | solution.py:386
  9.3 0.8 pad_maximum_fusion.2
  10.1 1.6 %collective-permute-start.1 = (bf16[2,8,2048]{2,1,0:T(8,128)(2,1)S(1)}, bf16[2,8,2048]{2,1,0:T(8,128)(2,1)S(1)}, u32[]{:S(2)}, u32[]{:S(2)}) collective-permute-start(bf16[2,8,2048]{2,1,0:T(8,128)(2,1)S(1)} %pad_maximum_fusion.2), channel_id=1, source_target_pairs={{0,2},{1,3},{2,0},{3,1},{4,6},{5,7},{6,4},{7,5},{8,10},{9,11},{10,... | collective-permute-start | bytes 196616 | tf_op jit(solution)/shard_map/ppermute | solution.py:386
  11.7 2.6 %collective-permute-start.2 = (bf16[2,8,2048]{2,1,0:T(8,128)(2,1)S(1)}, bf16[2,8,2048]{2,1,0:T(8,128)(2,1)S(1)}, u32[]{:S(2)}, u32[]{:S(2)}) collective-permute-start(bf16[2,8,2048]{2,1,0:T(8,128)(2,1)S(1)} %pad_maximum_fusion.2), channel_id=1, source_target_pairs={{0,4},{1,5},{2,6},{3,7},{4,0},{5,1},{6,2},{7,3},{8,12},{9,13},{10,... | collective-permute-start | bytes 196616 | tf_op jit(solution)/shard_map/ppermute | solution.py:386
  14.5 0.7 collective-permute-start.11
  15.3 3.5 %collective-permute-start.12 = (bf16[2,65,512]{2,1,0:T(8,128)(2,1)S(1)}, bf16[2,65,512]{2,1,0:T(8,128)(2,1)S(1)}, u32[]{:S(2)}, u32[]{:S(2)}) collective-permute-start(bf16[2,65,512]{2,1,0:T(8,128)(2,1)S(1)} %pad_maximum_fusion.1), channel_id=1, source_target_pairs={{0,4},{1,5},{2,6},{3,7},{4,0},{5,1},{6,2},{7,3},{8,12},{9,13},{10,... | collective-permute-start | bytes 399368 | tf_op jit(solution)/shard_map/ppermute | solution.py:386
  18.8 2.3 %collective-permute-done.3 = bf16[2,8,2048]{2,1,0:T(8,128)(2,1)S(1)} collective-permute-done((bf16[2,8,2048]{2,1,0:T(8,128)(2,1)S(1)}, bf16[2,8,2048]{2,1,0:T(8,128)(2,1)S(1)}, u32[]{:S(2)}, u32[]{:S(2)}) %collective-permute-start.3) | collective-permute-done | bytes 65568 | tf_op jit(solution)/shard_map/ppermute | solution.py:386
  21.2 1.6 %collective-permute-start.5 = (bf16[65,256]{1,0:T(8,128)(2,1)S(1)}, bf16[65,256]{1,0:T(8,128)(2,1)S(1)}, u32[]{:S(2)}, u32[]{:S(2)}) collective-permute-start(bf16[65,256]{1,0:T(8,128)(2,1)S(1)} %fusion.1), channel_id=1, source_target_pairs={{0,16},{8,24},{16,0},{24,8},{1,17},{9,25},{17,1},{25,9},{2,18},{10... | collective-permute-start | bytes 99848 | tf_op jit(solution)/shard_map/ppermute | solution.py:380
  23.1 0.9 %copy-done = bf16[2048,64]{0,1:T(8,128)(2,1)S(1)} copy-done((bf16[2048,64]{0,1:T(8,128)(2,1)S(1)}, bf16[2048,64]{0,1:T(8,128)(2,1)}, u32[]{:S(2)}) %copy-start) | copy-done | bytes 262168
  24.0 7.9 %cross_tile.1 = (f32[1,2048]{1,0:T(1,128)S(1)}, f32[1,2048]{1,0:T(1,128)S(1)}) custom-call(s32[1]{0:T(128)} %bitcast.turn.flip, bf16[8,8,2048]{2,1,0:T(8,128)(2,1)S(1)} %bitcast.56, bf16[1,2048]{1,0:T(2,128)(2,1)S(1)} %broadcast_in_dim.14.w_ref.z_ref.tm_ref, bf16[64,2048]{1,0:T(8,128)(2,1)S(1)} %bitcast.51, bf16[1,2048]{1,0:T(2,128)(2,1)S(1)} %broadcast_in_dim.15.z_ref.sm_ref), custom_call_target="tpu_custom_call" | custom-call | flops 2147483648 | bytes 1048576 | tf_op jit(solution)/shard_map/cross_tile/pallas_call | solution.py:177
  31.9 1.4 %collective-permute-start.13 = (bf16[2,65,512]{2,1,0:T(8,128)(2,1)S(1)}, bf16[2,65,512]{2,1,0:T(8,128)(2,1)S(1)}, u32[]{:S(2)}, u32[]{:S(2)}) collective-permute-start(bf16[2,65,512]{2,1,0:T(8,128)(2,1)S(1)} %pad_maximum_fusion.1), channel_id=1, source_target_pairs={{0,6},{1,7},{2,4},{3,5},{4,2},{5,3},{6,0},{7,1},{8,14},{9,15},{10,... | collective-permute-start | bytes 399368 | tf_op jit(solution)/shard_map/ppermute | solution.py:386
  33.4 6.6 %collective-permute-done.13 = bf16[2,65,512]{2,1,0:T(8,128)(2,1)S(1)} collective-permute-done((bf16[2,65,512]{2,1,0:T(8,128)(2,1)S(1)}, bf16[2,65,512]{2,1,0:T(8,128)(2,1)S(1)}, u32[]{:S(2)}, u32[]{:S(2)}) %collective-permute-start.13) | collective-permute-done | bytes 133152 | tf_op jit(solution)/shard_map/ppermute | solution.py:386
  40.0 5.9 %self_tile.3 = (f32[1,1,6144]{2,1,0:T(1,128)S(1)}, bf16[4096,2048]{1,0:T(8,128)(2,1)S(1)}) custom-call(s32[1]{0:T(128)} %bitcast.turn.flip, bf16[8,65,512]{2,1,0:T(8,128)(2,1)S(1)} %constant_dynamic-update-slice_fusion.5.u_ref, bf16[64,2048]{1,0:T(8,128)(2,1)S(1)} %bitcast.57, bf16[1,2048]{1,0:T(2,128)(2,1)S(1)} %broadcast_in_dim.14.w_ref.z_ref.tm_ref, ...), custom_call_target="tpu_custom_call" | custom-call | flops 2181038080 | bytes 266240 | tf_op jit(solution)/shard_map/self_tile/pallas_call | solution.py:309
  46.6 1.5 %self_tile.2 = (f32[1,1,3072]{2,1,0:T(1,128)S(1)}, bf16[1024,2048]{1,0:T(8,128)(2,1)S(1)}) custom-call(s32[1]{0:T(128)} %bitcast.8.flip, bf16[4,65,256]{2,1,0:T(8,128)(2,1)S(1)} %pad_maximum_fusion.u_ref, bf16[64,2048]{1,0:T(8,128)(2,1)S(1)} %bitcast.53, bf16[1,2048]{1,0:T(2,128)(2,1)S(1)} %broadcast_in_dim.15.z_ref.sm_ref, ...), custom_call_target="tpu_custom_call" | custom-call | flops 545259520 | bytes 66560 | tf_op jit(solution)/shard_map/self_tile/pallas_call | solution.py:309
  48.1 1.6 %collective-permute-start.8 = (f32[1,1,3072]{2,1,0:T(1,128)S(1)}, f32[1,1,3072]{2,1,0:T(1,128)S(1)}, u32[]{:S(2)}, u32[]{:S(2)}) collective-permute-start(f32[1,1,3072]{2,1,0:T(1,128)S(1)} %get-tuple-element.16.refs_0_), channel_id=1, source_target_pairs={{0,16},{8,24},{16,0},{24,8},{1,17},{9,25},{17,1},{25,9},{2,18},{10... | collective-permute-start | bytes 36872 | tf_op jit(solution)/shard_map/ppermute | solution.py:380
  50.0 3.0 %collective-permute-start.15 = (f32[1,6144]{1,0:T(1,128)S(1)}, f32[1,6144]{1,0:T(1,128)S(1)}, u32[]{:S(2)}, u32[]{:S(2)}) collective-permute-start(f32[1,6144]{1,0:T(1,128)S(1)} %compare_select_fusion.refs_0_.refs_4_), channel_id=1, source_target_pairs={{0,2},{1,3},{2,0},{3,1},{4,6},{5,7},{6,4},{7,5},{8,10},{9,11},{10,... | collective-permute-start | bytes 73736 | tf_op jit(solution)/shard_map/ppermute | solution.py:380
  53.1 2.4 %collective-permute-start.17 = (f32[1,6144]{1,0:T(1,128)S(1)}, f32[1,6144]{1,0:T(1,128)S(1)}, u32[]{:S(2)}, u32[]{:S(2)}) collective-permute-start(f32[1,6144]{1,0:T(1,128)S(1)} %compare_select_fusion.refs_0_.refs_4_), channel_id=1, source_target_pairs={{0,6},{1,7},{2,4},{3,5},{4,2},{5,3},{6,0},{7,1},{8,14},{9,15},{10,... | collective-permute-start | bytes 73736 | tf_op jit(solution)/shard_map/ppermute | solution.py:380
  55.5 0.7 again_tile.2
  56.2 1.7 %collective-permute-done.16.refs_2_.refs_6_ = f32[1,6144]{1,0:T(1,128)S(1)} collective-permute-done((f32[1,6144]{1,0:T(1,128)S(1)}, f32[1,6144]{1,0:T(1,128)S(1)}, u32[]{:S(2)}, u32[]{:S(2)}) %collective-permute-start.16) | collective-permute-done | bytes 24608 | tf_op jit(solution)/shard_map/ppermute | solution.py:380
  58.0 0.7 collective-permute-done.17.refs_3_.refs_7_
  58.7 3.1 %again_tile.3 = f32[1,1,4096]{2,1,0:T(1,128)S(1)} custom-call(s32[2]{0:T(128)S(1)} %pad_add_fusion.flip, bf16[8,65,512]{2,1,0:T(8,128)(2,1)S(1)} %constant_dynamic-update-slice_fusion.5.u_ref, bf16[1,2048]{1,0:T(2,128)(2,1)S(1)} %broadcast_in_dim.14.w_ref.z_ref.tm_ref, bf16[4096,2048]{1,0:T(8,128)(2,1)S(1)} %get-tuple-element.18.plan_ref, ...), custom_call_target="tpu_custom_call" | custom-call | flops 268435456 | bytes 16777216 | tf_op jit(solution)/shard_map/again_tile/pallas_call | solution.py:366
  61.8 8.5 %cross_again.1 = (f32[1,1,6144]{2,1,0:T(1,128)S(1)}, f32[1,2048]{1,0:T(1,128)S(1)}, f32[1,2048]{1,0:T(1,128)S(1)}, f32[8,1,4352]{2,1,0:T(1,128)}) custom-call(s32[1]{0:T(128)} %bitcast.turn.flip, bf16[8,8,2048]{2,1,0:T(8,128)(2,1)S(1)} %bitcast.58, bf16[1,2048]{1,0:T(2,128)(2,1)S(1)} %broadcast_in_dim.14.w_ref.z_ref.tm_ref, bf16[64,2048]{1,0:T(8,128)(2,1)S(1)} %bitcast.54, ...), custom_call_target="tpu_custom_call" | custom-call | flops 2147483648 | bytes 1048576 | tf_op jit(solution)/shard_map/cross_again/pallas_call | solution.py:236
  70.3 1.5 %collective-permute-start.19 = (f32[1,1,6144]{2,1,0:T(1,128)S(1)}, f32[1,1,6144]{2,1,0:T(1,128)S(1)}, u32[]{:S(2)}, u32[]{:S(2)}) collective-permute-start(f32[1,1,6144]{2,1,0:T(1,128)S(1)} %get-tuple-element.23), channel_id=1, source_target_pairs={{0,16},{8,24},{16,0},{24,8},{1,17},{9,25},{17,1},{25,9},{2,18},{10... | collective-permute-start | bytes 73736 | tf_op jit(solution)/shard_map/ppermute | solution.py:380
  72.2 4.5 %all-to-all-start = ((f32[8,1,4352]{2,1,0:T(1,128)}), f32[8,1,4352]{2,1,0:T(1,128)S(1)}, u32[]{:S(2)}, u32[]{:S(2)}) async-start(f32[8,1,4352]{2,1,0:T(1,128)} %get-tuple-element.21), calls=%async_computation | async-start | bytes 278528 | tf_op jit(solution)/shard_map/all_to_all | solution.py:396
  76.7 0.7 multiply_subtract_fusion
  77.4 6.8 %all-to-all-done = f32[8,1,4352]{2,1,0:T(1,128)S(1)} async-done(((f32[8,1,4352]{2,1,0:T(1,128)}), f32[8,1,4352]{2,1,0:T(1,128)S(1)}, u32[]{:S(2)}, u32[]{:S(2)}) %all-to-all-start) | async-done | bytes 139296 | tf_op jit(solution)/shard_map/all_to_all | solution.py:396
  84.3 0.7 multiply_subtract_fusion.1
  (46 shorter events, 2.4 us)
Async XLA Ops:
  2.2 12.3 %collective-permute-start.10 = (bf16[65,512]{1,0:T(8,128)(2,1)S(1)}, bf16[65,512]{1,0:T(8,128)(2,1)S(1)}, u32[]{:S(2)}, u32[]{:S(2)}) collective-permute-start(bf16[65,512]{1,0:T(8,128)(2,1)S(1)} %get-tuple-element.25), channel_id=1, source_target_pairs={{0,1},{1,0},{2,3},{3,2},{4,5},{5,4},{6,7},{7,6},{8,9},{9,8},{10,11... | collective-permute-start | bytes 199688 | tf_op jit(solution)/shard_map/ppermute | solution.py:386
  5.2 4.1 %collective-permute-start = (bf16[8,2048]{1,0:T(8,128)(2,1)}, bf16[8,2048]{1,0:T(8,128)(2,1)S(1)}, u32[]{:S(2)}, u32[]{:S(2)}) collective-permute-start(bf16[8,2048]{1,0:T(8,128)(2,1)} %bitcast.65), channel_id=1, source_target_pairs={{0,1},{1,0},{2,3},{3,2},{4,5},{5,4},{6,7},{7,6},{8,9},{9,8},{10,11... | collective-permute-start | bytes 98312 | tf_op jit(solution)/shard_map/ppermute | solution.py:386
  10.1 8.7 %collective-permute-start.1 = (bf16[2,8,2048]{2,1,0:T(8,128)(2,1)S(1)}, bf16[2,8,2048]{2,1,0:T(8,128)(2,1)S(1)}, u32[]{:S(2)}, u32[]{:S(2)}) collective-permute-start(bf16[2,8,2048]{2,1,0:T(8,128)(2,1)S(1)} %pad_maximum_fusion.2), channel_id=1, source_target_pairs={{0,2},{1,3},{2,0},{3,1},{4,6},{5,7},{6,4},{7,5},{8,10},{9,11},{10,... | collective-permute-start | bytes 196616 | tf_op jit(solution)/shard_map/ppermute | solution.py:386
  11.7 7.1 %collective-permute-start.2 = (bf16[2,8,2048]{2,1,0:T(8,128)(2,1)S(1)}, bf16[2,8,2048]{2,1,0:T(8,128)(2,1)S(1)}, u32[]{:S(2)}, u32[]{:S(2)}) collective-permute-start(bf16[2,8,2048]{2,1,0:T(8,128)(2,1)S(1)} %pad_maximum_fusion.2), channel_id=1, source_target_pairs={{0,4},{1,5},{2,6},{3,7},{4,0},{5,1},{6,2},{7,3},{8,12},{9,13},{10,... | collective-permute-start | bytes 196616 | tf_op jit(solution)/shard_map/ppermute | solution.py:386
  14.3 6.9 %collective-permute-start.3 = (bf16[2,8,2048]{2,1,0:T(8,128)(2,1)S(1)}, bf16[2,8,2048]{2,1,0:T(8,128)(2,1)S(1)}, u32[]{:S(2)}, u32[]{:S(2)}) collective-permute-start(bf16[2,8,2048]{2,1,0:T(8,128)(2,1)S(1)} %pad_maximum_fusion.2), channel_id=1, source_target_pairs={{0,6},{1,7},{2,4},{3,5},{4,2},{5,3},{6,0},{7,1},{8,14},{9,15},{10,... | collective-permute-start | bytes 196616 | tf_op jit(solution)/shard_map/ppermute | solution.py:386
  14.5 18.8 %collective-permute-start.11 = (bf16[2,65,512]{2,1,0:T(8,128)(2,1)S(1)}, bf16[2,65,512]{2,1,0:T(8,128)(2,1)S(1)}, u32[]{:S(2)}, u32[]{:S(2)}) collective-permute-start(bf16[2,65,512]{2,1,0:T(8,128)(2,1)S(1)} %pad_maximum_fusion.1), channel_id=1, source_target_pairs={{0,2},{1,3},{2,0},{3,1},{4,6},{5,7},{6,4},{7,5},{8,10},{9,11},{10,... | collective-permute-start | bytes 399368 | tf_op jit(solution)/shard_map/ppermute | solution.py:386
  15.3 18.1 %collective-permute-start.12 = (bf16[2,65,512]{2,1,0:T(8,128)(2,1)S(1)}, bf16[2,65,512]{2,1,0:T(8,128)(2,1)S(1)}, u32[]{:S(2)}, u32[]{:S(2)}) collective-permute-start(bf16[2,65,512]{2,1,0:T(8,128)(2,1)S(1)} %pad_maximum_fusion.1), channel_id=1, source_target_pairs={{0,4},{1,5},{2,6},{3,7},{4,0},{5,1},{6,2},{7,3},{8,12},{9,13},{10,... | collective-permute-start | bytes 399368 | tf_op jit(solution)/shard_map/ppermute | solution.py:386
  21.2 10.8 %collective-permute-start.4 = (bf16[65,256]{1,0:T(8,128)(2,1)S(1)}, bf16[65,256]{1,0:T(8,128)(2,1)S(1)}, u32[]{:S(2)}, u32[]{:S(2)}) collective-permute-start(bf16[65,256]{1,0:T(8,128)(2,1)S(1)} %fusion.1), channel_id=1, source_target_pairs={{0,8},{8,0},{16,24},{24,16},{1,9},{9,1},{17,25},{25,17},{2,10},{10... | collective-permute-start | bytes 99848 | tf_op jit(solution)/shard_map/ppermute | solution.py:380
  21.2 12.1 %collective-permute-start.5 = (bf16[65,256]{1,0:T(8,128)(2,1)S(1)}, bf16[65,256]{1,0:T(8,128)(2,1)S(1)}, u32[]{:S(2)}, u32[]{:S(2)}) collective-permute-start(bf16[65,256]{1,0:T(8,128)(2,1)S(1)} %fusion.1), channel_id=1, source_target_pairs={{0,16},{8,24},{16,0},{24,8},{1,17},{9,25},{17,1},{25,9},{2,18},{10... | collective-permute-start | bytes 99848 | tf_op jit(solution)/shard_map/ppermute | solution.py:380
  22.8 10.5 %collective-permute-start.6 = (bf16[65,256]{1,0:T(8,128)(2,1)S(1)}, bf16[65,256]{1,0:T(8,128)(2,1)S(1)}, u32[]{:S(2)}, u32[]{:S(2)}) collective-permute-start(bf16[65,256]{1,0:T(8,128)(2,1)S(1)} %fusion.1), channel_id=1, source_target_pairs={{0,24},{8,16},{16,8},{24,0},{1,25},{9,17},{17,9},{25,1},{2,26},{10... | collective-permute-start | bytes 99848 | tf_op jit(solution)/shard_map/ppermute | solution.py:380
  23.1 0.9 %copy-start = (bf16[2048,64]{0,1:T(8,128)(2,1)S(1)}, bf16[2048,64]{0,1:T(8,128)(2,1)}, u32[]{:S(2)}) copy-start(bf16[2048,64]{0,1:T(8,128)(2,1)} %param.5) | copy-start | bytes 786436
  31.9 8.1 %collective-permute-start.13 = (bf16[2,65,512]{2,1,0:T(8,128)(2,1)S(1)}, bf16[2,65,512]{2,1,0:T(8,128)(2,1)S(1)}, u32[]{:S(2)}, u32[]{:S(2)}) collective-permute-start(bf16[2,65,512]{2,1,0:T(8,128)(2,1)S(1)} %pad_maximum_fusion.1), channel_id=1, source_target_pairs={{0,6},{1,7},{2,4},{3,5},{4,2},{5,3},{6,0},{7,1},{8,14},{9,15},{10,... | collective-permute-start | bytes 399368 | tf_op jit(solution)/shard_map/ppermute | solution.py:386
  45.9 15.9 %copy-start.1 = (bf16[2048,64]{0,1:T(8,128)(2,1)S(1)}, bf16[2048,64]{0,1:T(8,128)(2,1)}, u32[]{:S(2)}) copy-start(bf16[2048,64]{0,1:T(8,128)(2,1)} %param.5) | copy-start | bytes 786436
  45.9 4.0 %collective-permute-start.14 = (f32[1,6144]{1,0:T(1,128)S(1)}, f32[1,6144]{1,0:T(1,128)S(1)}, u32[]{:S(2)}, u32[]{:S(2)}) collective-permute-start(f32[1,6144]{1,0:T(1,128)S(1)} %bitcast.59), channel_id=1, source_target_pairs={{0,1},{1,0},{2,3},{3,2},{4,5},{5,4},{6,7},{7,6},{8,9},{9,8},{10,11... | collective-permute-start | bytes 73736 | tf_op jit(solution)/shard_map/ppermute | solution.py:428
  48.0 5.0 %collective-permute-start.7 = (f32[1,1,3072]{2,1,0:T(1,128)S(1)}, f32[1,1,3072]{2,1,0:T(1,128)S(1)}, u32[]{:S(2)}, u32[]{:S(2)}) collective-permute-start(f32[1,1,3072]{2,1,0:T(1,128)S(1)} %get-tuple-element.16.refs_0_), channel_id=1, source_target_pairs={{0,8},{8,0},{16,24},{24,16},{1,9},{9,1},{17,25},{25,17},{2,10},{10... | collective-permute-start | bytes 36872 | tf_op jit(solution)/shard_map/ppermute | solution.py:380
  48.1 7.4 %collective-permute-start.8 = (f32[1,1,3072]{2,1,0:T(1,128)S(1)}, f32[1,1,3072]{2,1,0:T(1,128)S(1)}, u32[]{:S(2)}, u32[]{:S(2)}) collective-permute-start(f32[1,1,3072]{2,1,0:T(1,128)S(1)} %get-tuple-element.16.refs_0_), channel_id=1, source_target_pairs={{0,16},{8,24},{16,0},{24,8},{1,17},{9,25},{17,1},{25,9},{2,18},{10... | collective-permute-start | bytes 36872 | tf_op jit(solution)/shard_map/ppermute | solution.py:380
  49.7 5.8 %collective-permute-start.9 = (f32[1,1,3072]{2,1,0:T(1,128)S(1)}, f32[1,1,3072]{2,1,0:T(1,128)S(1)}, u32[]{:S(2)}, u32[]{:S(2)}) collective-permute-start(f32[1,1,3072]{2,1,0:T(1,128)S(1)} %get-tuple-element.16.refs_0_), channel_id=1, source_target_pairs={{0,24},{8,16},{16,8},{24,0},{1,25},{9,17},{17,9},{25,1},{2,26},{10... | collective-permute-start | bytes 36872 | tf_op jit(solution)/shard_map/ppermute | solution.py:380
  50.0 6.2 %collective-permute-start.15 = (f32[1,6144]{1,0:T(1,128)S(1)}, f32[1,6144]{1,0:T(1,128)S(1)}, u32[]{:S(2)}, u32[]{:S(2)}) collective-permute-start(f32[1,6144]{1,0:T(1,128)S(1)} %compare_select_fusion.refs_0_.refs_4_), channel_id=1, source_target_pairs={{0,2},{1,3},{2,0},{3,1},{4,6},{5,7},{6,4},{7,5},{8,10},{9,11},{10,... | collective-permute-start | bytes 73736 | tf_op jit(solution)/shard_map/ppermute | solution.py:380
  53.0 5.0 %collective-permute-start.16 = (f32[1,6144]{1,0:T(1,128)S(1)}, f32[1,6144]{1,0:T(1,128)S(1)}, u32[]{:S(2)}, u32[]{:S(2)}) collective-permute-start(f32[1,6144]{1,0:T(1,128)S(1)} %compare_select_fusion.refs_0_.refs_4_), channel_id=1, source_target_pairs={{0,4},{1,5},{2,6},{3,7},{4,0},{5,1},{6,2},{7,3},{8,12},{9,13},{10,... | collective-permute-start | bytes 73736 | tf_op jit(solution)/shard_map/ppermute | solution.py:380
  53.1 5.6 %collective-permute-start.17 = (f32[1,6144]{1,0:T(1,128)S(1)}, f32[1,6144]{1,0:T(1,128)S(1)}, u32[]{:S(2)}, u32[]{:S(2)}) collective-permute-start(f32[1,6144]{1,0:T(1,128)S(1)} %compare_select_fusion.refs_0_.refs_4_), channel_id=1, source_target_pairs={{0,6},{1,7},{2,4},{3,5},{4,2},{5,3},{6,0},{7,1},{8,14},{9,15},{10,... | collective-permute-start | bytes 73736 | tf_op jit(solution)/shard_map/ppermute | solution.py:380
  70.3 6.4 %collective-permute-start.18 = (f32[1,1,6144]{2,1,0:T(1,128)S(1)}, f32[1,1,6144]{2,1,0:T(1,128)S(1)}, u32[]{:S(2)}, u32[]{:S(2)}) collective-permute-start(f32[1,1,6144]{2,1,0:T(1,128)S(1)} %get-tuple-element.23), channel_id=1, source_target_pairs={{0,8},{8,0},{16,24},{24,16},{1,9},{9,1},{17,25},{25,17},{2,10},{10... | collective-permute-start | bytes 73736 | tf_op jit(solution)/shard_map/ppermute | solution.py:380
  70.3 6.4 %collective-permute-start.19 = (f32[1,1,6144]{2,1,0:T(1,128)S(1)}, f32[1,1,6144]{2,1,0:T(1,128)S(1)}, u32[]{:S(2)}, u32[]{:S(2)}) collective-permute-start(f32[1,1,6144]{2,1,0:T(1,128)S(1)} %get-tuple-element.23), channel_id=1, source_target_pairs={{0,16},{8,24},{16,0},{24,8},{1,17},{9,25},{17,1},{25,9},{2,18},{10... | collective-permute-start | bytes 73736 | tf_op jit(solution)/shard_map/ppermute | solution.py:380
  71.8 4.9 %collective-permute-start.20 = (f32[1,1,6144]{2,1,0:T(1,128)S(1)}, f32[1,1,6144]{2,1,0:T(1,128)S(1)}, u32[]{:S(2)}, u32[]{:S(2)}) collective-permute-start(f32[1,1,6144]{2,1,0:T(1,128)S(1)} %get-tuple-element.23), channel_id=1, source_target_pairs={{0,24},{8,16},{16,8},{24,0},{1,25},{9,17},{17,9},{25,1},{2,26},{10... | collective-permute-start | bytes 73736 | tf_op jit(solution)/shard_map/ppermute | solution.py:380
  72.2 12.1 %all-to-all-start = ((f32[8,1,4352]{2,1,0:T(1,128)}), f32[8,1,4352]{2,1,0:T(1,128)S(1)}, u32[]{:S(2)}, u32[]{:S(2)}) async-start(f32[8,1,4352]{2,1,0:T(1,128)} %get-tuple-element.21), calls=%async_computation | async-start | bytes 278528 | tf_op jit(solution)/shard_map/all_to_all | solution.py:396

commit v6 on v5

--- a/solution.py
+++ b/solution.py
@@ -25,16 +25,22 @@
     return hi, mid, rest - mid
 
 
-def operand(desc, weight, scale, own):
+def bias_of(desc, weight):
     wide = desc.astype(jnp.float32)
-    desc = desc.astype(jnp.bfloat16)
-    bias = weight - 2.0 * jnp.sum(wide * wide, axis=0, keepdims=True)
+    return weight - 2.0 * jnp.sum(wide * wide, axis=0, keepdims=True)
+
+
+def extra_rows(bias, own):
     hi, mid, lo = split3(bias)
-    row = lax.broadcasted_iota(jnp.int32, (EXTRA, wide.shape[1]), 0) - own
+    row = lax.broadcasted_iota(jnp.int32, (EXTRA, bias.shape[1]), 0) - own
     other = jnp.where((row + own >= 3 - own) & (row + own < 6 - own), 1.0, 0.0)
     extra = jnp.where(row == 0, hi, jnp.where(row == 1, mid, jnp.where(row == 2, lo, other)))
-    main = desc if scale == 1.0 else (scale * wide).astype(jnp.bfloat16)
-    return jnp.concatenate([main, extra.astype(jnp.bfloat16)], axis=0)
+    return extra.astype(jnp.bfloat16)
+
+
+def operand(desc, weight, scale, own):
+    main = (scale * desc.astype(jnp.float32)).astype(jnp.bfloat16)
+    return jnp.concatenate([main, extra_rows(bias_of(desc, weight), own)], axis=0)
 
 
 def scores(lhs, rhs):
@@ -89,13 +95,17 @@
     return top + jnp.log(tree([jnp.exp(part - top) for part in parts], jnp.add))
 
 
-def start_cross(s, z, rhs, ctop, csum):
+def start_cross(s, z, rhs, low, bias, fbuf, ctop, csum):
+    ch = s.shape[0]
     rhs[...] = operand(s, z, 4.0, 0)
+    low[0:ch, :] = rhs[0:ch, :]
+    bias[...] = bias_of(s, z)
     ctop[...] = jnp.full(ctop.shape, -jnp.inf, jnp.float32)
     csum[...] = jnp.zeros(csum.shape, jnp.float32)
 
 
-def cross_block(t, w, rhs, fbuf, ctop, csum):
+def cross_block(t, w, rhs, low, bias, fbuf, ctop, csum):
+    ch = t.shape[0]
     n = rhs.shape[1]
     bt = t.shape[1]
     lhs = operand(t, w, 1.0, 3)
@@ -110,14 +120,15 @@
         new = jnp.maximum(old, top)
         csum[:, k : k + STRIP] = csum[:, k : k + STRIP] * jnp.exp(old - new)
         ctop[:, k : k + STRIP] = new
+        low[ch:, k : k + STRIP] = extra_rows(bias[:, k : k + STRIP] - new[0:1, :], 0)
     r1 = jnp.max(rmax, axis=1, keepdims=True)
     r = jnp.broadcast_to(r1, (bt, 128))
     racc = jnp.zeros((bt, 128), jnp.float32)
-    for h in range(0, n, 128):
-        f = fbuf[:, h : h + 128]
-        racc = racc + jnp.exp(f - r)
-        e2 = jnp.exp(f - ctop[0:1, h : h + 128])
-        csum[:, h : h + 128] = csum[:, h : h + 128] + fold_rows(e2, jnp.add)
+    for k in range(0, n, STRIP):
+        e2 = jnp.exp(scores(lhs, low[:, k : k + STRIP]))
+        csum[:, k : k + STRIP] = csum[:, k : k + STRIP] + fold_rows(e2, jnp.add)
+        for h in range(k, k + STRIP, 128):
+            racc = racc + jnp.exp(fbuf[:, h : h + 128] - r)
     total = jnp.sum(racc, axis=1, keepdims=True)
     return to_lanes(jnp.broadcast_to(r1 + jnp.log(total), (bt, 128)))
 
@@ -140,11 +151,11 @@
 
 
 def cross_kernel(turn, t_ref, w_ref, s_ref, z_ref, row_ref, col_ref, *scratch):
-    rhs, _, ctop, csum = scratch
+    ctop, csum = scratch[-2:]
 
     @pl.when(pl.program_id(0) == 0)
     def _():
-        start_cross(s_ref[...], log_of(z_ref[...]), rhs, ctop, csum)
+        start_cross(s_ref[...], log_of(z_ref[...]), *scratch)
 
     row_ref[...] = cross_block(swapped(turn, t_ref), log_of(w_ref[...]), *scratch)
 
@@ -156,6 +167,8 @@
 def cross_scratch(ch, bt, n):
     return [
         pltpu.VMEM((ch + EXTRA, n), jnp.bfloat16),
+        pltpu.VMEM((ch + EXTRA, n), jnp.bfloat16),
+        pltpu.VMEM((1, n), jnp.float32),
         pltpu.VMEM((bt, n), jnp.float32),
         pltpu.VMEM((8, n), jnp.float32),
         pltpu.VMEM((8, n), jnp.float32),
@@ -199,7 +212,7 @@
     parts, cols = refs[:count], refs[count : count + width]
     row_ref, w_ref, z_ref, col_ref = refs[count + width : count + width + 4]
     scratch = refs[count + width + 4 :]
-    rhs, _, ctop, csum = scratch
+    ctop, csum = scratch[-2:]
     n = s_ref.shape[1]
 
     @pl.when(pl.program_id(0) == 0)
@@ -207,7 +220,7 @@
         log_mass = log_of(sm_ref[...])
         z = damped(log_mass, log_sum([part[:, 0:n] for part in cols]))
         z_ref[...] = kept(log_mass, z)
-        start_cross(s_ref[...], z, rhs, ctop, csum)
+        start_cross(s_ref[...], z, *scratch)
 
     log_mass = log_of(tm_ref[...])
     w = damped(log_mass, log_sum([part[0] for part in parts]))
@@ -408,7 +421,8 @@
     half = DAMPING * EPSILON * 0.5
 
     target_lanes = target_desc.T
-    target_blocks = target_lanes.reshape(cols, -1, nt)
+    target_blocks = jnp.where(col < cols, target_lanes.reshape(cols, -1, nt), 0)
+    target_blocks = lax.optimization_barrier(target_blocks)
     source_lanes = gather(source_desc.T, "col").reshape(-1, ns)
     piece = jnp.concatenate([target_lanes, target_mass[None]], axis=0)
     piece = lax.dynamic_slice_in_dim(piece, row * pt, pt, 1)
@@ -423,7 +437,8 @@
     spot = jnp.stack([col, row]).astype(jnp.int32)
 
     ct, cs = cross_tile(turn, target_blocks, target_mass, source_lanes, source_mass)
-    sums, target_plan = self_tile(target_set, target_lanes, target_mass, turn, cs, 1)
+    sums, target_plan = self_tile(
+        target_set, target_blocks.reshape(-1, nt), target_mass, turn, cs, 1)
     sums = sums[0]
     other = lax.ppermute(sums, "col", [(i, i ^ 1) for i in range(cols)])
     logs = lax.broadcasted_iota(jnp.int32, sums.shape, 1) < ns

time: 85.5 us -> 83.8 us (0.980)
  local copies, waits for them, and re-layouts: 3.21 us -> 2.23 us
  other arithmetic: 3.25 us -> 4.22 us
    unnamed x11 -> x7, local copies, waits for them, and re-layouts: 1.8 us -> 0.81 us
    select_n x0 -> x1, other arithmetic: none -> 0.97 us  [body(): target_blocks = jnp.where(col < cols, target_lanes.reshape(cols, -1, nt), 0)]
    ppermute x8, waiting for transfers between devices: 11.5 us -> 10.6 us  [send(): return lax.ppermute(x, axis, [(i, i ^ step) for i in range(count)])]
  transfers between devices with their start and end apart: 22 -> 22, of which waited for: 6 -> 6; matrix products, arithmetic and copies ran while one was open for 4% -> 5% of each run, Pallas kernels for 12% -> 12%
where the time goes in v6:
time: 83.8 us; the launch traced here: 83.3 us
  starting transfers between devices  29.2 us (35%)
  Pallas kernels  26.8 us (32%)
  waiting for transfers between devices  20 us (24%)
  other arithmetic  4.22 us (5%)
  local copies, waits for them, and re-layouts  2.23 us (3%)
  between operations  0.85 us (1%)
    ppermute x8, starting transfers between devices, send(): return lax.ppermute(x, axis, [(i, i ^ step) for i in range(count)])  13.1 us
    ppermute x12, starting transfers between devices, collect(): lax.ppermute(x, axis, [(i, i ^ k) for i in range(count)])  11.1 us
    ppermute x8, waiting for transfers between devices, send(): return lax.ppermute(x, axis, [(i, i ^ step) for i in range(count)])  10.6 us
    pallas_call x1, Pallas kernels, cross_again(): pl.pallas_call(functools.partial(cross_again_kernel, len(by_row), len(by_...  8.18 us
    pallas_call x1, Pallas kernels, cross_tile(): pl.pallas_call(cross_kernel, grid_spec=pltpu.PrefetchScalarGridSpec(num_s...  7.5 us
    pallas_call x2, Pallas kernels, self_tile(): pl.pallas_call(self_kernel, grid_spec=pltpu.PrefetchScalarGridSpec(num_sc...  7.33 us
    all_to_all x1, waiting for transfers between devices, swap(): return lax.all_to_all(x, axis, 0, 0)  6.82 us
    all_to_all x1, starting transfers between devices, swap(): return lax.all_to_all(x, axis, 0, 0)  4.37 us
  transfers between devices with their start and end apart: 22, of which 6 were waited for; matrix products, arithmetic and copies ran while one was open for 5% of the time, Pallas kernels for 12%

profile of v6, /device:TPU:0, one launch (start us, length us, event | category | flops | bytes accessed | tf_op | source)
XLA Modules:
  0.0 83.3 jit_solution(220685117986835540)
XLA Ops:
  0.6 0.7 broadcast_in_dim.19.w_ref.z_ref.tm_ref
  1.3 0.8 %constant_dynamic-update-slice_fusion.9 = (bf16[8,65,512]{2,1,0:T(8,128)(2,1)S(1)}, bf16[65,512]{1,0:T(8,128)(2,1)S(1)}) fusion(s32[]{:T(128)S(6)} %select_n.25, bf16[1,2048]{1,0:T(2,128)(2,1)S(1)} %broadcast_in_dim.19.w_ref.z_ref.tm_ref, bf16[64,2048]{1,0:T(8,128)(2,1)} %bitcast.62), kind=kLoop, calls=%fused_computation.22 | loop fusion | flops 133119 | bytes 413700
  2.2 3.0 %collective-permute-start.10 = (bf16[65,512]{1,0:T(8,128)(2,1)S(1)}, bf16[65,512]{1,0:T(8,128)(2,1)S(1)}, u32[]{:S(2)}, u32[]{:S(2)}) collective-permute-start(bf16[65,512]{1,0:T(8,128)(2,1)S(1)} %get-tuple-element.25), channel_id=1, source_target_pairs={{0,1},{1,0},{2,3},{3,2},{4,5},{5,4},{6,7},{7,6},{8,9},{9,8},{10,11... | collective-permute-start | bytes 199688 | tf_op jit(solution)/shard_map/ppermute | solution.py:399
  5.3 1.0 %select_bitcast_fusion.t_ref = bf16[8,8,2048]{2,1,0:T(8,128)(2,1)S(1)} fusion(pred[]{:T(512)S(6)} %lt.23, bf16[2048,64]{0,1:T(8,128)(2,1)} %param.5), kind=kLoop, calls=%fused_computation.4 | loop fusion | flops 131072 | bytes 524289 | tf_op jit(solution)/shard_map/jit(_where)/select_n | solution.py:424
  6.3 0.8 constant_dynamic-update-slice_fusion.4
  7.0 0.7 broadcast_in_dim.20.z_ref.sm_ref
  7.7 1.6 %collective-permute-done = bf16[8,2048]{1,0:T(8,128)(2,1)S(1)} collective-permute-done((bf16[8,2048]{1,0:T(8,128)(2,1)}, bf16[8,2048]{1,0:T(8,128)(2,1)S(1)}, u32[]{:S(2)}, u32[]{:S(2)}) %collective-permute-start) | collective-permute-done | bytes 32800 | tf_op jit(solution)/shard_map/ppermute | solution.py:399
  9.3 0.8 pad_maximum_fusion.2
  10.1 1.6 %collective-permute-start.1 = (bf16[2,8,2048]{2,1,0:T(8,128)(2,1)S(1)}, bf16[2,8,2048]{2,1,0:T(8,128)(2,1)S(1)}, u32[]{:S(2)}, u32[]{:S(2)}) collective-permute-start(bf16[2,8,2048]{2,1,0:T(8,128)(2,1)S(1)} %pad_maximum_fusion.2), channel_id=1, source_target_pairs={{0,2},{1,3},{2,0},{3,1},{4,6},{5,7},{6,4},{7,5},{8,10},{9,11},{10,... | collective-permute-start | bytes 196616 | tf_op jit(solution)/shard_map/ppermute | solution.py:399
  11.7 2.6 %collective-permute-start.2 = (bf16[2,8,2048]{2,1,0:T(8,128)(2,1)S(1)}, bf16[2,8,2048]{2,1,0:T(8,128)(2,1)S(1)}, u32[]{:S(2)}, u32[]{:S(2)}) collective-permute-start(bf16[2,8,2048]{2,1,0:T(8,128)(2,1)S(1)} %pad_maximum_fusion.2), channel_id=1, source_target_pairs={{0,4},{1,5},{2,6},{3,7},{4,0},{5,1},{6,2},{7,3},{8,12},{9,13},{10,... | collective-permute-start | bytes 196616 | tf_op jit(solution)/shard_map/ppermute | solution.py:399
  14.5 0.7 collective-permute-start.11
  15.3 3.5 %collective-permute-start.12 = (bf16[2,65,512]{2,1,0:T(8,128)(2,1)S(1)}, bf16[2,65,512]{2,1,0:T(8,128)(2,1)S(1)}, u32[]{:S(2)}, u32[]{:S(2)}) collective-permute-start(bf16[2,65,512]{2,1,0:T(8,128)(2,1)S(1)} %pad_maximum_fusion.1), channel_id=1, source_target_pairs={{0,4},{1,5},{2,6},{3,7},{4,0},{5,1},{6,2},{7,3},{8,12},{9,13},{10,... | collective-permute-start | bytes 399368 | tf_op jit(solution)/shard_map/ppermute | solution.py:399
  18.8 2.3 %collective-permute-done.3 = bf16[2,8,2048]{2,1,0:T(8,128)(2,1)S(1)} collective-permute-done((bf16[2,8,2048]{2,1,0:T(8,128)(2,1)S(1)}, bf16[2,8,2048]{2,1,0:T(8,128)(2,1)S(1)}, u32[]{:S(2)}, u32[]{:S(2)}) %collective-permute-start.3) | collective-permute-done | bytes 65568 | tf_op jit(solution)/shard_map/ppermute | solution.py:399
  21.2 1.6 %collective-permute-start.5 = (bf16[65,256]{1,0:T(8,128)(2,1)S(1)}, bf16[65,256]{1,0:T(8,128)(2,1)S(1)}, u32[]{:S(2)}, u32[]{:S(2)}) collective-permute-start(bf16[65,256]{1,0:T(8,128)(2,1)S(1)} %fusion.1), channel_id=1, source_target_pairs={{0,16},{8,24},{16,0},{24,8},{1,17},{9,25},{17,1},{25,9},{2,18},{10... | collective-permute-start | bytes 99848 | tf_op jit(solution)/shard_map/ppermute | solution.py:393
  23.1 7.5 %cross_tile.1 = (f32[1,2048]{1,0:T(1,128)S(1)}, f32[1,2048]{1,0:T(1,128)S(1)}) custom-call(s32[1]{0:T(128)} %bitcast.turn.flip, bf16[8,8,2048]{2,1,0:T(8,128)(2,1)S(1)} %select_bitcast_fusion.t_ref, bf16[1,2048]{1,0:T(2,128)(2,1)S(1)} %broadcast_in_dim.19.w_ref.z_ref.tm_ref, bf16[64,2048]{1,0:T(8,128)(2,1)S(1)} %bitcast.53, ...), custom_call_target="tpu_custom_call" | custom-call | flops 2147483648 | bytes 1048576 | tf_op jit(solution)/shard_map/cross_tile/pallas_call | solution.py:190
  30.6 1.4 %collective-permute-start.13 = (bf16[2,65,512]{2,1,0:T(8,128)(2,1)S(1)}, bf16[2,65,512]{2,1,0:T(8,128)(2,1)S(1)}, u32[]{:S(2)}, u32[]{:S(2)}) collective-permute-start(bf16[2,65,512]{2,1,0:T(8,128)(2,1)S(1)} %pad_maximum_fusion.1), channel_id=1, source_target_pairs={{0,6},{1,7},{2,4},{3,5},{4,2},{5,3},{6,0},{7,1},{8,14},{9,15},{10,... | collective-permute-start | bytes 399368 | tf_op jit(solution)/shard_map/ppermute | solution.py:399
  32.1 6.6 %collective-permute-done.13 = bf16[2,65,512]{2,1,0:T(8,128)(2,1)S(1)} collective-permute-done((bf16[2,65,512]{2,1,0:T(8,128)(2,1)S(1)}, bf16[2,65,512]{2,1,0:T(8,128)(2,1)S(1)}, u32[]{:S(2)}, u32[]{:S(2)}) %collective-permute-start.13) | collective-permute-done | bytes 133152 | tf_op jit(solution)/shard_map/ppermute | solution.py:399
  38.7 5.9 %self_tile.3 = (f32[1,1,6144]{2,1,0:T(1,128)S(1)}, bf16[4096,2048]{1,0:T(8,128)(2,1)S(1)}) custom-call(s32[1]{0:T(128)} %bitcast.turn.flip, bf16[8,65,512]{2,1,0:T(8,128)(2,1)S(1)} %constant_dynamic-update-slice_fusion.5.u_ref, bf16[64,2048]{1,0:T(8,128)(2,1)S(1)} %bitcast.57, bf16[1,2048]{1,0:T(2,128)(2,1)S(1)} %broadcast_in_dim.19.w_ref.z_ref.tm_ref, ...), custom_call_target="tpu_custom_call" | custom-call | flops 2181038080 | bytes 266240 | tf_op jit(solution)/shard_map/self_tile/pallas_call | solution.py:322
  45.2 1.5 %self_tile.2 = (f32[1,1,3072]{2,1,0:T(1,128)S(1)}, bf16[1024,2048]{1,0:T(8,128)(2,1)S(1)}) custom-call(s32[1]{0:T(128)} %bitcast.8.flip, bf16[4,65,256]{2,1,0:T(8,128)(2,1)S(1)} %pad_maximum_fusion.u_ref, bf16[64,2048]{1,0:T(8,128)(2,1)S(1)} %bitcast.55, bf16[1,2048]{1,0:T(2,128)(2,1)S(1)} %broadcast_in_dim.20.z_ref.sm_ref, ...), custom_call_target="tpu_custom_call" | custom-call | flops 545259520 | bytes 66560 | tf_op jit(solution)/shard_map/self_tile/pallas_call | solution.py:322
  46.8 1.6 %collective-permute-start.8 = (f32[1,1,3072]{2,1,0:T(1,128)S(1)}, f32[1,1,3072]{2,1,0:T(1,128)S(1)}, u32[]{:S(2)}, u32[]{:S(2)}) collective-permute-start(f32[1,1,3072]{2,1,0:T(1,128)S(1)} %get-tuple-element.16.refs_0_), channel_id=1, source_target_pairs={{0,16},{8,24},{16,0},{24,8},{1,17},{9,25},{17,1},{25,9},{2,18},{10... | collective-permute-start | bytes 36872 | tf_op jit(solution)/shard_map/ppermute | solution.py:393
  48.7 3.0 %collective-permute-start.15 = (f32[1,6144]{1,0:T(1,128)S(1)}, f32[1,6144]{1,0:T(1,128)S(1)}, u32[]{:S(2)}, u32[]{:S(2)}) collective-permute-start(f32[1,6144]{1,0:T(1,128)S(1)} %compare_select_fusion.refs_0_.refs_4_), channel_id=1, source_target_pairs={{0,2},{1,3},{2,0},{3,1},{4,6},{5,7},{6,4},{7,5},{8,10},{9,11},{10,... | collective-permute-start | bytes 73736 | tf_op jit(solution)/shard_map/ppermute | solution.py:393
  51.9 2.2 %collective-permute-start.17 = (f32[1,6144]{1,0:T(1,128)S(1)}, f32[1,6144]{1,0:T(1,128)S(1)}, u32[]{:S(2)}, u32[]{:S(2)}) collective-permute-start(f32[1,6144]{1,0:T(1,128)S(1)} %compare_select_fusion.refs_0_.refs_4_), channel_id=1, source_target_pairs={{0,6},{1,7},{2,4},{3,5},{4,2},{5,3},{6,0},{7,1},{8,14},{9,15},{10,... | collective-permute-start | bytes 73736 | tf_op jit(solution)/shard_map/ppermute | solution.py:393
  54.2 0.7 again_tile.2
  54.9 1.8 %collective-permute-done.16.refs_2_.refs_6_ = f32[1,6144]{1,0:T(1,128)S(1)} collective-permute-done((f32[1,6144]{1,0:T(1,128)S(1)}, f32[1,6144]{1,0:T(1,128)S(1)}, u32[]{:S(2)}, u32[]{:S(2)}) %collective-permute-start.16) | collective-permute-done | bytes 24608 | tf_op jit(solution)/shard_map/ppermute | solution.py:393
  56.7 0.8 collective-permute-done.17.refs_3_.refs_7_
  57.5 3.1 %again_tile.3 = f32[1,1,4096]{2,1,0:T(1,128)S(1)} custom-call(s32[2]{0:T(128)S(1)} %pad_add_fusion.flip, bf16[8,65,512]{2,1,0:T(8,128)(2,1)S(1)} %constant_dynamic-update-slice_fusion.5.u_ref, bf16[1,2048]{1,0:T(2,128)(2,1)S(1)} %broadcast_in_dim.19.w_ref.z_ref.tm_ref, bf16[4096,2048]{1,0:T(8,128)(2,1)S(1)} %get-tuple-element.18.plan_ref, ...), custom_call_target="tpu_custom_call" | custom-call | flops 268435456 | bytes 16777216 | tf_op jit(solution)/shard_map/again_tile/pallas_call | solution.py:379
  60.6 8.2 %cross_again.1 = (f32[1,1,6144]{2,1,0:T(1,128)S(1)}, f32[1,2048]{1,0:T(1,128)S(1)}, f32[1,2048]{1,0:T(1,128)S(1)}, f32[8,1,4352]{2,1,0:T(1,128)}) custom-call(s32[1]{0:T(128)} %bitcast.turn.flip, bf16[8,8,2048]{2,1,0:T(8,128)(2,1)S(1)} %select_bitcast_fusion.t_ref, bf16[1,2048]{1,0:T(2,128)(2,1)S(1)} %broadcast_in_dim.19.w_ref.z_ref.tm_ref, ...), custom_call_target="tpu_custom_call" | custom-call | flops 2147483648 | bytes 1048576 | tf_op jit(solution)/shard_map/cross_again/pallas_call | solution.py:249
  68.8 1.5 %collective-permute-start.19 = (f32[1,1,6144]{2,1,0:T(1,128)S(1)}, f32[1,1,6144]{2,1,0:T(1,128)S(1)}, u32[]{:S(2)}, u32[]{:S(2)}) collective-permute-start(f32[1,1,6144]{2,1,0:T(1,128)S(1)} %get-tuple-element.23), channel_id=1, source_target_pairs={{0,16},{8,24},{16,0},{24,8},{1,17},{9,25},{17,1},{25,9},{2,18},{10... | collective-permute-start | bytes 73736 | tf_op jit(solution)/shard_map/ppermute | solution.py:393
  70.6 4.4 %all-to-all-start = ((f32[8,1,4352]{2,1,0:T(1,128)}), f32[8,1,4352]{2,1,0:T(1,128)S(1)}, u32[]{:S(2)}, u32[]{:S(2)}) async-start(f32[8,1,4352]{2,1,0:T(1,128)} %get-tuple-element.21), calls=%async_computation | async-start | bytes 278528 | tf_op jit(solution)/shard_map/all_to_all | solution.py:409
  75.0 0.7 multiply_subtract_fusion
  75.7 6.8 %all-to-all-done = f32[8,1,4352]{2,1,0:T(1,128)S(1)} async-done(((f32[8,1,4352]{2,1,0:T(1,128)}), f32[8,1,4352]{2,1,0:T(1,128)S(1)}, u32[]{:S(2)}, u32[]{:S(2)}) %all-to-all-start) | async-done | bytes 139296 | tf_op jit(solution)/shard_map/all_to_all | solution.py:409
  82.6 0.7 multiply_subtract_fusion.1
  (43 shorter events, 2.4 us)
Async XLA Ops:
  2.2 12.3 %collective-permute-start.10 = (bf16[65,512]{1,0:T(8,128)(2,1)S(1)}, bf16[65,512]{1,0:T(8,128)(2,1)S(1)}, u32[]{:S(2)}, u32[]{:S(2)}) collective-permute-start(bf16[65,512]{1,0:T(8,128)(2,1)S(1)} %get-tuple-element.25), channel_id=1, source_target_pairs={{0,1},{1,0},{2,3},{3,2},{4,5},{5,4},{6,7},{7,6},{8,9},{9,8},{10,11... | collective-permute-start | bytes 199688 | tf_op jit(solution)/shard_map/ppermute | solution.py:399
  5.2 4.1 %collective-permute-start = (bf16[8,2048]{1,0:T(8,128)(2,1)}, bf16[8,2048]{1,0:T(8,128)(2,1)S(1)}, u32[]{:S(2)}, u32[]{:S(2)}) collective-permute-start(bf16[8,2048]{1,0:T(8,128)(2,1)} %bitcast.65), channel_id=1, source_target_pairs={{0,1},{1,0},{2,3},{3,2},{4,5},{5,4},{6,7},{7,6},{8,9},{9,8},{10,11... | collective-permute-start | bytes 98312 | tf_op jit(solution)/shard_map/ppermute | solution.py:399
  10.1 8.7 %collective-permute-start.1 = (bf16[2,8,2048]{2,1,0:T(8,128)(2,1)S(1)}, bf16[2,8,2048]{2,1,0:T(8,128)(2,1)S(1)}, u32[]{:S(2)}, u32[]{:S(2)}) collective-permute-start(bf16[2,8,2048]{2,1,0:T(8,128)(2,1)S(1)} %pad_maximum_fusion.2), channel_id=1, source_target_pairs={{0,2},{1,3},{2,0},{3,1},{4,6},{5,7},{6,4},{7,5},{8,10},{9,11},{10,... | collective-permute-start | bytes 196616 | tf_op jit(solution)/shard_map/ppermute | solution.py:399
  11.7 7.1 %collective-permute-start.2 = (bf16[2,8,2048]{2,1,0:T(8,128)(2,1)S(1)}, bf16[2,8,2048]{2,1,0:T(8,128)(2,1)S(1)}, u32[]{:S(2)}, u32[]{:S(2)}) collective-permute-start(bf16[2,8,2048]{2,1,0:T(8,128)(2,1)S(1)} %pad_maximum_fusion.2), channel_id=1, source_target_pairs={{0,4},{1,5},{2,6},{3,7},{4,0},{5,1},{6,2},{7,3},{8,12},{9,13},{10,... | collective-permute-start | bytes 196616 | tf_op jit(solution)/shard_map/ppermute | solution.py:399
  14.3 6.9 %collective-permute-start.3 = (bf16[2,8,2048]{2,1,0:T(8,128)(2,1)S(1)}, bf16[2,8,2048]{2,1,0:T(8,128)(2,1)S(1)}, u32[]{:S(2)}, u32[]{:S(2)}) collective-permute-start(bf16[2,8,2048]{2,1,0:T(8,128)(2,1)S(1)} %pad_maximum_fusion.2), channel_id=1, source_target_pairs={{0,6},{1,7},{2,4},{3,5},{4,2},{5,3},{6,0},{7,1},{8,14},{9,15},{10,... | collective-permute-start | bytes 196616 | tf_op jit(solution)/shard_map/ppermute | solution.py:399
  14.5 17.5 %collective-permute-start.11 = (bf16[2,65,512]{2,1,0:T(8,128)(2,1)S(1)}, bf16[2,65,512]{2,1,0:T(8,128)(2,1)S(1)}, u32[]{:S(2)}, u32[]{:S(2)}) collective-permute-start(bf16[2,65,512]{2,1,0:T(8,128)(2,1)S(1)} %pad_maximum_fusion.1), channel_id=1, source_target_pairs={{0,2},{1,3},{2,0},{3,1},{4,6},{5,7},{6,4},{7,5},{8,10},{9,11},{10,... | collective-permute-start | bytes 399368 | tf_op jit(solution)/shard_map/ppermute | solution.py:399
  15.3 16.8 %collective-permute-start.12 = (bf16[2,65,512]{2,1,0:T(8,128)(2,1)S(1)}, bf16[2,65,512]{2,1,0:T(8,128)(2,1)S(1)}, u32[]{:S(2)}, u32[]{:S(2)}) collective-permute-start(bf16[2,65,512]{2,1,0:T(8,128)(2,1)S(1)} %pad_maximum_fusion.1), channel_id=1, source_target_pairs={{0,4},{1,5},{2,6},{3,7},{4,0},{5,1},{6,2},{7,3},{8,12},{9,13},{10,... | collective-permute-start | bytes 399368 | tf_op jit(solution)/shard_map/ppermute | solution.py:399
  21.2 9.5 %collective-permute-start.4 = (bf16[65,256]{1,0:T(8,128)(2,1)S(1)}, bf16[65,256]{1,0:T(8,128)(2,1)S(1)}, u32[]{:S(2)}, u32[]{:S(2)}) collective-permute-start(bf16[65,256]{1,0:T(8,128)(2,1)S(1)} %fusion.1), channel_id=1, source_target_pairs={{0,8},{8,0},{16,24},{24,16},{1,9},{9,1},{17,25},{25,17},{2,10},{10... | collective-permute-start | bytes 99848 | tf_op jit(solution)/shard_map/ppermute | solution.py:393
  21.2 10.7 %collective-permute-start.5 = (bf16[65,256]{1,0:T(8,128)(2,1)S(1)}, bf16[65,256]{1,0:T(8,128)(2,1)S(1)}, u32[]{:S(2)}, u32[]{:S(2)}) collective-permute-start(bf16[65,256]{1,0:T(8,128)(2,1)S(1)} %fusion.1), channel_id=1, source_target_pairs={{0,16},{8,24},{16,0},{24,8},{1,17},{9,25},{17,1},{25,9},{2,18},{10... | collective-permute-start | bytes 99848 | tf_op jit(solution)/shard_map/ppermute | solution.py:393
  22.8 9.2 %collective-permute-start.6 = (bf16[65,256]{1,0:T(8,128)(2,1)S(1)}, bf16[65,256]{1,0:T(8,128)(2,1)S(1)}, u32[]{:S(2)}, u32[]{:S(2)}) collective-permute-start(bf16[65,256]{1,0:T(8,128)(2,1)S(1)} %fusion.1), channel_id=1, source_target_pairs={{0,24},{8,16},{16,8},{24,0},{1,25},{9,17},{17,9},{25,1},{2,26},{10... | collective-permute-start | bytes 99848 | tf_op jit(solution)/shard_map/ppermute | solution.py:393
  30.6 8.1 %collective-permute-start.13 = (bf16[2,65,512]{2,1,0:T(8,128)(2,1)S(1)}, bf16[2,65,512]{2,1,0:T(8,128)(2,1)S(1)}, u32[]{:S(2)}, u32[]{:S(2)}) collective-permute-start(bf16[2,65,512]{2,1,0:T(8,128)(2,1)S(1)} %pad_maximum_fusion.1), channel_id=1, source_target_pairs={{0,6},{1,7},{2,4},{3,5},{4,2},{5,3},{6,0},{7,1},{8,14},{9,15},{10,... | collective-permute-start | bytes 399368 | tf_op jit(solution)/shard_map/ppermute | solution.py:399
  44.6 4.0 %collective-permute-start.14 = (f32[1,6144]{1,0:T(1,128)S(1)}, f32[1,6144]{1,0:T(1,128)S(1)}, u32[]{:S(2)}, u32[]{:S(2)}) collective-permute-start(f32[1,6144]{1,0:T(1,128)S(1)} %bitcast.58), channel_id=1, source_target_pairs={{0,1},{1,0},{2,3},{3,2},{4,5},{5,4},{6,7},{7,6},{8,9},{9,8},{10,11... | collective-permute-start | bytes 73736 | tf_op jit(solution)/shard_map/ppermute | solution.py:443
  46.7 5.2 %collective-permute-start.7 = (f32[1,1,3072]{2,1,0:T(1,128)S(1)}, f32[1,1,3072]{2,1,0:T(1,128)S(1)}, u32[]{:S(2)}, u32[]{:S(2)}) collective-permute-start(f32[1,1,3072]{2,1,0:T(1,128)S(1)} %get-tuple-element.16.refs_0_), channel_id=1, source_target_pairs={{0,8},{8,0},{16,24},{24,16},{1,9},{9,1},{17,25},{25,17},{2,10},{10... | collective-permute-start | bytes 36872 | tf_op jit(solution)/shard_map/ppermute | solution.py:393
  46.8 7.4 %collective-permute-start.8 = (f32[1,1,3072]{2,1,0:T(1,128)S(1)}, f32[1,1,3072]{2,1,0:T(1,128)S(1)}, u32[]{:S(2)}, u32[]{:S(2)}) collective-permute-start(f32[1,1,3072]{2,1,0:T(1,128)S(1)} %get-tuple-element.16.refs_0_), channel_id=1, source_target_pairs={{0,16},{8,24},{16,0},{24,8},{1,17},{9,25},{17,1},{25,9},{2,18},{10... | collective-permute-start | bytes 36872 | tf_op jit(solution)/shard_map/ppermute | solution.py:393
  48.3 5.8 %collective-permute-start.9 = (f32[1,1,3072]{2,1,0:T(1,128)S(1)}, f32[1,1,3072]{2,1,0:T(1,128)S(1)}, u32[]{:S(2)}, u32[]{:S(2)}) collective-permute-start(f32[1,1,3072]{2,1,0:T(1,128)S(1)} %get-tuple-element.16.refs_0_), channel_id=1, source_target_pairs={{0,24},{8,16},{16,8},{24,0},{1,25},{9,17},{17,9},{25,1},{2,26},{10... | collective-permute-start | bytes 36872 | tf_op jit(solution)/shard_map/ppermute | solution.py:393
  48.7 6.2 %collective-permute-start.15 = (f32[1,6144]{1,0:T(1,128)S(1)}, f32[1,6144]{1,0:T(1,128)S(1)}, u32[]{:S(2)}, u32[]{:S(2)}) collective-permute-start(f32[1,6144]{1,0:T(1,128)S(1)} %compare_select_fusion.refs_0_.refs_4_), channel_id=1, source_target_pairs={{0,2},{1,3},{2,0},{3,1},{4,6},{5,7},{6,4},{7,5},{8,10},{9,11},{10,... | collective-permute-start | bytes 73736 | tf_op jit(solution)/shard_map/ppermute | solution.py:393
  51.7 5.0 %collective-permute-start.16 = (f32[1,6144]{1,0:T(1,128)S(1)}, f32[1,6144]{1,0:T(1,128)S(1)}, u32[]{:S(2)}, u32[]{:S(2)}) collective-permute-start(f32[1,6144]{1,0:T(1,128)S(1)} %compare_select_fusion.refs_0_.refs_4_), channel_id=1, source_target_pairs={{0,4},{1,5},{2,6},{3,7},{4,0},{5,1},{6,2},{7,3},{8,12},{9,13},{10,... | collective-permute-start | bytes 73736 | tf_op jit(solution)/shard_map/ppermute | solution.py:393
  51.9 5.6 %collective-permute-start.17 = (f32[1,6144]{1,0:T(1,128)S(1)}, f32[1,6144]{1,0:T(1,128)S(1)}, u32[]{:S(2)}, u32[]{:S(2)}) collective-permute-start(f32[1,6144]{1,0:T(1,128)S(1)} %compare_select_fusion.refs_0_.refs_4_), channel_id=1, source_target_pairs={{0,6},{1,7},{2,4},{3,5},{4,2},{5,3},{6,0},{7,1},{8,14},{9,15},{10,... | collective-permute-start | bytes 73736 | tf_op jit(solution)/shard_map/ppermute | solution.py:393
  68.8 6.2 %collective-permute-start.18 = (f32[1,1,6144]{2,1,0:T(1,128)S(1)}, f32[1,1,6144]{2,1,0:T(1,128)S(1)}, u32[]{:S(2)}, u32[]{:S(2)}) collective-permute-start(f32[1,1,6144]{2,1,0:T(1,128)S(1)} %get-tuple-element.23), channel_id=1, source_target_pairs={{0,8},{8,0},{16,24},{24,16},{1,9},{9,1},{17,25},{25,17},{2,10},{10... | collective-permute-start | bytes 73736 | tf_op jit(solution)/shard_map/ppermute | solution.py:393
  68.8 6.2 %collective-permute-start.19 = (f32[1,1,6144]{2,1,0:T(1,128)S(1)}, f32[1,1,6144]{2,1,0:T(1,128)S(1)}, u32[]{:S(2)}, u32[]{:S(2)}) collective-permute-start(f32[1,1,6144]{2,1,0:T(1,128)S(1)} %get-tuple-element.23), channel_id=1, source_target_pairs={{0,16},{8,24},{16,0},{24,8},{1,17},{9,25},{17,1},{25,9},{2,18},{10... | collective-permute-start | bytes 73736 | tf_op jit(solution)/shard_map/ppermute | solution.py:393
  70.3 4.7 %collective-permute-start.20 = (f32[1,1,6144]{2,1,0:T(1,128)S(1)}, f32[1,1,6144]{2,1,0:T(1,128)S(1)}, u32[]{:S(2)}, u32[]{:S(2)}) collective-permute-start(f32[1,1,6144]{2,1,0:T(1,128)S(1)} %get-tuple-element.23), channel_id=1, source_target_pairs={{0,24},{8,16},{16,8},{24,0},{1,25},{9,17},{17,9},{25,1},{2,26},{10... | collective-permute-start | bytes 73736 | tf_op jit(solution)/shard_map/ppermute | solution.py:393
  70.6 11.9 %all-to-all-start = ((f32[8,1,4352]{2,1,0:T(1,128)}), f32[8,1,4352]{2,1,0:T(1,128)S(1)}, u32[]{:S(2)}, u32[]{:S(2)}) async-start(f32[8,1,4352]{2,1,0:T(1,128)} %get-tuple-element.21), calls=%async_computation | async-start | bytes 278528 | tf_op jit(solution)/shard_map/all_to_all | solution.py:409

commit v7 on v6

--- a/solution.py
+++ b/solution.py
@@ -15,6 +15,8 @@
 STRIP = 256
 EXTRA = 16
 GROUP = 1024
+SUB = 256
+SPAN = 2048
 LIMIT = 16 * 2**20
 
 
@@ -107,30 +109,40 @@
 def cross_block(t, w, rhs, low, bias, fbuf, ctop, csum):
     ch = t.shape[0]
     n = rhs.shape[1]
-    bt = t.shape[1]
-    lhs = operand(t, w, 1.0, 3)
-    rmax = None
-    for k in range(0, n, STRIP):
-        f = scores(lhs, rhs[:, k : k + STRIP])
-        fbuf[:, k : k + STRIP] = f
+    bt = fbuf.shape[1]
+    count = t.shape[1] // bt
+    lhs = [operand(t[:, j : j + bt], w[:, j : j + bt], 1.0, 3) for j in range(0, count * bt, bt)]
+    rmax = [None] * count
+
+    def first_pass(j, k):
+        f = scores(lhs[j], rhs[:, k : k + STRIP])
+        fbuf[j % 2, :, k : k + STRIP] = f
         m = fold_lanes(f, jnp.maximum)
-        rmax = m if rmax is None else jnp.maximum(rmax, m)
+        rmax[j] = m if rmax[j] is None else jnp.maximum(rmax[j], m)
         top = jnp.max(fold_rows(f, jnp.maximum), axis=0, keepdims=True)
         old = ctop[:, k : k + STRIP]
         new = jnp.maximum(old, top)
         csum[:, k : k + STRIP] = csum[:, k : k + STRIP] * jnp.exp(old - new)
         ctop[:, k : k + STRIP] = new
         low[ch:, k : k + STRIP] = extra_rows(bias[:, k : k + STRIP] - new[0:1, :], 0)
-    r1 = jnp.max(rmax, axis=1, keepdims=True)
-    r = jnp.broadcast_to(r1, (bt, 128))
-    racc = jnp.zeros((bt, 128), jnp.float32)
+
     for k in range(0, n, STRIP):
-        e2 = jnp.exp(scores(lhs, low[:, k : k + STRIP]))
-        csum[:, k : k + STRIP] = csum[:, k : k + STRIP] + fold_rows(e2, jnp.add)
-        for h in range(k, k + STRIP, 128):
-            racc = racc + jnp.exp(fbuf[:, h : h + 128] - r)
-    total = jnp.sum(racc, axis=1, keepdims=True)
-    return to_lanes(jnp.broadcast_to(r1 + jnp.log(total), (bt, 128)))
+        first_pass(0, k)
+    rows = []
+    for j in range(count):
+        r1 = jnp.max(rmax[j], axis=1, keepdims=True)
+        r = jnp.broadcast_to(r1, (bt, 128))
+        racc = jnp.zeros((bt, 128), jnp.float32)
+        for k in range(0, n, STRIP):
+            e2 = jnp.exp(scores(lhs[j], low[:, k : k + STRIP]))
+            csum[:, k : k + STRIP] = csum[:, k : k + STRIP] + fold_rows(e2, jnp.add)
+            for h in range(k, k + STRIP, 128):
+                racc = racc + jnp.exp(fbuf[j % 2, :, h : h + 128] - r)
+            if j + 1 < count:
+                first_pass(j + 1, k)
+        total = jnp.sum(racc, axis=1, keepdims=True)
+        rows.append(to_lanes(jnp.broadcast_to(r1 + jnp.log(total), (bt, 128))))
+    return jnp.concatenate(rows, axis=1)
 
 
 def col_logs(ctop, csum):
@@ -169,7 +181,7 @@
         pltpu.VMEM((ch + EXTRA, n), jnp.bfloat16),
         pltpu.VMEM((ch + EXTRA, n), jnp.bfloat16),
         pltpu.VMEM((1, n), jnp.float32),
-        pltpu.VMEM((bt, n), jnp.float32),
+        pltpu.VMEM((2, math.gcd(SUB, bt), n), jnp.float32),
         pltpu.VMEM((8, n), jnp.float32),
         pltpu.VMEM((8, n), jnp.float32),
     ]
@@ -185,7 +197,7 @@
     count, ch, nt = t.shape
     ch = ch * count
     n = s.shape[1]
-    bt = math.gcd(GROUP, nt)
+    bt = math.gcd(SPAN, nt)
     lanes = pl.BlockSpec((1, bt), lambda i, f: (0, i))
     return pl.pallas_call(
         cross_kernel,
@@ -242,7 +254,7 @@
     count, ch, nt = t.shape
     ch = ch * count
     n = s.shape[1]
-    bt = math.gcd(GROUP, nt)
+    bt = math.gcd(SPAN, nt)
     lanes = pl.BlockSpec((1, bt), lambda i, f: (0, i))
     shape = (count, 1, n + more.shape[1])
     long = (1, 1, nt + rest.shape[1])

time: 83.8 us -> 82.1 us (0.980)
  Pallas kernels: 26.8 us -> 25.1 us
    pallas_call x1, Pallas kernels: 7.5 us -> 6.53 us  [cross_tile(): pl.pallas_call(cross_kernel, grid_spec=pltpu.PrefetchScalarGridSpec(num_s...]
    pallas_call x1, Pallas kernels: 8.18 us -> 7.24 us  [cross_again(): pl.pallas_call(functools.partial(cross_again_kernel, len(by_row), len(by_...]
  transfers between devices with their start and end apart: 22 -> 22, of which waited for: 6 -> 6; matrix products, arithmetic and copies ran while one was open for 5% -> 5% of each run, Pallas kernels for 12% -> 11%
where the time goes in v7:
time: 82.1 us; the launch traced here: 81.6 us
  starting transfers between devices  29.2 us (36%)
  Pallas kernels  25.1 us (31%)
  waiting for transfers between devices  20 us (24%)
  other arithmetic  4.22 us (5%)
  local copies, waits for them, and re-layouts  2.23 us (3%)
  between operations  0.85 us (1%)
    ppermute x8, starting transfers between devices, send(): return lax.ppermute(x, axis, [(i, i ^ step) for i in range(count)])  13.1 us
    ppermute x12, starting transfers between devices, collect(): lax.ppermute(x, axis, [(i, i ^ k) for i in range(count)])  11.1 us
    ppermute x8, waiting for transfers between devices, send(): return lax.ppermute(x, axis, [(i, i ^ step) for i in range(count)])  10.6 us
    pallas_call x2, Pallas kernels, self_tile(): pl.pallas_call(self_kernel, grid_spec=pltpu.PrefetchScalarGridSpec(num_sc...  7.51 us
    pallas_call x1, Pallas kernels, cross_again(): pl.pallas_call(functools.partial(cross_again_kernel, len(by_row), len(by_...  7.24 us
    all_to_all x1, waiting for transfers between devices, swap(): return lax.all_to_all(x, axis, 0, 0)  6.82 us
    pallas_call x1, Pallas kernels, cross_tile(): pl.pallas_call(cross_kernel, grid_spec=pltpu.PrefetchScalarGridSpec(num_s...  6.53 us
    all_to_all x1, starting transfers between devices, swap(): return lax.all_to_all(x, axis, 0, 0)  4.36 us
  transfers between devices with their start and end apart: 22, of which 6 were waited for; matrix products, arithmetic and copies ran while one was open for 5% of the time, Pallas kernels for 11%

profile of v7, /device:TPU:0, one launch (start us, length us, event | category | flops | bytes accessed | tf_op | source)
XLA Modules:
  0.0 81.6 jit_solution(7302010958245286975)
XLA Ops:
  0.6 0.7 broadcast_in_dim.19.w_ref.z_ref.tm_ref
  1.3 0.8 %constant_dynamic-update-slice_fusion.9 = (bf16[8,65,512]{2,1,0:T(8,128)(2,1)S(1)}, bf16[65,512]{1,0:T(8,128)(2,1)S(1)}) fusion(s32[]{:T(128)S(6)} %select_n.25, bf16[1,2048]{1,0:T(2,128)(2,1)S(1)} %broadcast_in_dim.19.w_ref.z_ref.tm_ref, bf16[64,2048]{1,0:T(8,128)(2,1)} %bitcast.62), kind=kLoop, calls=%fused_computation.22 | loop fusion | flops 133119 | bytes 413700
  2.2 3.0 %collective-permute-start.10 = (bf16[65,512]{1,0:T(8,128)(2,1)S(1)}, bf16[65,512]{1,0:T(8,128)(2,1)S(1)}, u32[]{:S(2)}, u32[]{:S(2)}) collective-permute-start(bf16[65,512]{1,0:T(8,128)(2,1)S(1)} %get-tuple-element.25), channel_id=1, source_target_pairs={{0,1},{1,0},{2,3},{3,2},{4,5},{5,4},{6,7},{7,6},{8,9},{9,8},{10,11... | collective-permute-start | bytes 199688 | tf_op jit(solution)/shard_map/ppermute | solution.py:411
  5.3 1.0 %select_bitcast_fusion.t_ref = bf16[8,8,2048]{2,1,0:T(8,128)(2,1)S(1)} fusion(pred[]{:T(512)S(6)} %lt.23, bf16[2048,64]{0,1:T(8,128)(2,1)} %param.5), kind=kLoop, calls=%fused_computation.4 | loop fusion | flops 131072 | bytes 524289 | tf_op jit(solution)/shard_map/jit(_where)/select_n | solution.py:436
  6.3 0.8 constant_dynamic-update-slice_fusion.4
  7.0 0.7 broadcast_in_dim.20.z_ref.sm_ref
  7.7 1.6 %collective-permute-done = bf16[8,2048]{1,0:T(8,128)(2,1)S(1)} collective-permute-done((bf16[8,2048]{1,0:T(8,128)(2,1)}, bf16[8,2048]{1,0:T(8,128)(2,1)S(1)}, u32[]{:S(2)}, u32[]{:S(2)}) %collective-permute-start) | collective-permute-done | bytes 32800 | tf_op jit(solution)/shard_map/ppermute | solution.py:411
  9.3 0.8 pad_maximum_fusion.2
  10.1 1.6 %collective-permute-start.1 = (bf16[2,8,2048]{2,1,0:T(8,128)(2,1)S(1)}, bf16[2,8,2048]{2,1,0:T(8,128)(2,1)S(1)}, u32[]{:S(2)}, u32[]{:S(2)}) collective-permute-start(bf16[2,8,2048]{2,1,0:T(8,128)(2,1)S(1)} %pad_maximum_fusion.2), channel_id=1, source_target_pairs={{0,2},{1,3},{2,0},{3,1},{4,6},{5,7},{6,4},{7,5},{8,10},{9,11},{10,... | collective-permute-start | bytes 196616 | tf_op jit(solution)/shard_map/ppermute | solution.py:411
  11.7 2.6 %collective-permute-start.2 = (bf16[2,8,2048]{2,1,0:T(8,128)(2,1)S(1)}, bf16[2,8,2048]{2,1,0:T(8,128)(2,1)S(1)}, u32[]{:S(2)}, u32[]{:S(2)}) collective-permute-start(bf16[2,8,2048]{2,1,0:T(8,128)(2,1)S(1)} %pad_maximum_fusion.2), channel_id=1, source_target_pairs={{0,4},{1,5},{2,6},{3,7},{4,0},{5,1},{6,2},{7,3},{8,12},{9,13},{10,... | collective-permute-start | bytes 196616 | tf_op jit(solution)/shard_map/ppermute | solution.py:411
  14.5 0.7 collective-permute-start.11
  15.3 3.5 %collective-permute-start.12 = (bf16[2,65,512]{2,1,0:T(8,128)(2,1)S(1)}, bf16[2,65,512]{2,1,0:T(8,128)(2,1)S(1)}, u32[]{:S(2)}, u32[]{:S(2)}) collective-permute-start(bf16[2,65,512]{2,1,0:T(8,128)(2,1)S(1)} %pad_maximum_fusion.1), channel_id=1, source_target_pairs={{0,4},{1,5},{2,6},{3,7},{4,0},{5,1},{6,2},{7,3},{8,12},{9,13},{10,... | collective-permute-start | bytes 399368 | tf_op jit(solution)/shard_map/ppermute | solution.py:411
  18.8 2.3 %collective-permute-done.3 = bf16[2,8,2048]{2,1,0:T(8,128)(2,1)S(1)} collective-permute-done((bf16[2,8,2048]{2,1,0:T(8,128)(2,1)S(1)}, bf16[2,8,2048]{2,1,0:T(8,128)(2,1)S(1)}, u32[]{:S(2)}, u32[]{:S(2)}) %collective-permute-start.3) | collective-permute-done | bytes 65568 | tf_op jit(solution)/shard_map/ppermute | solution.py:411
  21.2 1.6 %collective-permute-start.5 = (bf16[65,256]{1,0:T(8,128)(2,1)S(1)}, bf16[65,256]{1,0:T(8,128)(2,1)S(1)}, u32[]{:S(2)}, u32[]{:S(2)}) collective-permute-start(bf16[65,256]{1,0:T(8,128)(2,1)S(1)} %fusion.1), channel_id=1, source_target_pairs={{0,16},{8,24},{16,0},{24,8},{1,17},{9,25},{17,1},{25,9},{2,18},{10... | collective-permute-start | bytes 99848 | tf_op jit(solution)/shard_map/ppermute | solution.py:405
  23.1 6.5 %cross_tile.1 = (f32[1,2048]{1,0:T(1,128)S(1)}, f32[1,2048]{1,0:T(1,128)S(1)}) custom-call(s32[1]{0:T(128)} %bitcast.turn.flip, bf16[8,8,2048]{2,1,0:T(8,128)(2,1)S(1)} %select_bitcast_fusion.t_ref, bf16[1,2048]{1,0:T(2,128)(2,1)S(1)} %broadcast_in_dim.19.w_ref.z_ref.tm_ref, bf16[64,2048]{1,0:T(8,128)(2,1)S(1)} %bitcast.53, ...), custom_call_target="tpu_custom_call" | custom-call | flops 2147483648 | bytes 1048576 | tf_op jit(solution)/shard_map/cross_tile/pallas_call | solution.py:202
  29.7 1.4 %collective-permute-start.13 = (bf16[2,65,512]{2,1,0:T(8,128)(2,1)S(1)}, bf16[2,65,512]{2,1,0:T(8,128)(2,1)S(1)}, u32[]{:S(2)}, u32[]{:S(2)}) collective-permute-start(bf16[2,65,512]{2,1,0:T(8,128)(2,1)S(1)} %pad_maximum_fusion.1), channel_id=1, source_target_pairs={{0,6},{1,7},{2,4},{3,5},{4,2},{5,3},{6,0},{7,1},{8,14},{9,15},{10,... | collective-permute-start | bytes 399368 | tf_op jit(solution)/shard_map/ppermute | solution.py:411
  31.1 6.6 %collective-permute-done.13 = bf16[2,65,512]{2,1,0:T(8,128)(2,1)S(1)} collective-permute-done((bf16[2,65,512]{2,1,0:T(8,128)(2,1)S(1)}, bf16[2,65,512]{2,1,0:T(8,128)(2,1)S(1)}, u32[]{:S(2)}, u32[]{:S(2)}) %collective-permute-start.13) | collective-permute-done | bytes 133152 | tf_op jit(solution)/shard_map/ppermute | solution.py:411
  37.7 6.0 %self_tile.3 = (f32[1,1,6144]{2,1,0:T(1,128)S(1)}, bf16[4096,2048]{1,0:T(8,128)(2,1)S(1)}) custom-call(s32[1]{0:T(128)} %bitcast.turn.flip, bf16[8,65,512]{2,1,0:T(8,128)(2,1)S(1)} %constant_dynamic-update-slice_fusion.5.u_ref, bf16[64,2048]{1,0:T(8,128)(2,1)S(1)} %bitcast.57, bf16[1,2048]{1,0:T(2,128)(2,1)S(1)} %broadcast_in_dim.19.w_ref.z_ref.tm_ref, ...), custom_call_target="tpu_custom_call" | custom-call | flops 2181038080 | bytes 266240 | tf_op jit(solution)/shard_map/self_tile/pallas_call | solution.py:334
  44.4 1.5 %self_tile.2 = (f32[1,1,3072]{2,1,0:T(1,128)S(1)}, bf16[1024,2048]{1,0:T(8,128)(2,1)S(1)}) custom-call(s32[1]{0:T(128)} %bitcast.8.flip, bf16[4,65,256]{2,1,0:T(8,128)(2,1)S(1)} %pad_maximum_fusion.u_ref, bf16[64,2048]{1,0:T(8,128)(2,1)S(1)} %bitcast.55, bf16[1,2048]{1,0:T(2,128)(2,1)S(1)} %broadcast_in_dim.20.z_ref.sm_ref, ...), custom_call_target="tpu_custom_call" | custom-call | flops 545259520 | bytes 66560 | tf_op jit(solution)/shard_map/self_tile/pallas_call | solution.py:334
  46.0 1.6 %collective-permute-start.8 = (f32[1,1,3072]{2,1,0:T(1,128)S(1)}, f32[1,1,3072]{2,1,0:T(1,128)S(1)}, u32[]{:S(2)}, u32[]{:S(2)}) collective-permute-start(f32[1,1,3072]{2,1,0:T(1,128)S(1)} %get-tuple-element.16.refs_0_), channel_id=1, source_target_pairs={{0,16},{8,24},{16,0},{24,8},{1,17},{9,25},{17,1},{25,9},{2,18},{10... | collective-permute-start | bytes 36872 | tf_op jit(solution)/shard_map/ppermute | solution.py:405
  47.9 3.0 %collective-permute-start.15 = (f32[1,6144]{1,0:T(1,128)S(1)}, f32[1,6144]{1,0:T(1,128)S(1)}, u32[]{:S(2)}, u32[]{:S(2)}) collective-permute-start(f32[1,6144]{1,0:T(1,128)S(1)} %compare_select_fusion.refs_0_.refs_4_), channel_id=1, source_target_pairs={{0,2},{1,3},{2,0},{3,1},{4,6},{5,7},{6,4},{7,5},{8,10},{9,11},{10,... | collective-permute-start | bytes 73736 | tf_op jit(solution)/shard_map/ppermute | solution.py:405
  51.1 2.2 %collective-permute-start.17 = (f32[1,6144]{1,0:T(1,128)S(1)}, f32[1,6144]{1,0:T(1,128)S(1)}, u32[]{:S(2)}, u32[]{:S(2)}) collective-permute-start(f32[1,6144]{1,0:T(1,128)S(1)} %compare_select_fusion.refs_0_.refs_4_), channel_id=1, source_target_pairs={{0,6},{1,7},{2,4},{3,5},{4,2},{5,3},{6,0},{7,1},{8,14},{9,15},{10,... | collective-permute-start | bytes 73736 | tf_op jit(solution)/shard_map/ppermute | solution.py:405
  53.4 0.7 again_tile.2
  54.1 1.8 %collective-permute-done.16.refs_2_.refs_6_ = f32[1,6144]{1,0:T(1,128)S(1)} collective-permute-done((f32[1,6144]{1,0:T(1,128)S(1)}, f32[1,6144]{1,0:T(1,128)S(1)}, u32[]{:S(2)}, u32[]{:S(2)}) %collective-permute-start.16) | collective-permute-done | bytes 24608 | tf_op jit(solution)/shard_map/ppermute | solution.py:405
  55.9 0.8 collective-permute-done.17.refs_3_.refs_7_
  56.7 3.1 %again_tile.3 = f32[1,1,4096]{2,1,0:T(1,128)S(1)} custom-call(s32[2]{0:T(128)S(1)} %pad_add_fusion.flip, bf16[8,65,512]{2,1,0:T(8,128)(2,1)S(1)} %constant_dynamic-update-slice_fusion.5.u_ref, bf16[1,2048]{1,0:T(2,128)(2,1)S(1)} %broadcast_in_dim.19.w_ref.z_ref.tm_ref, bf16[4096,2048]{1,0:T(8,128)(2,1)S(1)} %get-tuple-element.18.plan_ref, ...), custom_call_target="tpu_custom_call" | custom-call | flops 268435456 | bytes 16777216 | tf_op jit(solution)/shard_map/again_tile/pallas_call | solution.py:391
  59.8 7.2 %cross_again.1 = (f32[1,1,6144]{2,1,0:T(1,128)S(1)}, f32[1,2048]{1,0:T(1,128)S(1)}, f32[1,2048]{1,0:T(1,128)S(1)}, f32[8,1,4352]{2,1,0:T(1,128)}) custom-call(s32[1]{0:T(128)} %bitcast.turn.flip, bf16[8,8,2048]{2,1,0:T(8,128)(2,1)S(1)} %select_bitcast_fusion.t_ref, bf16[1,2048]{1,0:T(2,128)(2,1)S(1)} %broadcast_in_dim.19.w_ref.z_ref.tm_ref, ...), custom_call_target="tpu_custom_call" | custom-call | flops 2147483648 | bytes 1048576 | tf_op jit(solution)/shard_map/cross_again/pallas_call | solution.py:261
  67.1 1.5 %collective-permute-start.19 = (f32[1,1,6144]{2,1,0:T(1,128)S(1)}, f32[1,1,6144]{2,1,0:T(1,128)S(1)}, u32[]{:S(2)}, u32[]{:S(2)}) collective-permute-start(f32[1,1,6144]{2,1,0:T(1,128)S(1)} %get-tuple-element.23), channel_id=1, source_target_pairs={{0,16},{8,24},{16,0},{24,8},{1,17},{9,25},{17,1},{25,9},{2,18},{10... | collective-permute-start | bytes 73736 | tf_op jit(solution)/shard_map/ppermute | solution.py:405
  68.9 4.4 %all-to-all-start = ((f32[8,1,4352]{2,1,0:T(1,128)}), f32[8,1,4352]{2,1,0:T(1,128)S(1)}, u32[]{:S(2)}, u32[]{:S(2)}) async-start(f32[8,1,4352]{2,1,0:T(1,128)} %get-tuple-element.21), calls=%async_computation | async-start | bytes 278528 | tf_op jit(solution)/shard_map/all_to_all | solution.py:421
  73.3 0.7 multiply_subtract_fusion
  74.0 6.8 %all-to-all-done = f32[8,1,4352]{2,1,0:T(1,128)S(1)} async-done(((f32[8,1,4352]{2,1,0:T(1,128)}), f32[8,1,4352]{2,1,0:T(1,128)S(1)}, u32[]{:S(2)}, u32[]{:S(2)}) %all-to-all-start) | async-done | bytes 139296 | tf_op jit(solution)/shard_map/all_to_all | solution.py:421
  80.9 0.7 multiply_subtract_fusion.1
  (43 shorter events, 2.5 us)
Async XLA Ops:
  2.2 12.3 %collective-permute-start.10 = (bf16[65,512]{1,0:T(8,128)(2,1)S(1)}, bf16[65,512]{1,0:T(8,128)(2,1)S(1)}, u32[]{:S(2)}, u32[]{:S(2)}) collective-permute-start(bf16[65,512]{1,0:T(8,128)(2,1)S(1)} %get-tuple-element.25), channel_id=1, source_target_pairs={{0,1},{1,0},{2,3},{3,2},{4,5},{5,4},{6,7},{7,6},{8,9},{9,8},{10,11... | collective-permute-start | bytes 199688 | tf_op jit(solution)/shard_map/ppermute | solution.py:411
  5.2 4.1 %collective-permute-start = (bf16[8,2048]{1,0:T(8,128)(2,1)}, bf16[8,2048]{1,0:T(8,128)(2,1)S(1)}, u32[]{:S(2)}, u32[]{:S(2)}) collective-permute-start(bf16[8,2048]{1,0:T(8,128)(2,1)} %bitcast.65), channel_id=1, source_target_pairs={{0,1},{1,0},{2,3},{3,2},{4,5},{5,4},{6,7},{7,6},{8,9},{9,8},{10,11... | collective-permute-start | bytes 98312 | tf_op jit(solution)/shard_map/ppermute | solution.py:411
  10.1 8.7 %collective-permute-start.1 = (bf16[2,8,2048]{2,1,0:T(8,128)(2,1)S(1)}, bf16[2,8,2048]{2,1,0:T(8,128)(2,1)S(1)}, u32[]{:S(2)}, u32[]{:S(2)}) collective-permute-start(bf16[2,8,2048]{2,1,0:T(8,128)(2,1)S(1)} %pad_maximum_fusion.2), channel_id=1, source_target_pairs={{0,2},{1,3},{2,0},{3,1},{4,6},{5,7},{6,4},{7,5},{8,10},{9,11},{10,... | collective-permute-start | bytes 196616 | tf_op jit(solution)/shard_map/ppermute | solution.py:411
  11.7 7.1 %collective-permute-start.2 = (bf16[2,8,2048]{2,1,0:T(8,128)(2,1)S(1)}, bf16[2,8,2048]{2,1,0:T(8,128)(2,1)S(1)}, u32[]{:S(2)}, u32[]{:S(2)}) collective-permute-start(bf16[2,8,2048]{2,1,0:T(8,128)(2,1)S(1)} %pad_maximum_fusion.2), channel_id=1, source_target_pairs={{0,4},{1,5},{2,6},{3,7},{4,0},{5,1},{6,2},{7,3},{8,12},{9,13},{10,... | collective-permute-start | bytes 196616 | tf_op jit(solution)/shard_map/ppermute | solution.py:411
  14.3 6.9 %collective-permute-start.3 = (bf16[2,8,2048]{2,1,0:T(8,128)(2,1)S(1)}, bf16[2,8,2048]{2,1,0:T(8,128)(2,1)S(1)}, u32[]{:S(2)}, u32[]{:S(2)}) collective-permute-start(bf16[2,8,2048]{2,1,0:T(8,128)(2,1)S(1)} %pad_maximum_fusion.2), channel_id=1, source_target_pairs={{0,6},{1,7},{2,4},{3,5},{4,2},{5,3},{6,0},{7,1},{8,14},{9,15},{10,... | collective-permute-start | bytes 196616 | tf_op jit(solution)/shard_map/ppermute | solution.py:411
  14.5 16.5 %collective-permute-start.11 = (bf16[2,65,512]{2,1,0:T(8,128)(2,1)S(1)}, bf16[2,65,512]{2,1,0:T(8,128)(2,1)S(1)}, u32[]{:S(2)}, u32[]{:S(2)}) collective-permute-start(bf16[2,65,512]{2,1,0:T(8,128)(2,1)S(1)} %pad_maximum_fusion.1), channel_id=1, source_target_pairs={{0,2},{1,3},{2,0},{3,1},{4,6},{5,7},{6,4},{7,5},{8,10},{9,11},{10,... | collective-permute-start | bytes 399368 | tf_op jit(solution)/shard_map/ppermute | solution.py:411
  15.3 15.8 %collective-permute-start.12 = (bf16[2,65,512]{2,1,0:T(8,128)(2,1)S(1)}, bf16[2,65,512]{2,1,0:T(8,128)(2,1)S(1)}, u32[]{:S(2)}, u32[]{:S(2)}) collective-permute-start(bf16[2,65,512]{2,1,0:T(8,128)(2,1)S(1)} %pad_maximum_fusion.1), channel_id=1, source_target_pairs={{0,4},{1,5},{2,6},{3,7},{4,0},{5,1},{6,2},{7,3},{8,12},{9,13},{10,... | collective-permute-start | bytes 399368 | tf_op jit(solution)/shard_map/ppermute | solution.py:411
  21.2 8.5 %collective-permute-start.4 = (bf16[65,256]{1,0:T(8,128)(2,1)S(1)}, bf16[65,256]{1,0:T(8,128)(2,1)S(1)}, u32[]{:S(2)}, u32[]{:S(2)}) collective-permute-start(bf16[65,256]{1,0:T(8,128)(2,1)S(1)} %fusion.1), channel_id=1, source_target_pairs={{0,8},{8,0},{16,24},{24,16},{1,9},{9,1},{17,25},{25,17},{2,10},{10... | collective-permute-start | bytes 99848 | tf_op jit(solution)/shard_map/ppermute | solution.py:405
  21.2 9.8 %collective-permute-start.5 = (bf16[65,256]{1,0:T(8,128)(2,1)S(1)}, bf16[65,256]{1,0:T(8,128)(2,1)S(1)}, u32[]{:S(2)}, u32[]{:S(2)}) collective-permute-start(bf16[65,256]{1,0:T(8,128)(2,1)S(1)} %fusion.1), channel_id=1, source_target_pairs={{0,16},{8,24},{16,0},{24,8},{1,17},{9,25},{17,1},{25,9},{2,18},{10... | collective-permute-start | bytes 99848 | tf_op jit(solution)/shard_map/ppermute | solution.py:405
  22.8 8.2 %collective-permute-start.6 = (bf16[65,256]{1,0:T(8,128)(2,1)S(1)}, bf16[65,256]{1,0:T(8,128)(2,1)S(1)}, u32[]{:S(2)}, u32[]{:S(2)}) collective-permute-start(bf16[65,256]{1,0:T(8,128)(2,1)S(1)} %fusion.1), channel_id=1, source_target_pairs={{0,24},{8,16},{16,8},{24,0},{1,25},{9,17},{17,9},{25,1},{2,26},{10... | collective-permute-start | bytes 99848 | tf_op jit(solution)/shard_map/ppermute | solution.py:405
  29.7 8.1 %collective-permute-start.13 = (bf16[2,65,512]{2,1,0:T(8,128)(2,1)S(1)}, bf16[2,65,512]{2,1,0:T(8,128)(2,1)S(1)}, u32[]{:S(2)}, u32[]{:S(2)}) collective-permute-start(bf16[2,65,512]{2,1,0:T(8,128)(2,1)S(1)} %pad_maximum_fusion.1), channel_id=1, source_target_pairs={{0,6},{1,7},{2,4},{3,5},{4,2},{5,3},{6,0},{7,1},{8,14},{9,15},{10,... | collective-permute-start | bytes 399368 | tf_op jit(solution)/shard_map/ppermute | solution.py:411
  43.8 4.0 %collective-permute-start.14 = (f32[1,6144]{1,0:T(1,128)S(1)}, f32[1,6144]{1,0:T(1,128)S(1)}, u32[]{:S(2)}, u32[]{:S(2)}) collective-permute-start(f32[1,6144]{1,0:T(1,128)S(1)} %bitcast.58), channel_id=1, source_target_pairs={{0,1},{1,0},{2,3},{3,2},{4,5},{5,4},{6,7},{7,6},{8,9},{9,8},{10,11... | collective-permute-start | bytes 73736 | tf_op jit(solution)/shard_map/ppermute | solution.py:455
  45.9 5.2 %collective-permute-start.7 = (f32[1,1,3072]{2,1,0:T(1,128)S(1)}, f32[1,1,3072]{2,1,0:T(1,128)S(1)}, u32[]{:S(2)}, u32[]{:S(2)}) collective-permute-start(f32[1,1,3072]{2,1,0:T(1,128)S(1)} %get-tuple-element.16.refs_0_), channel_id=1, source_target_pairs={{0,8},{8,0},{16,24},{24,16},{1,9},{9,1},{17,25},{25,17},{2,10},{10... | collective-permute-start | bytes 36872 | tf_op jit(solution)/shard_map/ppermute | solution.py:405
  46.0 7.4 %collective-permute-start.8 = (f32[1,1,3072]{2,1,0:T(1,128)S(1)}, f32[1,1,3072]{2,1,0:T(1,128)S(1)}, u32[]{:S(2)}, u32[]{:S(2)}) collective-permute-start(f32[1,1,3072]{2,1,0:T(1,128)S(1)} %get-tuple-element.16.refs_0_), channel_id=1, source_target_pairs={{0,16},{8,24},{16,0},{24,8},{1,17},{9,25},{17,1},{25,9},{2,18},{10... | collective-permute-start | bytes 36872 | tf_op jit(solution)/shard_map/ppermute | solution.py:405
  47.6 5.8 %collective-permute-start.9 = (f32[1,1,3072]{2,1,0:T(1,128)S(1)}, f32[1,1,3072]{2,1,0:T(1,128)S(1)}, u32[]{:S(2)}, u32[]{:S(2)}) collective-permute-start(f32[1,1,3072]{2,1,0:T(1,128)S(1)} %get-tuple-element.16.refs_0_), channel_id=1, source_target_pairs={{0,24},{8,16},{16,8},{24,0},{1,25},{9,17},{17,9},{25,1},{2,26},{10... | collective-permute-start | bytes 36872 | tf_op jit(solution)/shard_map/ppermute | solution.py:405
  47.9 6.2 %collective-permute-start.15 = (f32[1,6144]{1,0:T(1,128)S(1)}, f32[1,6144]{1,0:T(1,128)S(1)}, u32[]{:S(2)}, u32[]{:S(2)}) collective-permute-start(f32[1,6144]{1,0:T(1,128)S(1)} %compare_select_fusion.refs_0_.refs_4_), channel_id=1, source_target_pairs={{0,2},{1,3},{2,0},{3,1},{4,6},{5,7},{6,4},{7,5},{8,10},{9,11},{10,... | collective-permute-start | bytes 73736 | tf_op jit(solution)/shard_map/ppermute | solution.py:405
  50.9 5.0 %collective-permute-start.16 = (f32[1,6144]{1,0:T(1,128)S(1)}, f32[1,6144]{1,0:T(1,128)S(1)}, u32[]{:S(2)}, u32[]{:S(2)}) collective-permute-start(f32[1,6144]{1,0:T(1,128)S(1)} %compare_select_fusion.refs_0_.refs_4_), channel_id=1, source_target_pairs={{0,4},{1,5},{2,6},{3,7},{4,0},{5,1},{6,2},{7,3},{8,12},{9,13},{10,... | collective-permute-start | bytes 73736 | tf_op jit(solution)/shard_map/ppermute | solution.py:405
  51.1 5.6 %collective-permute-start.17 = (f32[1,6144]{1,0:T(1,128)S(1)}, f32[1,6144]{1,0:T(1,128)S(1)}, u32[]{:S(2)}, u32[]{:S(2)}) collective-permute-start(f32[1,6144]{1,0:T(1,128)S(1)} %compare_select_fusion.refs_0_.refs_4_), channel_id=1, source_target_pairs={{0,6},{1,7},{2,4},{3,5},{4,2},{5,3},{6,0},{7,1},{8,14},{9,15},{10,... | collective-permute-start | bytes 73736 | tf_op jit(solution)/shard_map/ppermute | solution.py:405
  67.1 6.2 %collective-permute-start.18 = (f32[1,1,6144]{2,1,0:T(1,128)S(1)}, f32[1,1,6144]{2,1,0:T(1,128)S(1)}, u32[]{:S(2)}, u32[]{:S(2)}) collective-permute-start(f32[1,1,6144]{2,1,0:T(1,128)S(1)} %get-tuple-element.23), channel_id=1, source_target_pairs={{0,8},{8,0},{16,24},{24,16},{1,9},{9,1},{17,25},{25,17},{2,10},{10... | collective-permute-start | bytes 73736 | tf_op jit(solution)/shard_map/ppermute | solution.py:405
  67.1 6.2 %collective-permute-start.19 = (f32[1,1,6144]{2,1,0:T(1,128)S(1)}, f32[1,1,6144]{2,1,0:T(1,128)S(1)}, u32[]{:S(2)}, u32[]{:S(2)}) collective-permute-start(f32[1,1,6144]{2,1,0:T(1,128)S(1)} %get-tuple-element.23), channel_id=1, source_target_pairs={{0,16},{8,24},{16,0},{24,8},{1,17},{9,25},{17,1},{25,9},{2,18},{10... | collective-permute-start | bytes 73736 | tf_op jit(solution)/shard_map/ppermute | solution.py:405
  68.6 4.7 %collective-permute-start.20 = (f32[1,1,6144]{2,1,0:T(1,128)S(1)}, f32[1,1,6144]{2,1,0:T(1,128)S(1)}, u32[]{:S(2)}, u32[]{:S(2)}) collective-permute-start(f32[1,1,6144]{2,1,0:T(1,128)S(1)} %get-tuple-element.23), channel_id=1, source_target_pairs={{0,24},{8,16},{16,8},{24,0},{1,25},{9,17},{17,9},{25,1},{2,26},{10... | collective-permute-start | bytes 73736 | tf_op jit(solution)/shard_map/ppermute | solution.py:405
  68.9 11.9 %all-to-all-start = ((f32[8,1,4352]{2,1,0:T(1,128)}), f32[8,1,4352]{2,1,0:T(1,128)S(1)}, u32[]{:S(2)}, u32[]{:S(2)}) async-start(f32[8,1,4352]{2,1,0:T(1,128)} %get-tuple-element.21), calls=%async_computation | async-start | bytes 278528 | tf_op jit(solution)/shard_map/all_to_all | solution.py:421
